TPU v7x, 32 devices: a whole 2x2x4 slice. The times are simulated.
32 devices in a mesh: seq: 4 (over x, core), fsdp: 8 (over z, y).
Axes of the slice: x: 2, y: 2, z: 4, core: 2. Of those that a mesh axis runs over, the one named last changes fastest.
Arguments:
- tokens_in: bfloat16 [16, 512, 1024], P('fsdp', 'seq'), may hold values from -6 to 6
- cotangent: bfloat16 [16, 512, 1024], P('fsdp', 'seq'), may hold values from -6 to 6
- query_weight: bfloat16 [1024, 1024], P('fsdp'), may hold values from -0.1875 to 0.1875
- key_weight: bfloat16 [1024, 1024], P('fsdp'), may hold values from -0.1875 to 0.1875
- value_weight: bfloat16 [1024, 1024], P('fsdp'), may hold values from -0.1875 to 0.1875
- out_weight: bfloat16 [1024, 1024], P('fsdp'), may hold values from -1.5 to 1.5
- up_weight: bfloat16 [1024, 4096], P('fsdp'), may hold values from -0.1875 to 0.1875
- down_weight: bfloat16 [4096, 1024], P('fsdp'), may hold values from -0.09375 to 0.09375
- query_bias: bfloat16 [1024], P('fsdp'), may hold values from -4 to 4
- value_bias: bfloat16 [1024], P('fsdp'), may hold values from -0.75 to 0.75
- out_bias: bfloat16 [1024], P('fsdp'), may hold values from -4 to 4
- up_bias: bfloat16 [4096], P('fsdp'), may hold values from -4 to 4
- down_bias: bfloat16 [1024], P('fsdp'), may hold values from -4 to 4
- first_gain: bfloat16 [1024], P('fsdp'), may hold values from 0.25 to 1.75
- first_shift: bfloat16 [1024], P('fsdp'), may hold values from -4 to 4
- second_gain: bfloat16 [1024], P('fsdp'), may hold values from 0.25 to 1.75
- second_shift: bfloat16 [1024], P('fsdp'), may hold values from -4 to 4
Outputs:
- layer_out: bfloat16 [16, 512, 1024], P('fsdp', 'seq')
- input_grad: float32 [16, 512, 1024], P('fsdp', 'seq')
- query_weight_grad: float32 [1024, 1024], P('fsdp')
- key_weight_grad: float32 [1024, 1024], P('fsdp')
- value_weight_grad: float32 [1024, 1024], P('fsdp')
- out_weight_grad: float32 [1024, 1024], P('fsdp')
- up_weight_grad: float32 [1024, 4096], P('fsdp')
- down_weight_grad: float32 [4096, 1024], P('fsdp')
- query_bias_grad: float32 [1024], P('fsdp')
- value_bias_grad: float32 [1024], P('fsdp')
- out_bias_grad: float32 [1024], P('fsdp')
- up_bias_grad: float32 [4096], P('fsdp')
- down_bias_grad: float32 [1024], P('fsdp')
- first_gain_grad: float32 [1024], P('fsdp')
- first_shift_grad: float32 [1024], P('fsdp')
- second_gain_grad: float32 [1024], P('fsdp')
- second_shift_grad: float32 [1024], P('fsdp')
All inputs are finite; a program needn't handle non-finite values.
Results may differ from a plain program's by a relative error of at most 0.018.
Values may be sent and summed in bfloat16 or wider, within the bound.
No kernel may reach another device: no remote copies, remote signals or barrier semaphores. Data moves between devices by JAX's collectives and lax.ppermute only.
A program may use at most 192 MiB of HBM per device.

v0:
```python
from functools import partial
from functools import reduce
import math

import jax
import jax.numpy as jnp
from jax import lax
from jax.sharding import PartitionSpec as P

HD = 64
MICRO = 2


EPSILON = 1e-05


def layer_norm(hidden, gain, shift):
    average = jnp.mean(hidden, -1, keepdims=True)
    centered = hidden - average
    spread = jnp.mean(centered * centered, -1, keepdims=True)
    return centered * lax.rsqrt(spread + EPSILON) * gain + shift


def matmul(left_side, right_side):
    return jnp.dot(left_side, right_side, preferred_element_type=jnp.float32)


def matmul_tleft(left_side, right_side):
    return lax.dot_general(
        left_side, right_side, (((0,), (0,)), ((), ())), preferred_element_type=jnp.float32
    )


def matmul_tright(left_side, right_side):
    return lax.dot_general(
        left_side, right_side, (((1,), (1,)), ((), ())), preferred_element_type=jnp.float32
    )


def column_sum(matrix):
    return jnp.sum(matrix.astype(jnp.float32), 0)


def to_heads(matrix):
    return matrix.reshape(matrix.shape[0], matrix.shape[1] // HD, HD)


def attend(triple):
    query_heads = to_heads(triple[0])
    key_heads = to_heads(triple[1])
    value_heads = to_heads(triple[2])
    scaling = 1.0 / math.sqrt(HD)
    scores = (
        jnp.einsum("qhd,khd->hqk", query_heads, key_heads, preferred_element_type=jnp.float32)
        * scaling
    )
    highest = jnp.max(scores, -1, keepdims=True)
    raised = jnp.exp(scores - highest)
    summed = jnp.sum(raised, -1, keepdims=True)
    attention_low = (raised / summed).astype(jnp.bfloat16)
    mixture = jnp.einsum(
        "hqk,khd->qhd", attention_low, value_heads, preferred_element_type=jnp.float32
    )
    log_total = highest[..., 0] + jnp.log(summed[..., 0])
    return (mixture.astype(jnp.bfloat16).reshape(triple[0].shape), log_total)


def attend_back(bundle):
    query_heads = to_heads(bundle[0])
    key_heads = to_heads(bundle[1])
    value_heads = to_heads(bundle[2])
    log_total = bundle[3]
    grad_heads = to_heads(bundle[4])
    scaling = 1.0 / math.sqrt(HD)
    scores = (
        jnp.einsum("qhd,khd->hqk", query_heads, key_heads, preferred_element_type=jnp.float32)
        * scaling
    )
    attention = jnp.exp(scores - log_total[..., None])
    attention_grad = jnp.einsum(
        "qhd,khd->hqk", grad_heads, value_heads, preferred_element_type=jnp.float32
    )
    value_back = jnp.einsum(
        "hqk,qhd->khd",
        attention.astype(jnp.bfloat16),
        grad_heads,
        preferred_element_type=jnp.float32,
    )
    inner = jnp.sum(attention * attention_grad, -1, keepdims=True)
    score_low = (attention * (attention_grad - inner)).astype(jnp.bfloat16)
    query_back = (
        jnp.einsum("hqk,khd->qhd", score_low, key_heads, preferred_element_type=jnp.float32)
        * scaling
    )
    key_back = (
        jnp.einsum("hqk,qhd->khd", score_low, query_heads, preferred_element_type=jnp.float32)
        * scaling
    )
    shape = bundle[0].shape
    return (
        query_back.astype(jnp.bfloat16).reshape(shape),
        key_back.astype(jnp.bfloat16).reshape(shape),
        value_back.astype(jnp.bfloat16).reshape(shape),
    )


def forward(batch_in, params):
    (
        query_weight,
        key_weight,
        value_weight,
        out_weight,
        up_weight,
        down_weight,
        query_bias,
        value_bias,
        out_bias,
        up_bias,
        down_bias,
        first_gain,
        first_shift,
        second_gain,
        second_shift,
    ) = params
    number, slice_len, width = batch_in.shape
    token_rows = batch_in.reshape(number * slice_len, width)
    query_rows = (matmul(token_rows, query_weight) + query_bias.astype(jnp.float32)).astype(
        jnp.bfloat16
    )
    key_rows = matmul(token_rows, key_weight).astype(jnp.bfloat16)
    value_rows = (matmul(token_rows, value_weight) + value_bias.astype(jnp.float32)).astype(
        jnp.bfloat16
    )
    query_rows = query_rows.reshape(number, slice_len, width)
    key_rows = key_rows.reshape(number, slice_len, width)
    value_rows = value_rows.reshape(number, slice_len, width)
    query_heads, key_heads, value_heads = (
        lax.all_to_all(query_rows, "seq", split_axis=2, concat_axis=1, tiled=True),
        lax.all_to_all(key_rows, "seq", split_axis=2, concat_axis=1, tiled=True),
        lax.all_to_all(value_rows, "seq", split_axis=2, concat_axis=1, tiled=True),
    )
    mixture, log_total = lax.map(attend, (query_heads, key_heads, value_heads))
    mixture_rows = lax.all_to_all(mixture, "seq", split_axis=1, concat_axis=2, tiled=True).reshape(
        number * slice_len, width
    )
    attn_sum = (
        token_rows.astype(jnp.float32)
        + matmul(mixture_rows, out_weight)
        + out_bias.astype(jnp.float32)
    )
    normed_first = layer_norm(
        attn_sum, first_gain.astype(jnp.float32), first_shift.astype(jnp.float32)
    )
    first_low = normed_first.astype(jnp.bfloat16)
    up_rows = matmul(first_low, up_weight) + up_bias.astype(jnp.float32)
    gelu_low = jax.nn.gelu(up_rows, approximate=False).astype(jnp.bfloat16)
    ffn_sum = normed_first + matmul(gelu_low, down_weight) + down_bias.astype(jnp.float32)
    layer_rows = layer_norm(
        ffn_sum, second_gain.astype(jnp.float32), second_shift.astype(jnp.float32)
    )
    saved = (
        query_heads,
        key_heads,
        value_heads,
        log_total,
        mixture_rows,
        attn_sum,
        first_low,
        up_rows,
        gelu_low,
        ffn_sum,
    )
    return (saved, layer_rows.astype(jnp.bfloat16).reshape(number, slice_len, width))


def backward(batch_in, batch_cot, saved, params):
    (
        query_weight,
        key_weight,
        value_weight,
        out_weight,
        up_weight,
        down_weight,
        query_bias,
        value_bias,
        out_bias,
        up_bias,
        down_bias,
        first_gain,
        first_shift,
        second_gain,
        second_shift,
    ) = params
    (
        query_heads,
        key_heads,
        value_heads,
        log_total,
        mixture_rows,
        attn_sum,
        first_low,
        up_rows,
        gelu_low,
        ffn_sum,
    ) = saved
    number, slice_len, width = batch_in.shape
    token_rows = batch_in.reshape(number * slice_len, width)
    cot_rows = batch_cot.reshape(number * slice_len, width).astype(jnp.float32)
    layer_value, second_pull = jax.vjp(
        layer_norm, ffn_sum, second_gain.astype(jnp.float32), second_shift.astype(jnp.float32)
    )
    ffn_grad, second_gain_grad, second_shift_grad = second_pull(cot_rows)
    down_low = ffn_grad.astype(jnp.bfloat16)
    down_weight_grad = matmul_tleft(gelu_low, down_low)
    down_bias_grad = column_sum(down_low)
    gelu_grad = matmul_tright(down_low, down_weight)
    gelu_value, gelu_pull = jax.vjp(partial(jax.nn.gelu, approximate=False), up_rows)
    (up_grad,) = gelu_pull(gelu_grad)
    up_low = up_grad.astype(jnp.bfloat16)
    up_weight_grad = matmul_tleft(first_low, up_low)
    up_bias_grad = column_sum(up_low)
    first_grad = ffn_grad + matmul_tright(up_low, up_weight)
    first_value, first_pull = jax.vjp(
        layer_norm, attn_sum, first_gain.astype(jnp.float32), first_shift.astype(jnp.float32)
    )
    attn_grad, first_gain_grad, first_shift_grad = first_pull(first_grad)
    out_low = attn_grad.astype(jnp.bfloat16)
    out_weight_grad = matmul_tleft(mixture_rows, out_low)
    out_bias_grad = column_sum(out_low)
    mixture_grad = (
        matmul_tright(out_low, out_weight).astype(jnp.bfloat16).reshape(number, slice_len, width)
    )
    heads_grad = lax.all_to_all(mixture_grad, "seq", split_axis=2, concat_axis=1, tiled=True)
    query_grad, key_grad, value_grad = lax.map(
        attend_back, (query_heads, key_heads, value_heads, log_total, heads_grad)
    )
    query_back, key_back, value_back = (
        lax.all_to_all(query_grad, "seq", split_axis=1, concat_axis=2, tiled=True),
        lax.all_to_all(key_grad, "seq", split_axis=1, concat_axis=2, tiled=True),
        lax.all_to_all(value_grad, "seq", split_axis=1, concat_axis=2, tiled=True),
    )
    query_back = query_back.reshape(number * slice_len, width)
    key_back = key_back.reshape(number * slice_len, width)
    value_back = value_back.reshape(number * slice_len, width)
    query_weight_grad = matmul_tleft(token_rows, query_back)
    key_weight_grad = matmul_tleft(token_rows, key_back)
    value_weight_grad = matmul_tleft(token_rows, value_back)
    query_bias_grad = column_sum(query_back)
    value_bias_grad = column_sum(value_back)
    input_rows = (
        attn_grad
        + matmul_tright(query_back, query_weight)
        + matmul_tright(key_back, key_weight)
        + matmul_tright(value_back, value_weight)
    )
    terms = (
        query_weight_grad,
        key_weight_grad,
        value_weight_grad,
        out_weight_grad,
        up_weight_grad,
        down_weight_grad,
        query_bias_grad,
        value_bias_grad,
        out_bias_grad,
        up_bias_grad,
        down_bias_grad,
        first_gain_grad,
        first_shift_grad,
        second_gain_grad,
        second_shift_grad,
    )
    return (input_rows.reshape(number, slice_len, width), terms)


def add_trees(earlier, later):
    return jax.tree.map(jnp.add, earlier, later)


def body(
    tokens_in,
    cotangent,
    query_weight,
    key_weight,
    value_weight,
    out_weight,
    up_weight,
    down_weight,
    query_bias,
    value_bias,
    out_bias,
    up_bias,
    down_bias,
    first_gain,
    first_shift,
    second_gain,
    second_shift,
):
    per_micro = tokens_in.shape[0] // MICRO
    layer_parts = []
    input_parts = []
    grad_parts = []
    for micro_step in range(MICRO):
        begin = micro_step * per_micro
        batch_in = tokens_in[begin : begin + per_micro]
        batch_cot = cotangent[begin : begin + per_micro]
        forward_params = (
            lax.all_gather(query_weight, "fsdp", axis=0, tiled=True),
            lax.all_gather(key_weight, "fsdp", axis=0, tiled=True),
            lax.all_gather(value_weight, "fsdp", axis=0, tiled=True),
            lax.all_gather(out_weight, "fsdp", axis=0, tiled=True),
            lax.all_gather(up_weight, "fsdp", axis=0, tiled=True),
            lax.all_gather(down_weight, "fsdp", axis=0, tiled=True),
            lax.all_gather(query_bias, "fsdp", axis=0, tiled=True),
            lax.all_gather(value_bias, "fsdp", axis=0, tiled=True),
            lax.all_gather(out_bias, "fsdp", axis=0, tiled=True),
            lax.all_gather(up_bias, "fsdp", axis=0, tiled=True),
            lax.all_gather(down_bias, "fsdp", axis=0, tiled=True),
            lax.all_gather(first_gain, "fsdp", axis=0, tiled=True),
            lax.all_gather(first_shift, "fsdp", axis=0, tiled=True),
            lax.all_gather(second_gain, "fsdp", axis=0, tiled=True),
            lax.all_gather(second_shift, "fsdp", axis=0, tiled=True),
        )
        saved, layer_batch = forward(batch_in, forward_params)
        backward_params = (
            lax.all_gather(query_weight, "fsdp", axis=0, tiled=True),
            lax.all_gather(key_weight, "fsdp", axis=0, tiled=True),
            lax.all_gather(value_weight, "fsdp", axis=0, tiled=True),
            lax.all_gather(out_weight, "fsdp", axis=0, tiled=True),
            lax.all_gather(up_weight, "fsdp", axis=0, tiled=True),
            lax.all_gather(down_weight, "fsdp", axis=0, tiled=True),
            lax.all_gather(query_bias, "fsdp", axis=0, tiled=True),
            lax.all_gather(value_bias, "fsdp", axis=0, tiled=True),
            lax.all_gather(out_bias, "fsdp", axis=0, tiled=True),
            lax.all_gather(up_bias, "fsdp", axis=0, tiled=True),
            lax.all_gather(down_bias, "fsdp", axis=0, tiled=True),
            lax.all_gather(first_gain, "fsdp", axis=0, tiled=True),
            lax.all_gather(first_shift, "fsdp", axis=0, tiled=True),
            lax.all_gather(second_gain, "fsdp", axis=0, tiled=True),
            lax.all_gather(second_shift, "fsdp", axis=0, tiled=True),
        )
        input_batch, terms = backward(batch_in, batch_cot, saved, backward_params)
        layer_parts.append(layer_batch)
        input_parts.append(input_batch)
        grad_parts.append(terms)
    totals = reduce(add_trees, grad_parts)
    sharded = (
        lax.psum_scatter(totals[0], "fsdp", scatter_dimension=0, tiled=True),
        lax.psum_scatter(totals[1], "fsdp", scatter_dimension=0, tiled=True),
        lax.psum_scatter(totals[2], "fsdp", scatter_dimension=0, tiled=True),
        lax.psum_scatter(totals[3], "fsdp", scatter_dimension=0, tiled=True),
        lax.psum_scatter(totals[4], "fsdp", scatter_dimension=0, tiled=True),
        lax.psum_scatter(totals[5], "fsdp", scatter_dimension=0, tiled=True),
        lax.psum_scatter(totals[6], "fsdp", scatter_dimension=0, tiled=True),
        lax.psum_scatter(totals[7], "fsdp", scatter_dimension=0, tiled=True),
        lax.psum_scatter(totals[8], "fsdp", scatter_dimension=0, tiled=True),
        lax.psum_scatter(totals[9], "fsdp", scatter_dimension=0, tiled=True),
        lax.psum_scatter(totals[10], "fsdp", scatter_dimension=0, tiled=True),
        lax.psum_scatter(totals[11], "fsdp", scatter_dimension=0, tiled=True),
        lax.psum_scatter(totals[12], "fsdp", scatter_dimension=0, tiled=True),
        lax.psum_scatter(totals[13], "fsdp", scatter_dimension=0, tiled=True),
        lax.psum_scatter(totals[14], "fsdp", scatter_dimension=0, tiled=True),
    )
    final = (
        lax.psum(sharded[0].astype(jnp.bfloat16), "seq").astype(jnp.float32),
        lax.psum(sharded[1].astype(jnp.bfloat16), "seq").astype(jnp.float32),
        lax.psum(sharded[2].astype(jnp.bfloat16), "seq").astype(jnp.float32),
        lax.psum(sharded[3].astype(jnp.bfloat16), "seq").astype(jnp.float32),
        lax.psum(sharded[4].astype(jnp.bfloat16), "seq").astype(jnp.float32),
        lax.psum(sharded[5].astype(jnp.bfloat16), "seq").astype(jnp.float32),
        lax.psum(sharded[6].astype(jnp.bfloat16), "seq").astype(jnp.float32),
        lax.psum(sharded[7].astype(jnp.bfloat16), "seq").astype(jnp.float32),
        lax.psum(sharded[8].astype(jnp.bfloat16), "seq").astype(jnp.float32),
        lax.psum(sharded[9].astype(jnp.bfloat16), "seq").astype(jnp.float32),
        lax.psum(sharded[10].astype(jnp.bfloat16), "seq").astype(jnp.float32),
        lax.psum(sharded[11].astype(jnp.bfloat16), "seq").astype(jnp.float32),
        lax.psum(sharded[12].astype(jnp.bfloat16), "seq").astype(jnp.float32),
        lax.psum(sharded[13].astype(jnp.bfloat16), "seq").astype(jnp.float32),
        lax.psum(sharded[14].astype(jnp.bfloat16), "seq").astype(jnp.float32),
    )
    layer_out = jnp.concatenate(layer_parts, 0)
    input_grad = jnp.concatenate(input_parts, 0)
    return (
        layer_out,
        input_grad,
        final[0],
        final[1],
        final[2],
        final[3],
        final[4],
        final[5],
        final[6],
        final[7],
        final[8],
        final[9],
        final[10],
        final[11],
        final[12],
        final[13],
        final[14],
    )


def solution(mesh):
    in_specs = (
        P("fsdp", "seq", None),
        P("fsdp", "seq", None),
        P("fsdp", None),
        P("fsdp", None),
        P("fsdp", None),
        P("fsdp", None),
        P("fsdp", None),
        P("fsdp", None),
        P("fsdp"),
        P("fsdp"),
        P("fsdp"),
        P("fsdp"),
        P("fsdp"),
        P("fsdp"),
        P("fsdp"),
        P("fsdp"),
        P("fsdp"),
    )
    out_specs = (
        P("fsdp", "seq", None),
        P("fsdp", "seq", None),
        P("fsdp", None),
        P("fsdp", None),
        P("fsdp", None),
        P("fsdp", None),
        P("fsdp", None),
        P("fsdp", None),
        P("fsdp"),
        P("fsdp"),
        P("fsdp"),
        P("fsdp"),
        P("fsdp"),
        P("fsdp"),
        P("fsdp"),
        P("fsdp"),
        P("fsdp"),
    )
    return jax.shard_map(body, mesh=mesh, in_specs=in_specs, out_specs=out_specs, check_vma=False)
```

profile of v0, /device:TPU:13, one launch (start us, length us, event | category | flops | bytes accessed | tf_op | source)
XLA Modules:
  0.0 1525.7 jit_solution(8803495947754608472)
XLA Ops:
  11.2 10.8 all-gather.1
  22.0 16.3 %all-gather = bf16[8,1,128]{2,1,0:T(2,128)(2,1)S(1)} all-gather(bf16[1,1,128]{2,1,0:T(2,128)(2,1)S(1)} %bitcast.428), channel_id=1, replica_groups=mesh['seq'=4,'fsdp'=8] {'fsdp'}, dimensions={0}, use_global_device_ids=true | all-gather | bytes 2304 | tf_op jit(solution)/shard_map/all_gather | solution.py:315
  38.4 20.6 %all-gather.16.cloned.1.call-done = bf16[1024,1024]{1,0:T(8,128)(2,1)} async-done(((bf16[128,1024]{1,0:T(8,128)(2,1)}), bf16[1024,1024]{1,0:T(8,128)(2,1)}) %all-gather.16.cloned.1.call-update) | async-done | bytes 2097168 | tf_op jit(solution)/shard_map/all_gather | solution.py:310
  65.1 4.9 all-to-all-start
  75.3 4.8 all-to-all-start.4
  80.0 28.9 %all-gather.18.cloned.1.call-done = bf16[1024,1024]{1,0:T(8,128)(2,1)} async-done(((bf16[128,1024]{1,0:T(8,128)(2,1)}), bf16[1024,1024]{1,0:T(8,128)(2,1)}) %all-gather.18.cloned.1.call-update) | async-done | bytes 2097168 | tf_op jit(solution)/shard_map/all_gather | solution.py:308
  114.5 4.9 all-to-all-start.1
  124.7 5.0 all-to-all-start.5
  129.7 29.1 %all-gather.20.cloned.1.call-done = bf16[1024,1024]{1,0:T(8,128)(2,1)} async-done(((bf16[128,1024]{1,0:T(8,128)(2,1)}), bf16[1024,1024]{1,0:T(8,128)(2,1)}) %all-gather.20.cloned.1.call-update) | async-done | bytes 2097168 | tf_op jit(solution)/shard_map/all_gather | solution.py:309
  164.5 4.9 all-to-all-start.6
  174.6 4.2 all-to-all-start.2
  191.9 14.2 all-to-all-start.3
  217.0 12.4 all-gather.2
  229.4 14.4 all-gather.6
  243.8 13.2 all-gather.3
  257.0 14.4 all-gather.4
  271.4 13.7 all-gather.7
  285.2 14.7 all-gather.8
  299.9 21.4 %all-gather.5 = bf16[8,1,512]{2,1,0:T(2,128)(2,1)S(1)} all-gather(bf16[1,1,512]{2,1,0:T(2,128)(2,1)S(1)} %reshape.387), channel_id=1, replica_groups=mesh['seq'=4,'fsdp'=8] {'fsdp'}, dimensions={0}, use_global_device_ids=true | all-gather | bytes 9216 | tf_op jit(solution)/shard_map/all_gather | solution.py:317
  326.4 6.8 all-gather.24.cloned.1.call-done
  333.2 9.6 multiply_convert_fusion.2
  342.8 115.5 %all-gather.26.cloned.1.call-done = bf16[4096,1024]{1,0:T(8,128)(2,1)} async-done(((bf16[512,1024]{1,0:T(8,128)(2,1)}), bf16[4096,1024]{1,0:T(8,128)(2,1)}) %all-gather.26.cloned.1.call-update) | async-done | bytes 8388624 | tf_op jit(solution)/shard_map/all_gather | solution.py:313
  458.4 5.3 fusion.121
  464.5 9.1 multiply_convert_fusion.3
  477.5 5.7 convert_reduce_fusion
  486.2 5.6 convert_reduce_fusion.1
  504.9 3.8 reduce.14
  510.5 4.9 all-to-all-start.12
  533.8 3.7 all-to-all-start.15
  548.6 4.6 all-to-all-done.11
  566.2 3.8 reduce.20
  571.8 5.2 all-to-all-start.10
  577.1 3.7 multiply_reduce_fusion
  586.7 3.8 reduce.16
  592.2 4.0 all-to-all-start.14
  615.8 3.9 reduce.19
  621.4 4.6 all-to-all-start.9
  631.5 4.1 all-to-all-start.13
  637.1 3.7 all-to-all-done.13
  648.6 8.2 convolution_add_fusion.1
  660.4 8.1 convolution_add_fusion
  684.1 90.1 %reduce-scatter.9.cloned.1.call-done = f32[128,1024]{0,1:T(8,128)} async-done(((f32[1024,1024]{0,1:T(8,128)}), f32[128,1024]{0,1:T(8,128)}) %reduce-scatter.9.cloned.1.call-update) | async-done | bytes 524304 | tf_op jit(solution)/shard_map/reduce_scatter | solution.py:349
  775.9 90.2 %reduce-scatter.7.cloned.1.call-done = f32[128,1024]{0,1:T(8,128)} async-done(((f32[1024,1024]{0,1:T(8,128)}), f32[128,1024]{0,1:T(8,128)}) %reduce-scatter.7.cloned.1.call-update) | async-done | bytes 524304 | tf_op jit(solution)/shard_map/reduce_scatter | solution.py:348
  867.9 282.1 %reduce-scatter.15.cloned.1.call-done = f32[128,4096]{1,0:T(8,128)} async-done(((f32[1024,4096]{1,0:T(8,128)}), f32[128,4096]{1,0:T(8,128)}) %reduce-scatter.15.cloned.1.call-update) | async-done | bytes 2097168 | tf_op jit(solution)/shard_map/reduce_scatter | solution.py:352
  1152.7 283.2 %reduce-scatter.17.cloned.1.call-done = f32[512,1024]{1,0:T(8,128)} async-done(((f32[4096,1024]{1,0:T(8,128)}), f32[512,1024]{1,0:T(8,128)}) %reduce-scatter.17.cloned.1.call-update) | async-done | bytes 2097168 | tf_op jit(solution)/shard_map/reduce_scatter | solution.py:353
  1438.7 24.9 %all-reduce.9 = (bf16[1024]{0:T(1024)(128)(2,1)S(1)}, bf16[1024]{0:T(1024)(128)(2,1)S(1)}, bf16[1024]{0:T(1024)(128)(2,1)S(1)}, bf16[4096]{0:T(1024)(128)(2,1)S(...) all-reduce(f32[1024]{0:T(1024)S(1)} %bitcast.424, ...), channel_id=8, replica_groups=mesh['seq'=4,'fsdp'=8] {'fsdp'}, use_global_device_ids=true, to_apply=%region_36.37.clone | all-reduce | flops 12288 | bytes 73728
  1464.3 12.1 all-reduce.10
  1489.2 20.0 %all-reduce.14.cloned.1.call-done = (bf16[128,1024]{0,1:T(8,128)(2,1)}, bf16[128,1024]{0,1:T(8,128)(2,1)}, bf16[128,1024]{0,1:T(8,128)(2,1)}, bf16[128,1024]{1,0...) async-done(((bf16[128,1024]{0,1:T(8,128)(2,1)}, bf16[128,1024]{0,1:T(8,128)(2,1)}, bf16[128,1024]{0,1:T(8,128)(2,1)}, bf16[128,1024]{1,0:T(8,128)(2,1)}, ...) | async-done | bytes 3145744 | tf_op jit(solution)/shard_map/psum | solution.py:365
  (443 shorter events, 225.0 us)
Async XLA Ops:
  7.2 14.8 copy-start.72
  7.2 51.8 %copy-start.12 = (bf16[2,128,1024]{2,1,0:T(8,128)(2,1)S(1)}, bf16[2,128,1024]{2,1,0:T(8,128)(2,1)}, u32[]{:S(2)}) copy-start(bf16[2,128,1024]{2,1,0:T(8,128)(2,1)} %param.17) | copy-start | bytes 1572868
  7.2 51.8 %all-gather.16.cloned.1.call-start = ((), (), s32[]{:S(2)}) async-start(), calls=%async_computation.22 | async-start | bytes 2359296 | tf_op jit(solution)/shard_map/all_gather | solution.py:310
  8.0 101.0 %all-gather.18.cloned.1.call-start = ((), (), s32[]{:S(2)}) async-start(), calls=%async_computation.23 | async-start | bytes 2359296 | tf_op jit(solution)/shard_map/all_gather | solution.py:308
  8.7 150.2 %all-gather.20.cloned.1.call-start = ((), (), s32[]{:S(2)}) async-start(), calls=%async_computation.24 | async-start | bytes 2359296 | tf_op jit(solution)/shard_map/all_gather | solution.py:309
  9.4 313.7 %all-gather.22.cloned.1.call-start = ((), (), s32[]{:S(2)}) async-start(), calls=%async_computation.25 | async-start | bytes 2359296 | tf_op jit(solution)/shard_map/all_gather | solution.py:311
  10.0 323.2 %all-gather.24.cloned.1.call-start = ((), (), s32[]{:S(2)}) async-start(), calls=%async_computation.26 | async-start | bytes 9437184 | tf_op jit(solution)/shard_map/all_gather | solution.py:312
  10.6 447.7 %all-gather.26.cloned.1.call-start = ((), (), s32[]{:S(2)}) async-start(), calls=%async_computation.27 | async-start | bytes 9437184 | tf_op jit(solution)/shard_map/all_gather | solution.py:313
  59.0 11.0 copy-start.8
  65.1 10.2 all-to-all-start
  75.3 33.6 %copy-start.65 = (bf16[4,2,16384]{2,1,0:T(2,128)(2,1)}, bf16[4,2,16384]{2,1,0:T(2,128)(2,1)S(1)}, u32[]{:S(2)}) copy-start(bf16[4,2,16384]{2,1,0:T(2,128)(2,1)S(1)} %all-to-all-done) | copy-start | bytes 786436
  75.3 39.2 %all-to-all-start.4 = ((bf16[4,2,16384]{2,1,0:T(2,128)(2,1)}), bf16[4,2,16384]{2,1,0:T(2,128)(2,1)}, u32[]{:S(2)}, u32[]{:S(2)}) async-start(bf16[4,2,16384]{2,1,0:T(2,128)(2,1)} %reshape.421), calls=%async_computation.4 | async-start | bytes 524288 | tf_op jit(solution)/shard_map/all_to_all | solution.py:140
  108.9 10.5 copy-start.5
  114.5 10.2 all-to-all-start.1
  124.7 34.2 %copy-start.67 = (bf16[4,2,16384]{2,1,0:T(2,128)(2,1)}, bf16[4,2,16384]{2,1,0:T(2,128)(2,1)S(1)}, u32[]{:S(2)}) copy-start(bf16[4,2,16384]{2,1,0:T(2,128)(2,1)S(1)} %all-to-all-done.1) | copy-start | bytes 786436
  124.7 39.8 %all-to-all-start.5 = ((bf16[4,2,16384]{2,1,0:T(2,128)(2,1)}), bf16[4,2,16384]{2,1,0:T(2,128)(2,1)}, u32[]{:S(2)}, u32[]{:S(2)}) async-start(bf16[4,2,16384]{2,1,0:T(2,128)(2,1)} %reshape.423), calls=%async_computation.5 | async-start | bytes 524288 | tf_op jit(solution)/shard_map/all_to_all | solution.py:138
  158.9 10.5 copy-start.10
  164.5 10.2 all-to-all-start.6
  174.6 9.5 all-to-all-start.2
  181.1 26.6 %copy-start.62 = (bf16[512,4,64]{0,2,1:T(8,128)(2,1)}, bf16[512,4,64]{0,2,1:T(8,128)(2,1)S(1)}, u32[]{:S(2)}) copy-start(bf16[512,4,64]{0,2,1:T(8,128)(2,1)S(1)} %reshape.358) | copy-start | bytes 786436
  183.4 22.7 %copy-start.32 = (bf16[512,4,64]{0,2,1:T(8,128)(2,1)}, bf16[512,4,64]{0,2,1:T(8,128)(2,1)S(1)}, u32[]{:S(2)}) copy-start(bf16[512,4,64]{0,2,1:T(8,128)(2,1)S(1)} %reshape.360) | copy-start | bytes 786436
  191.9 21.4 %all-to-all-start.3 = ((bf16[4,2,16384]{2,1,0:T(2,128)(2,1)}), bf16[4,2,16384]{2,1,0:T(2,128)(2,1)S(1)}, u32[]{:S(2)}, u32[]{:S(2)}) async-start(bf16[4,2,16384]{2,1,0:T(2,128)(2,1)} %reshape.419), calls=%async_computation.3 | async-start | bytes 524288 | tf_op jit(solution)/shard_map/all_to_all | solution.py:143
  209.9 19.5 %copy-start.74 = (bf16[128]{0:T(256)(128)(2,1)S(1)}, bf16[128]{0:T(256)(128)(2,1)}, u32[]{:S(2)}) copy-start(bf16[128]{0:T(256)(128)(2,1)} %param.29) | copy-start | bytes 772
  209.9 34.0 %copy-start.75 = (bf16[128]{0:T(256)(128)(2,1)S(1)}, bf16[128]{0:T(256)(128)(2,1)}, u32[]{:S(2)}) copy-start(bf16[128]{0:T(256)(128)(2,1)} %param.30) | copy-start | bytes 772
  209.9 47.1 %copy-start.76 = (bf16[128]{0:T(256)(128)(2,1)S(1)}, bf16[128]{0:T(256)(128)(2,1)}, u32[]{:S(2)}) copy-start(bf16[128]{0:T(256)(128)(2,1)} %param.31) | copy-start | bytes 772
  209.9 61.5 %copy-start.77 = (bf16[128]{0:T(256)(128)(2,1)S(1)}, bf16[128]{0:T(256)(128)(2,1)}, u32[]{:S(2)}) copy-start(bf16[128]{0:T(256)(128)(2,1)} %param.32) | copy-start | bytes 772
  209.9 75.2 %copy-start.78 = (bf16[128]{0:T(256)(128)(2,1)S(1)}, bf16[128]{0:T(256)(128)(2,1)}, u32[]{:S(2)}) copy-start(bf16[128]{0:T(256)(128)(2,1)} %param.33) | copy-start | bytes 772
  213.4 108.5 %all-to-all-start.7 = ((bf16[4,2,16384]{2,1,0:T(2,128)(2,1)}), bf16[4,2,16384]{2,1,0:T(2,128)(2,1)S(1)}, u32[]{:S(2)}, u32[]{:S(2)}) async-start(bf16[4,2,16384]{2,1,0:T(2,128)(2,1)} %reshape.427), calls=%async_computation.7 | async-start | bytes 524288 | tf_op jit(solution)/shard_map/all_to_all | solution.py:143
  217.0 462.8 %reduce-scatter.13.cloned.1.call-start = ((), (), s32[]{:S(2)}) async-start(), calls=%async_computation.31 | async-start | bytes 4718592 | tf_op jit(solution)/shard_map/reduce_scatter | solution.py:351
  458.3 15.3 %slice-start = ((s8[8388608]{0:T(1024)(128)(4,1)}), s8[4194304]{0:T(1024)(128)(4,1)S(1)}, s32[]{:S(2)}) async-start(s8[8388608]{0:T(1024)(128)(4,1)} %bitcast.320), calls=%async_computation.35 | async-start | bytes 8388608
  510.5 11.6 all-to-all-start.12
  522.1 11.7 all-to-all-start.8
  533.8 10.8 all-to-all-start.15
  544.7 8.6 all-to-all-start.11
  548.1 134.2 %reduce-scatter.11.cloned.1.call-start = ((), (), s32[]{:S(2)}) async-start(), calls=%async_computation.30 | async-start | bytes 4718592 | tf_op jit(solution)/shard_map/reduce_scatter | solution.py:350
  571.8 20.4 %all-to-all-start.10 = ((bf16[4,2,16384]{2,1,0:T(2,128)(2,1)}), bf16[4,2,16384]{2,1,0:T(2,128)(2,1)}, u32[]{:S(2)}, u32[]{:S(2)}) async-start(bf16[4,2,16384]{2,1,0:T(2,128)(2,1)} %reshape.437), calls=%async_computation.10 | async-start | bytes 524288 | tf_op jit(solution)/shard_map/all_to_all | solution.py:239
  592.2 9.5 all-to-all-start.14
  596.3 177.9 %reduce-scatter.9.cloned.1.call-start = ((), (), s32[]{:S(2)}) async-start(), calls=%async_computation.29 | async-start | bytes 4718592 | tf_op jit(solution)/shard_map/reduce_scatter | solution.py:349
  613.7 12.3 copy-start.14
  621.4 10.1 all-to-all-start.9
  631.5 9.3 all-to-all-start.13
  635.5 230.7 %reduce-scatter.7.cloned.1.call-start = ((), (), s32[]{:S(2)}) async-start(), calls=%async_computation.28 | async-start | bytes 4718592 | tf_op jit(solution)/shard_map/reduce_scatter | solution.py:348
  644.7 505.3 %reduce-scatter.15.cloned.1.call-start = ((), (), s32[]{:S(2)}) async-start(), calls=%async_computation.32 | async-start | bytes 18874368 | tf_op jit(solution)/shard_map/reduce_scatter | solution.py:352
  656.8 779.1 %reduce-scatter.17.cloned.1.call-start = ((), (), s32[]{:S(2)}) async-start(), calls=%async_computation.33 | async-start | bytes 18874368 | tf_op jit(solution)/shard_map/reduce_scatter | solution.py:353
  668.6 840.7 %all-reduce.14.cloned.1.call-start = ((), (), s32[]{:S(2)}) async-start(), calls=%async_computation.34 | async-start | bytes 6291456 | tf_op jit(solution)/shard_map/psum | solution.py:365
  1438.6 42.4 %copy-start.50 = (bf16[1,128,4,256]{1,3,2,0:T(8,128)(2,1)S(1)}, bf16[1,128,4,256]{1,3,2,0:T(8,128)(2,1)}, u32[]{:S(2)}) copy-start(bf16[1,128,4,256]{1,3,2,0:T(8,128)(2,1)} %copy.175) | copy-start | bytes 786436
  1438.6 42.4 %copy-start.55 = (f32[128,1024]{1,0:T(8,128)S(1)}, f32[128,1024]{1,0:T(8,128)}, u32[]{:S(2)}) copy-start(f32[128,1024]{1,0:T(8,128)} %convolution_add_fusion.10) | copy-start | bytes 1572868
  1438.7 45.0 %copy-start.47 = (bf16[1,128,4,256]{1,3,2,0:T(8,128)(2,1)S(1)}, bf16[1,128,4,256]{1,3,2,0:T(8,128)(2,1)}, u32[]{:S(2)}) copy-start(bf16[1,128,4,256]{1,3,2,0:T(8,128)(2,1)} %copy-done.46) | copy-start | bytes 786436
  (63 other events, 212.3 us)
Sparse Core Ops, SparseCore 0:
  10.2 48.7 all-gather.15
  61.1 47.7 all-gather.17
  111.1 47.7 all-gather.19
  160.8 47.7 all-gather.21
  210.6 122.5 all-gather.23
  335.2 123.0 all-gather.25
  500.6 89.3 reduce-scatter.12
  594.0 88.2 reduce-scatter.10
  685.9 88.1 reduce-scatter.8
  778.1 88.0 reduce-scatter.6
  870.0 280.0 reduce-scatter.14
  1154.1 281.7 reduce-scatter.16
  1439.3 69.9 all-reduce.13
where the time goes:
time: 1540 us; the launch traced here: 1530 us
  waiting for transfers between devices  984 us (64%)
  blocking collectives  168 us (11%)
  matrix products  126 us (8%)
  starting transfers between devices  80.5 us (5%)
  other arithmetic  77.6 us (5%)
  local copies, waits for them, and re-layouts  72.2 us (5%)
  between operations  17.3 us (1%)
    reduce_scatter x1, waiting for transfers between devices, body(): lax.psum_scatter(totals[5], 'fsdp', scatter_dimension=0, tiled=True)  283 us
    reduce_scatter x1, waiting for transfers between devices, body(): lax.psum_scatter(totals[4], 'fsdp', scatter_dimension=0, tiled=True)  282 us
    all_gather x1, waiting for transfers between devices, body(): lax.all_gather(down_weight, 'fsdp', axis=0, tiled=True)  116 us
    reduce_scatter x1, waiting for transfers between devices, body(): lax.psum_scatter(totals[0], 'fsdp', scatter_dimension=0, tiled=True)  90.2 us
    reduce_scatter x1, waiting for transfers between devices, body(): lax.psum_scatter(totals[1], 'fsdp', scatter_dimension=0, tiled=True)  90.1 us
    unnamed x229, local copies, waits for them, and re-layouts  49.8 us
    unnamed x19, other arithmetic  41.9 us
    dot_general x12, matrix products, matmul(): return jnp.dot(left_side, right_side, preferred_element_type=jnp.float32)  36.2 us
  transfers between devices with their start and end apart: 29, of which 16 were waited for; matrix products, arithmetic and copies ran while one was open for 14% of the time, Pallas kernels for 0%

commit v1 on v0

v1 whole, which is shorter than its diff:
```python
import functools
import math

import jax
import jax.numpy as jnp
from jax import lax
from jax.experimental import pallas as pl
from jax.experimental.pallas import tpu as pltpu
from jax.sharding import Mesh, PartitionSpec as P

HD = 64
EPSILON = 1e-05
F32 = jnp.float32
BF16 = jnp.bfloat16
SEQ = ("x", "c")
FSDP = ("z", "y")
SEQ_N = 4
VEC = 16
ROW_QB, ROW_VB, ROW_OB, ROW_DB, ROW_G1, ROW_S1, ROW_G2, ROW_S2, ROW_UB = range(9)
VMEM = pltpu.VMEM
ANY = pl.ANY


def dot(a, b):
    return lax.dot_general(a, b, (((1,), (0,)), ((), ())), preferred_element_type=F32)


def dot_nt(a, b):
    return lax.dot_general(a, b, (((1,), (1,)), ((), ())), preferred_element_type=F32)


def dot_tn(a, b):
    return lax.dot_general(a, b, (((0,), (0,)), ((), ())), preferred_element_type=F32)


def struct(shape, dtype):
    return jax.ShapeDtypeStruct(shape, dtype)


def nbytes(tree):
    return sum(math.prod(a.shape) * a.dtype.itemsize for a in jax.tree.leaves(tree))


def whole(space=VMEM):
    return pl.BlockSpec(memory_space=space)


def call(kernel, outs, args, *, name, grid=None, in_specs=None, out_specs=None, scratch=(), flops=0, trans=0):
    if in_specs is None:
        in_specs = [whole() for _ in args]
    if out_specs is None:
        out_specs = jax.tree.map(lambda _: whole(), outs)
    kwargs = {} if grid is None else {"grid": grid}
    return pl.pallas_call(
        kernel,
        out_shape=outs,
        in_specs=in_specs,
        out_specs=out_specs,
        scratch_shapes=list(scratch),
        compiler_params=pltpu.CompilerParams(vmem_limit_bytes=56 << 20),
        cost_estimate=pl.CostEstimate(
            flops=flops, bytes_accessed=nbytes(args) + nbytes(outs), transcendentals=trans
        ),
        name=name,
        **kwargs,
    )(*args)


def seq_swap(value, k):
    return lax.ppermute(value, SEQ, [(i, i ^ k) for i in range(SEQ_N)])


def gather_seq(value):
    far = seq_swap(value, 2)
    near = seq_swap(value, 1)
    return [value, near, far, seq_swap(far, 1)]


def reduce_seq(parts):
    near0 = seq_swap(parts[1], 1)
    near2 = seq_swap(parts[3], 1)
    onward = (parts[2].astype(F32) + near2.astype(F32)).astype(BF16)
    return [parts[0], near0, seq_swap(onward, 2)]


def exchange_seq(parts):
    return [parts[0]] + [seq_swap(parts[r], r) for r in (1, 2, 3)]


def fsdp_swap(value, k, count):
    return lax.ppermute(value, FSDP, [(i, i ^ k) for i in range(count)])


def early_pack_kernel(ids, wq, wk, wv, wo, vec, out, sems):
    s = ids[0]
    n = wq.shape[0]
    c = wq.shape[1] // SEQ_N
    cols = pl.ds(pl.multiple_of(s * c, c), c)
    copies = [
        pltpu.make_async_copy(w.at[:, cols], out.at[pl.ds(0, n), pl.ds(i * c, c)], sems.at[i])
        for i, w in enumerate((wq, wk, wv, wo))
    ]
    copies.append(
        pltpu.make_async_copy(vec, out.at[pl.ds(n, VEC), pl.ds(0, n)], sems.at[SEQ_N])
    )
    for copy in copies:
        copy.start()
    for copy in copies:
        copy.wait()


def late_pack_kernel(fs, ids, up, down, out, sems):
    s = ids[0]
    n = up.shape[0]
    w = up.shape[1] // fs // SEQ_N
    copies = []
    for j in range(fs):
        cols = pl.ds(pl.multiple_of((j * SEQ_N + s) * w, w), w)
        copies.append(
            pltpu.make_async_copy(
                up.at[:, cols], out.at[pl.ds(0, n), pl.ds(j * w, w)], sems.at[j]
            )
        )
    rows = pl.ds(pl.multiple_of(s * w, w), w)
    copies.append(pltpu.make_async_copy(down.at[rows, :], out.at[pl.ds(n, w), :], sems.at[fs]))
    for copy in copies:
        copy.start()
    for copy in copies:
        copy.wait()


def pack_weights(ids, s, fs, wq, wk, wv, wo, up, down, vectors):
    n, d = wq.shape
    up_bias = vectors.pop("up_bias")
    rows = jnp.stack([vectors[k] for k in sorted(vectors)], 0)
    rows = jnp.concatenate([rows, up_bias.reshape(SEQ_N, n)], 0)
    vec = jnp.pad(rows, ((0, VEC - rows.shape[0]), (0, 0)))
    w = up.shape[1] // fs // SEQ_N
    c = d // SEQ_N
    if n % 128 == 0:
        early = call(
            early_pack_kernel,
            struct((n + VEC, d), BF16),
            (ids, wq, wk, wv, wo, vec),
            name="early_pack",
            in_specs=[whole(pltpu.SMEM)] + [whole(ANY)] * 5,
            out_specs=whole(ANY),
            scratch=[pltpu.SemaphoreType.DMA((SEQ_N + 1,))],
        )
        late = call(
            functools.partial(late_pack_kernel, fs),
            struct((n + w, d), BF16),
            (ids, up, down),
            name="late_pack",
            in_specs=[whole(pltpu.SMEM)] + [whole(ANY)] * 2,
            out_specs=whole(ANY),
            scratch=[pltpu.SemaphoreType.DMA((fs + 1,))],
        )
        return early, late
    four = [lax.dynamic_slice(m, (0, s * c), (n, c)) for m in (wq, wk, wv, wo)]
    early = jnp.concatenate(
        [jnp.concatenate(four, 1), jnp.pad(vec, ((0, 0), (0, d - n)))], 0
    )
    mine = lax.dynamic_index_in_dim(up.reshape(n, fs, SEQ_N, w), s, 2, keepdims=False)
    late = jnp.concatenate(
        [mine.reshape(n, fs * w), lax.dynamic_slice(down, (s * w, 0), (w, d))], 0
    )
    return early, late


def assemble_kernel(fs, ids, *refs):
    pieces, (wqkv, wo, vec, held, sems) = refs[:fs], refs[fs:]
    f = ids[1]
    n = pieces[0].shape[0] - VEC
    c3 = wqkv.shape[1]
    c = wo.shape[1]
    copies, vecs = [], []
    for g in range(fs):
        place = pl.multiple_of((f ^ g) * n, n)
        vecs.append(
            pltpu.make_async_copy(
                pieces[g].at[pl.ds(n, VEC), pl.ds(0, n)], held.at[g], sems.at[g, 0]
            )
        )
        copies.append(
            pltpu.make_async_copy(
                pieces[g].at[pl.ds(0, n), pl.ds(0, c3)], wqkv.at[pl.ds(place, n), :], sems.at[g, 1]
            )
        )
        copies.append(
            pltpu.make_async_copy(
                pieces[g].at[pl.ds(0, n), pl.ds(c3, c)], wo.at[pl.ds(place, n), :], sems.at[g, 2]
            )
        )
    for copy in vecs + copies:
        copy.start()
    for g in range(fs):
        vecs[g].wait()
        vec[:, pl.ds(pl.multiple_of((f ^ g) * n, n), n)] = held[g].astype(F32)
    for copy in copies:
        copy.wait()


def gather_early(ids, early, fs):
    n = early.shape[0] - VEC
    d = early.shape[1]
    c = d // SEQ_N
    if fs == 8 and n % 128 == 0:
        pieces = [None] * fs
        pieces[0] = early
        for g in (2, 4, 6):
            pieces[g] = fsdp_swap(early, g, fs)
        for g in (0, 2, 4, 6):
            pieces[g + 1] = fsdp_swap(pieces[g], 1, fs)
        outs = (struct((d, 3 * c), BF16), struct((d, c), BF16), struct((VEC, d), F32))
        return call(
            functools.partial(assemble_kernel, fs),
            outs,
            (ids, *pieces),
            name="assemble",
            in_specs=[whole(pltpu.SMEM)] + [whole(ANY)] * fs,
            out_specs=(whole(ANY), whole(ANY), whole()),
            scratch=[VMEM((fs, VEC, n), BF16), pltpu.SemaphoreType.DMA((fs, 3))],
        )
    full = lax.all_gather(early, FSDP)
    weights = full[:, :n].reshape(d, d)
    vec = full[:, n:, :n].transpose(1, 0, 2).reshape(VEC, d).astype(F32)
    return weights[:, : 3 * c], weights[:, 3 * c :], vec


def attend_kernel(ids, x0, x1, x2, x3, w, vec, qkv, lse, m0, m1, m2, m3, held, mix):
    c = w.shape[1] // 3
    heads = c // HD
    block = x0.shape[1]
    length = SEQ_N * block
    for r, x in enumerate((x0, x1, x2, x3)):
        held[r * block : (r + 1) * block, :] = x[0]
    cols = pl.ds(pl.multiple_of(ids[0] * c, c), c)
    for part in range(3):
        acc = dot(held[...], w[:, part * c : (part + 1) * c])
        if part != 1:
            row = ROW_QB if part == 0 else ROW_VB
            acc = acc + vec[row : row + 1, cols]
        qkv[0, :, part * c : (part + 1) * c] = acc.astype(BF16)
    scale = 1.0 / math.sqrt(HD)
    for h in range(heads):
        at = h * HD
        query = (qkv[0, :, at : at + HD].astype(F32) * scale).astype(BF16)
        key = qkv[0, :, c + at : c + at + HD]
        value = qkv[0, :, 2 * c + at : 2 * c + at + HD]
        scores = dot_nt(key, query)
        highest = jnp.max(scores, 0, keepdims=True)
        raised = jnp.exp(scores - highest)
        summed = jnp.sum(raised, 0, keepdims=True)
        lse[0, h : h + 1, :] = highest + jnp.log(summed)
        low = (raised * (1.0 / summed)).astype(BF16)
        mix[at : at + HD, :] = dot_tn(value, low)
    mixture = mix[...].T.astype(BF16)
    for r, m in enumerate((m0, m1, m2, m3)):
        m[0] = mixture[r * block : (r + 1) * block, :]


def attend(ids, blocks, wqkv, vec):
    nb, block, d = blocks[0].shape
    c = wqkv.shape[1] // 3
    length = SEQ_N * block
    heads = c // HD
    one = lambda shape: pl.BlockSpec((1,) + shape, lambda b: (b,) + (0,) * len(shape))
    fixed = lambda shape: pl.BlockSpec(shape, lambda b: (0,) * len(shape))
    outs = (
        struct((nb, length, 3 * c), BF16),
        struct((nb, heads, length), F32),
    ) + (struct((nb, block, c), BF16),) * SEQ_N
    return call(
        attend_kernel,
        outs,
        (ids, *blocks, wqkv, vec),
        name="attend",
        grid=(nb,),
        in_specs=[whole(pltpu.SMEM)]
        + [one((block, d))] * SEQ_N
        + [fixed(wqkv.shape), fixed(vec.shape)],
        out_specs=(one((length, 3 * c)), one((heads, length))) + (one((block, c)),) * SEQ_N,
        scratch=[VMEM((length, d), BF16), VMEM((c, length), F32)],
        flops=2 * nb * length * (3 * c * d + 2 * length * c),
        trans=nb * heads * length * length,
    )


def attend_back_kernel(qkv, lse, h0, h1, h2, h3, w, back, sums, r0, r1, r2, r3, held, turned):
    c = w.shape[1] // 3
    heads = c // HD
    block = h0.shape[1]
    for r, h in enumerate((h0, h1, h2, h3)):
        held[r * block : (r + 1) * block, :] = h[0]
    scale = 1.0 / math.sqrt(HD)
    for h in range(heads):
        at = h * HD
        query = (qkv[0, :, at : at + HD].astype(F32) * scale).astype(BF16)
        key = qkv[0, :, c + at : c + at + HD]
        value = qkv[0, :, 2 * c + at : 2 * c + at + HD]
        grad = held[:, at : at + HD]
        scores = dot_nt(key, query)
        attention = jnp.exp(scores - lse[0, h : h + 1, :])
        attention_grad = dot_nt(value, grad)
        inner = jnp.sum(attention * attention_grad, 0, keepdims=True)
        low = (attention * (attention_grad - inner)).astype(BF16)
        turned[at : at + HD, :] = dot_tn(key, low) * scale
        back[0, :, c + at : c + at + HD] = dot(low, query).astype(BF16)
        back[0, :, 2 * c + at : 2 * c + at + HD] = dot(attention.astype(BF16), grad).astype(BF16)
    back[0, :, 0:c] = turned[...].T.astype(BF16)
    whole_back = back[0]
    total = jnp.sum(whole_back.astype(F32), 0, keepdims=True)

    @pl.when(pl.program_id(0) == 0)
    def _():
        sums[...] = jnp.zeros_like(sums)

    sums[0:1, :] += total
    for r, out in enumerate((r0, r1, r2, r3)):
        out[0] = dot_nt(back[0, r * block : (r + 1) * block, :], w[...]).astype(BF16)


def attend_back(qkv, lse, grads, wqkv):
    nb, length, c3 = qkv.shape
    d = wqkv.shape[0]
    block = length // SEQ_N
    c = c3 // 3
    heads = c // HD
    one = lambda shape: pl.BlockSpec((1,) + shape, lambda b: (b,) + (0,) * len(shape))
    fixed = lambda shape: pl.BlockSpec(shape, lambda b: (0,) * len(shape))
    outs = (struct((nb, length, c3), BF16), struct((8, c3), F32)) + (
        struct((nb, block, d), BF16),
    ) * SEQ_N
    return call(
        attend_back_kernel,
        outs,
        (qkv, lse, *grads, wqkv),
        name="attend_back",
        grid=(nb,),
        in_specs=[one((length, c3)), one((heads, length))]
        + [one((block, c))] * SEQ_N
        + [fixed(wqkv.shape)],
        out_specs=(one((length, c3)), fixed((8, c3))) + (one((block, d)),) * SEQ_N,
        scratch=[VMEM((length, c), BF16), VMEM((c, length), F32)],
        flops=2 * nb * length * (c3 * d + 5 * length * c),
        trans=nb * heads * length * length,
    )


def row_norm(hidden):
    average = jnp.mean(hidden, -1, keepdims=True)
    centered = hidden - average
    spread = jnp.mean(centered * centered, -1, keepdims=True)
    scale = lax.rsqrt(spread + EPSILON)
    return centered * scale, scale


def norm_back(grad, normed, scale, gain):
    inner = grad * gain
    first = jnp.mean(inner, -1, keepdims=True)
    second = jnp.mean(inner * normed, -1, keepdims=True)
    return scale * (inner - first - normed * second)


def out_kernel(ids, m0, m1, m2, m3, w0, w1, w2, w3, tokens, vec, attn_sum, normed, low, mix):
    s = ids[0]
    c = m0.shape[1]
    places = [pl.ds(pl.multiple_of((s ^ r) * c, c), c) for r in range(SEQ_N)]
    for place, m in zip(places, (m0, m1, m2, m3)):
        mix[:, place] = m[...]
    for place, w in zip(places, (w0, w1, w2, w3)):
        attn_sum[:, place] = dot(mix[...], w[...])
    hidden = tokens[...].astype(F32) + attn_sum[...] + vec[ROW_OB : ROW_OB + 1, :]
    attn_sum[...] = hidden
    unit, _ = row_norm(hidden)
    first = unit * vec[ROW_G1 : ROW_G1 + 1, :] + vec[ROW_S1 : ROW_S1 + 1, :]
    normed[...] = first
    low[...] = first.astype(BF16)


def out_project(ids, mixtures, wo, tokens, vec):
    rows, d = tokens.shape
    outs = (
        struct((rows, d), F32),
        struct((rows, d), F32),
        struct((rows, d), BF16),
        struct((rows, d), BF16),
    )
    args = (ids, *mixtures, *wo, tokens, vec)
    return call(
        out_kernel,
        outs,
        args,
        name="out_project",
        in_specs=[whole(pltpu.SMEM)] + [whole()] * (len(args) - 1),
        flops=2 * rows * d * d,
    )


def second_norm_kernel(normed, p0, p1, p2, cotangent, vec, layer_out, ffn_grad, low, sums):
    hidden = (
        normed[...]
        + (p0[...].astype(F32) + p1[...].astype(F32) + p2[...].astype(F32))
        + vec[ROW_DB : ROW_DB + 1, :]
    )
    unit, scale = row_norm(hidden)
    gain = vec[ROW_G2 : ROW_G2 + 1, :]
    layer_out[...] = (unit * gain + vec[ROW_S2 : ROW_S2 + 1, :]).astype(BF16)
    grad = cotangent[...].astype(F32)
    back = norm_back(grad, unit, scale, gain)
    ffn_grad[...] = back
    rounded = back.astype(BF16)
    low[...] = rounded
    sums[...] = jnp.zeros_like(sums)
    sums[0:1, :] = jnp.sum(grad * unit, 0, keepdims=True)
    sums[1:2, :] = jnp.sum(grad, 0, keepdims=True)
    sums[2:3, :] = jnp.sum(rounded.astype(F32), 0, keepdims=True)


def second_norm(normed, parts, cotangent, vec):
    rows, d = normed.shape
    outs = (
        struct((rows, d), BF16),
        struct((rows, d), F32),
        struct((rows, d), BF16),
        struct((8, d), F32),
    )
    return call(
        second_norm_kernel, outs, (normed, *parts, cotangent, vec), name="second_norm", flops=30 * rows * d
    )


def first_norm_kernel(ids, ffn_grad, p0, p1, p2, attn_sum, vec, mix, w0, w1, w2, w3,
                      attn_grad, sums, n0, n1, n2, n3, d0, d1, d2, d3, low, back):
    s = ids[0]
    c = w0.shape[1]
    grad = ffn_grad[...] + (p0[...].astype(F32) + p1[...].astype(F32) + p2[...].astype(F32))
    unit, scale = row_norm(attn_sum[...])
    gain = vec[ROW_G1 : ROW_G1 + 1, :]
    value = norm_back(grad, unit, scale, gain)
    attn_grad[...] = value
    rounded = value.astype(BF16)
    low[...] = rounded
    sums[...] = jnp.zeros_like(sums)
    sums[0:1, :] = jnp.sum(grad * unit, 0, keepdims=True)
    sums[1:2, :] = jnp.sum(grad, 0, keepdims=True)
    sums[2:3, :] = jnp.sum(rounded.astype(F32), 0, keepdims=True)
    places = [pl.ds(pl.multiple_of((s ^ r) * c, c), c) for r in range(SEQ_N)]
    total = dot_nt(low[:, places[0]], w0[...])
    for place, w in zip(places[1:], (w1, w2, w3)):
        total = total + dot_nt(low[:, place], w[...])
    back[...] = total
    for place, n in zip(places, (n0, n1, n2, n3)):
        n[...] = back[:, place].astype(BF16)
    for place, d in zip(places, (d0, d1, d2, d3)):
        d[...] = dot_tn(mix[...], low[:, place]).astype(BF16)


def first_norm(ids, ffn_grad, parts, attn_sum, vec, mix, wo):
    rows, d = ffn_grad.shape
    c = wo[0].shape[1]
    outs = (
        (struct((rows, d), F32), struct((8, d), F32))
        + (struct((rows, c), BF16),) * SEQ_N
        + (struct((d, c), BF16),) * SEQ_N
    )
    args = (ids, ffn_grad, *parts, attn_sum, vec, mix, *wo)
    return call(
        first_norm_kernel,
        outs,
        args,
        name="first_norm",
        in_specs=[whole(pltpu.SMEM)] + [whole()] * (len(args) - 1),
        scratch=[VMEM((rows, d), BF16), VMEM((rows, d), F32)],
        flops=4 * rows * d * d,
    )


TILE = 256
HALF = 512


def ffn_kernel(n, ids, f0, f1, f2, f3, weights, vec, p0, p1, p2, p3, gelu, slope, held, acc):
    fs = weights.shape[0]
    rows, d = f0.shape
    hidden = gelu.shape[1]
    for r, f in enumerate((f0, f1, f2, f3)):
        held[r * rows : (r + 1) * rows, :] = f[...]
    tiles = hidden // TILE
    per = fs // tiles
    inv = 1.0 / math.sqrt(2.0)
    norm = 1.0 / math.sqrt(2.0 * math.pi)

    def step(i, carry):
        part, t = i // tiles, i % tiles
        at = pl.ds(pl.multiple_of(part * HALF, HALF), HALF)
        cols = pl.ds(pl.multiple_of(t * TILE, TILE), TILE)
        up = weights[:, 0:n, cols].reshape(d, TILE)
        u = dot(held[at, :], up) + vec[pl.ds(ROW_UB + ids[0], 1), cols]
        phi = 0.5 * lax.erf(u * inv) + 0.5
        g = (u * phi).astype(BF16)
        gelu[at, cols] = g
        slope[at, cols] = phi + u * (norm * jnp.exp(-0.5 * u * u))
        down = weights[pl.ds(t * per, per), n:, :].reshape(TILE, d)
        y = dot(g, down)

        @pl.when(t == 0)
        def _():
            acc[at, :] = y

        @pl.when(t > 0)
        def _():
            acc[at, :] += y

        return carry

    lax.fori_loop(0, (SEQ_N * rows // HALF) * tiles, step, 0)
    for r, p in enumerate((p0, p1, p2, p3)):
        p[...] = acc[r * rows : (r + 1) * rows, :].astype(BF16)


def ffn(ids, blocks, weights, vec):
    rows, d = blocks[0].shape
    fs = weights.shape[0]
    n = d // fs
    hidden = fs * (weights.shape[1] - n)
    total = SEQ_N * rows
    outs = (struct((rows, d), BF16),) * SEQ_N + (
        struct((total, hidden), BF16),
        struct((total, hidden), F32),
    )
    args = (ids, *blocks, weights, vec)
    return call(
        functools.partial(ffn_kernel, n),
        outs,
        args,
        name="ffn",
        in_specs=[whole(pltpu.SMEM)] + [whole()] * (len(args) - 1),
        scratch=[VMEM((total, d), BF16), VMEM((total, d), F32)],
        flops=4 * total * d * hidden,
        trans=2 * total * hidden,
    )


def ffn_back_kernel(n, d0, d1, d2, d3, weights, slope, q0, q1, q2, q3, up_low, sums, held, acc):
    fs = weights.shape[0]
    rows, d = d0.shape
    hidden = up_low.shape[1]
    for r, x in enumerate((d0, d1, d2, d3)):
        held[r * rows : (r + 1) * rows, :] = x[...]
    tiles = hidden // TILE
    per = fs // tiles
    sums[...] = jnp.zeros_like(sums)

    def step(i, carry):
        part, t = i // tiles, i % tiles
        at = pl.ds(pl.multiple_of(part * HALF, HALF), HALF)
        cols = pl.ds(pl.multiple_of(t * TILE, TILE), TILE)
        down = weights[pl.ds(t * per, per), n:, :].reshape(TILE, d)
        u = (dot_nt(held[at, :], down) * slope[at, cols]).astype(BF16)
        up_low[at, cols] = u
        sums[0:1, cols] += jnp.sum(u.astype(F32), 0, keepdims=True)
        up = weights[:, 0:n, cols].reshape(d, TILE)
        y = dot_nt(u, up)

        @pl.when(t == 0)
        def _():
            acc[at, :] = y

        @pl.when(t > 0)
        def _():
            acc[at, :] += y

        return carry

    lax.fori_loop(0, (SEQ_N * rows // HALF) * tiles, step, 0)
    for r, q in enumerate((q0, q1, q2, q3)):
        q[...] = acc[r * rows : (r + 1) * rows, :].astype(BF16)


def ffn_back(blocks, weights, slope):
    rows, d = blocks[0].shape
    fs = weights.shape[0]
    total, hidden = slope.shape
    outs = (struct((rows, d), BF16),) * SEQ_N + (
        struct((total, hidden), BF16),
        struct((8, hidden), F32),
    )
    return call(
        functools.partial(ffn_back_kernel, d // fs),
        outs,
        (*blocks, weights, slope),
        name="ffn_back",
        scratch=[VMEM((total, d), BF16), VMEM((total, d), F32)],
        flops=4 * total * d * hidden,
    )


def ffn_grads_kernel(f0, f1, f2, f3, up_low, gelu, d0, d1, d2, d3, out, held):
    rows = f0.shape[0]
    per, both, d = out.shape
    n = both // 2

    @pl.when(pl.program_id(0) == 0)
    def _():
        for r, x in enumerate((d0, d1, d2, d3)):
            held[r * rows : (r + 1) * rows, :] = x[...]

    left = jnp.concatenate([f0[...], f1[...], f2[...], f3[...]], 0)
    out[:, 0:n, :] = dot_tn(left, up_low[...]).astype(BF16).reshape(per, n, d)
    out[:, n:, :] = dot_tn(gelu[...], held[...]).astype(BF16).reshape(per, n, d)


def ffn_grads(blocks, up_low, gelu, downs, fs):
    rows, d = blocks[0].shape
    total, hidden = gelu.shape
    steps = d // TILE
    n = d // fs
    col = lambda shape: pl.BlockSpec(shape, lambda i: (0, i))
    fixed = lambda shape: pl.BlockSpec(shape, lambda i: (0,) * len(shape))
    return call(
        ffn_grads_kernel,
        struct((fs, 2 * n, d), BF16),
        (*blocks, up_low, gelu, *downs),
        name="ffn_grads",
        grid=(steps,),
        in_specs=[col((rows, TILE))] * SEQ_N
        + [fixed((total, hidden)), col((total, TILE))]
        + [fixed((rows, d))] * SEQ_N,
        out_specs=pl.BlockSpec((fs // steps, 2 * n, d), lambda i: (i, 0, 0)),
        scratch=[VMEM((total, d), BF16)],
        flops=4 * total * d * hidden,
    )


def qkvo_grads_kernel(x0, x1, x2, x3, back, o0, o1, o2, out, held):
    nb, block, tile = x0.shape
    length = SEQ_N * block
    for b in range(nb):
        for r, x in enumerate((x0, x1, x2, x3)):
            held[b * length + r * block : b * length + (r + 1) * block, :] = x[b]
    c3 = back.shape[1]
    out[:, 0:c3] = dot_tn(held[...], back[...]).astype(BF16)
    total = o0[...].astype(F32) + o1[...].astype(F32) + o2[...].astype(F32)
    out[:, c3:] = total.astype(BF16)


def qkvo_grads(blocks, back, out_parts):
    nb, block, d = blocks[0].shape
    total, c3 = back.shape
    c = c3 // 3
    col = lambda i: (0, 0, i)
    return call(
        qkvo_grads_kernel,
        struct((d, c3 + c), BF16),
        (*blocks, back, *out_parts),
        name="qkvo_grads",
        grid=(d // TILE,),
        in_specs=[pl.BlockSpec((nb, block, TILE), col)] * SEQ_N
        + [pl.BlockSpec((total, c3), lambda i: (0, 0))]
        + [pl.BlockSpec((TILE, c), lambda i: (i, 0))] * 3,
        out_specs=pl.BlockSpec((TILE, c3 + c), lambda i: (i, 0)),
        scratch=[VMEM((total, TILE), BF16)],
        flops=2 * total * d * c3,
    )


def fill_vectors(s, vec, back_sums, first_sums, second_sums, up_sums):
    c = vec.shape[1] // SEQ_N
    vec[...] = jnp.zeros_like(vec)
    cols = pl.ds(pl.multiple_of(s * c, c), c)
    vec[ROW_QB : ROW_QB + 1, cols] = back_sums[0:1, 0:c]
    vec[ROW_VB : ROW_VB + 1, cols] = back_sums[0:1, 2 * c : 3 * c]
    vec[ROW_OB : ROW_OB + 1, :] = first_sums[2:3, :]
    vec[ROW_DB : ROW_DB + 1, :] = second_sums[2:3, :]
    vec[ROW_G1 : ROW_G1 + 1, :] = first_sums[0:1, :]
    vec[ROW_S1 : ROW_S1 + 1, :] = first_sums[1:2, :]
    vec[ROW_G2 : ROW_G2 + 1, :] = second_sums[0:1, :]
    vec[ROW_S2 : ROW_S2 + 1, :] = second_sums[1:2, :]
    vec[pl.ds(ROW_UB + s, 1), :] = up_sums[0:1, :]


def split_kernel(fs, ids, grads, back_sums, first_sums, second_sums, up_sums, *refs):
    outs, (vec, vec_low, sems) = refs[:fs], refs[fs:]
    s, f = ids[0], ids[1]
    n = outs[0].shape[0] - VEC
    copies = []
    for g in range(fs):
        rows = pl.ds(pl.multiple_of((f ^ g) * n, n), n)
        copies.append(
            pltpu.make_async_copy(grads.at[rows, :], outs[g].at[pl.ds(0, n), :], sems.at[g, 0])
        )
    for copy in copies:
        copy.start()
    fill_vectors(s, vec, back_sums, first_sums, second_sums, up_sums)
    vec_low[...] = jnp.zeros_like(vec_low)
    small = []
    for g in range(fs):
        cols = pl.ds(pl.multiple_of((f ^ g) * n, n), n)
        vec_low[g * VEC : (g + 1) * VEC, 0:n] = vec[:, cols].astype(BF16)
        small.append(
            pltpu.make_async_copy(
                vec_low.at[pl.ds(g * VEC, VEC), :], outs[g].at[pl.ds(n, VEC), :], sems.at[g, 1]
            )
        )
    for copy in small:
        copy.start()
    for copy in copies + small:
        copy.wait()


def vectors_kernel(ids, back_sums, first_sums, second_sums, up_sums, vec):
    fill_vectors(ids[0], vec, back_sums, first_sums, second_sums, up_sums)


def scatter_late(ids, grads, sums, fs):
    d = grads.shape[0]
    n = d // fs
    if fs == 8 and n % 128 == 0:
        pieces = call(
            functools.partial(split_kernel, fs),
            (struct((n + VEC, d), BF16),) * fs,
            (ids, grads, *sums),
            name="split",
            in_specs=[whole(pltpu.SMEM), whole(ANY)] + [whole()] * 4,
            out_specs=(whole(ANY),) * fs,
            scratch=[
                VMEM((VEC, d), F32),
                VMEM((fs * VEC, d), BF16),
                pltpu.SemaphoreType.DMA((fs, 2)),
            ],
        )
        add = lambda a, b: a.astype(F32) + b.astype(F32)
        total = None
        for g in (2, 4, 6, 0):
            here = add(pieces[g], fsdp_swap(pieces[g + 1], 1, fs))
            if g:
                here = fsdp_swap(here.astype(BF16), g, fs).astype(F32)
            total = here if total is None else total + here
        return total.astype(BF16)
    vec = call(
        vectors_kernel,
        struct((VEC, d), F32),
        (ids, *sums),
        name="vectors",
        in_specs=[whole(pltpu.SMEM)] + [whole()] * 4,
    )
    small = vec.reshape(VEC, fs, n).transpose(1, 0, 2).astype(BF16)
    small = jnp.pad(small, ((0, 0), (0, 0), (0, d - n)))
    packed = jnp.concatenate([grads.reshape(fs, n, d), small], 1)
    return lax.psum_scatter(packed.reshape(fs * (n + VEC), d), FSDP, scatter_dimension=0, tiled=True)


def finish_kernel(fs, ids, c0, c1, c2, c3, e0, e1, e2, e3, wq, wk, wv, wo, up, down, *vectors):
    s = ids[0]
    n = wq.shape[0]
    c = wq.shape[1] // SEQ_N
    w = up.shape[1] // fs // SEQ_N
    total = 0.0
    for r, (small, large) in enumerate(((c0, e0), (c1, e1), (c2, e2), (c3, e3))):
        at = s ^ r
        cols = pl.ds(pl.multiple_of(at * c, c), c)
        for i, out in enumerate((wq, wk, wv, wo)):
            out[:, cols] = small[0:n, i * c : (i + 1) * c].astype(F32)
        total = total + small[n:, 0:n].astype(F32)
        for j in range(fs):
            place = pl.ds(pl.multiple_of((j * SEQ_N + at) * w, w), w)
            up[:, place] = large[0:n, j * w : (j + 1) * w].astype(F32)
        down[pl.ds(pl.multiple_of(at * w, w), w), :] = large[n:, :].astype(F32)
    for row, out in enumerate(vectors[:ROW_UB]):
        out[...] = total[row : row + 1, :].reshape(n)
    for j in range(SEQ_N):
        vectors[ROW_UB][j * n : (j + 1) * n] = total[ROW_UB + j : ROW_UB + j + 1, :].reshape(n)


def finish(ids, s, small, large, fs):
    d = small[0].shape[1]
    n = d // fs
    c = d // SEQ_N
    w = large[0].shape[0] - n
    hidden = SEQ_N * fs * w
    if n % 128 == 0:
        outs = (
            (struct((n, d), F32),) * 4
            + (struct((n, hidden), F32), struct((SEQ_N * w, d), F32))
            + (struct((n,), F32),) * ROW_UB
            + (struct((SEQ_N * w,), F32),)
        )
        done = call(
            functools.partial(finish_kernel, fs),
            outs,
            (ids, *small, *large),
            name="finish",
            in_specs=[whole(pltpu.SMEM)] + [whole()] * 8,
        )
        return done[:4], done[4], done[5], done[6:]
    order = jnp.arange(SEQ_N) ^ s
    small = jnp.stack(small)[order].astype(F32)
    large = jnp.stack(large)[order].astype(F32)
    four = small[:, :n].reshape(SEQ_N, n, 4, c).transpose(2, 1, 0, 3).reshape(4, n, d)
    up = large[:, :n].reshape(SEQ_N, n, fs, w).transpose(1, 2, 0, 3).reshape(n, hidden)
    down = large[:, n:].reshape(SEQ_N * w, d)
    total = jnp.sum(small[:, n:, :n], 0)
    vectors = [total[row] for row in range(ROW_UB)]
    vectors.append(total[ROW_UB : ROW_UB + SEQ_N].reshape(SEQ_N * w))
    return [four[i] for i in range(4)], up, down, vectors


def body(fs, tokens_in, cotangent, query_weight, key_weight, value_weight, out_weight, up_weight,
         down_weight, query_bias, value_bias, out_bias, up_bias, down_bias, first_gain, first_shift,
         second_gain, second_shift):
    nb, block, d = tokens_in.shape
    rows = nb * block
    s = lax.axis_index(SEQ)
    f = lax.axis_index(FSDP)
    ids = jnp.stack([s, f]).astype(jnp.int32)
    flat = lambda a: a.reshape(rows, a.shape[-1])
    deep = lambda a: a.reshape(nb, block, a.shape[-1])

    vectors = {
        ROW_QB: query_bias, ROW_VB: value_bias, ROW_OB: out_bias, ROW_DB: down_bias,
        ROW_G1: first_gain, ROW_S1: first_shift, ROW_G2: second_gain, ROW_S2: second_shift,
        "up_bias": up_bias,
    }
    up_bias = vectors.pop("up_bias")
    named = {f"{k:02d}": v for k, v in vectors.items()}
    named["up_bias"] = up_bias
    early, late = pack_weights(
        ids, s, fs, query_weight, key_weight, value_weight, out_weight, up_weight, down_weight, named
    )
    weights = lax.all_gather(late, FSDP)
    tokens = gather_seq(tokens_in)
    wqkv, wo_own, vec = gather_early(ids, early, fs)
    wo = gather_seq(wo_own)

    qkv, lse, *mixtures = attend(ids, tokens, wqkv, vec)
    mixtures = exchange_seq([flat(m) for m in mixtures])
    attn_sum, normed, first_low, mix = out_project(ids, mixtures, wo, flat(tokens_in), vec)
    firsts = gather_seq(first_low)
    *parts, gelu, slope = ffn(ids, firsts, weights, vec)
    layer_out, ffn_grad, down_low, second_sums = second_norm(
        normed, reduce_seq(parts), flat(cotangent), vec
    )
    downs = gather_seq(down_low)
    *parts, up_low, up_sums = ffn_back(downs, weights, slope)
    packed = ffn_grads(firsts, up_low, gelu, downs, fs)
    large = lax.psum_scatter(
        packed.reshape(-1, d), FSDP, scatter_dimension=0, tiled=True
    )
    attn_grad, first_sums, *pieces = first_norm(
        ids, ffn_grad, reduce_seq(parts), attn_sum, vec, mix, wo
    )
    grads = exchange_seq(pieces[:SEQ_N])
    out_parts = reduce_seq(pieces[SEQ_N:])
    back, back_sums, *parts = attend_back(qkv, lse, [deep(g) for g in grads], wqkv)
    qkvo = qkvo_grads(tokens, back.reshape(-1, back.shape[-1]), out_parts)
    small = scatter_late(ids, qkvo, (back_sums, first_sums, second_sums, up_sums), fs)
    terms = reduce_seq([flat(p) for p in parts])
    input_grad = attn_grad + (
        terms[0].astype(F32) + terms[1].astype(F32) + terms[2].astype(F32)
    )
    four, up, down, vecs = finish(ids, s, gather_seq(small), gather_seq(large), fs)
    return (
        deep(layer_out), deep(input_grad), *four, up, down,
        vecs[ROW_QB], vecs[ROW_VB], vecs[ROW_OB], vecs[ROW_UB], vecs[ROW_DB],
        vecs[ROW_G1], vecs[ROW_S1], vecs[ROW_G2], vecs[ROW_S2],
    )


def solution(mesh):
    count, fs = mesh.shape["seq"], mesh.shape["fsdp"]
    assert count == SEQ_N and fs % 4 == 0
    inner = Mesh(mesh.devices.reshape(2, 2, fs // 2, 2), SEQ + FSDP)
    rows, matrix, vector = P(FSDP, SEQ, None), P(FSDP, None), P(FSDP)
    in_specs = (rows,) * 2 + (matrix,) * 6 + (vector,) * 9
    return jax.shard_map(
        functools.partial(body, fs), mesh=inner, in_specs=in_specs, out_specs=in_specs, check_vma=False
    )
```

time: 1540 us -> 525 us (0.34)
  waiting for transfers between devices: 984 us -> 174 us
  Pallas kernels: 0 us -> 256 us
  blocking collectives: 168 us -> 0 us
  matrix products: 126 us -> 0 us
  other arithmetic: 77.6 us -> 11.5 us
  local copies, waits for them, and re-layouts: 72.2 us -> 10.8 us
  starting transfers between devices: 80.5 us -> 54.3 us
    reduce_scatter x6 -> x1, waiting for transfers between devices: 746 us -> 0.01 us  [body(): lax.psum_scatter(packed.reshape(-1, d), FSDP, scatter_dimension=0, tiled=...]
    pallas_call x0 -> x14, Pallas kernels: none -> 256 us  [call(): pl.pallas_call(kernel, out_shape=outs, in_specs=in_specs, out_specs=out_s...]
    all_gather x6 -> x1, waiting for transfers between devices: 201 us -> 0.01 us  [body(): weights = lax.all_gather(late, FSDP)]
    ppermute x0 -> x50, waiting for transfers between devices: none -> 174 us  [the longest x36 87.2 us: seq_swap(): return lax.ppermute(value, SEQ, [(i, i ^ k) for i in range(SEQ_N)])]
    all_gather x9 -> x0, blocking collectives: 131 us -> none  [the longest x1 21.4 us: body(): lax.all_gather(up_bias, 'fsdp', axis=0, tiled=True)]
    dot_general x48 -> x0, matrix products: 126 us -> none  [the longest x12 36.2 us: matmul(): return jnp.dot(left_side, right_side, preferred_element_type=jnp.float32)]
    all_to_all x16 -> x0, starting transfers between devices: 79.9 us -> none  [the longest x2 17.9 us: forward(): lax.all_to_all(mixture, 'seq', split_axis=1, concat_axis=2, tiled=True)]
    ppermute x0 -> x50, starting transfers between devices: none -> 54.2 us  [the longest x36 34.6 us: seq_swap(): return lax.ppermute(value, SEQ, [(i, i ^ k) for i in range(SEQ_N)])]
  transfers between devices with their start and end apart: 29 -> 52, of which waited for: 16 -> 23; matrix products, arithmetic and copies ran while one was open for 14% -> 2% of each run, Pallas kernels for 0% -> 35%
where the time goes in v1:
time: 525 us; the launch traced here: 521 us
  Pallas kernels  256 us (49%)
  waiting for transfers between devices  174 us (33%)
  starting transfers between devices  54.3 us (10%)
  between operations  14.6 us (3%)
  other arithmetic  11.5 us (2%)
  local copies, waits for them, and re-layouts  10.8 us (2%)
    pallas_call x14, Pallas kernels, call(): pl.pallas_call(kernel, out_shape=outs, in_specs=in_specs, out_specs=out_s...  256 us
    ppermute x36, waiting for transfers between devices, seq_swap(): return lax.ppermute(value, SEQ, [(i, i ^ k) for i in range(SEQ_N)])  87.2 us
    ppermute x14, waiting for transfers between devices, fsdp_swap(): return lax.ppermute(value, FSDP, [(i, i ^ k) for i in range(count)])  86.8 us
    ppermute x36, starting transfers between devices, seq_swap(): return lax.ppermute(value, SEQ, [(i, i ^ k) for i in range(SEQ_N)])  34.6 us
    ppermute x14, starting transfers between devices, fsdp_swap(): return lax.ppermute(value, FSDP, [(i, i ^ k) for i in range(count)])  19.6 us
  transfers between devices with their start and end apart: 52, of which 23 were waited for; matrix products, arithmetic and copies ran while one was open for 2% of the time, Pallas kernels for 35%

profile of v1, /device:TPU:13, one launch (start us, length us, event | category | flops | bytes accessed | tf_op | source)
XLA Modules:
  0.0 521.3 jit_solution(2491372996598106781)
XLA Ops:
  8.0 17.9 %late_pack.1 = bf16[256,1024]{1,0:T(8,128)(2,1)} custom-call(s32[2]{0:T(128)} %pad_add_fusion.ids, bf16[128,4096]{1,0:T(8,128)(2,1)} %up.1, bf16[512,1024]{1,0:T(8,128)(2,1)} %down.1), custom_call_target="tpu_custom_call" | custom-call | bytes 2621448 | tf_op jit(solution)/shard_map/late_pack/pallas_call | solution.py:54
  26.6 9.9 %early_pack.1.refs_0_ = bf16[144,1024]{1,0:T(8,128)(2,1)} custom-call(s32[2]{0:T(128)} %pad_add_fusion.ids, bf16[128,1024]{1,0:T(8,128)(2,1)} %wq.1, bf16[128,1024]{1,0:T(8,128)(2,1)} %wk.1, bf16[128,1024]{1,0:T(8,128)(2,1)} %wv.1, bf16[128,1024]{1,0:T(8,128)(2,1)} %wo.1, bf16[16,128]{1,0:T(8,128)(2,1)} %pad.4.vec), custom_call_target="tpu_custom_call" | custom-call | bytes 1347592 | tf_op jit(solution)/shard_map/early_pack/pallas_call | solution.py:54
  41.5 30.5 %collective-permute-done.8.refs_6_ = bf16[144,1024]{1,0:T(8,128)(2,1)S(1)} collective-permute-done((bf16[144,1024]{1,0:T(8,128)(2,1)}, bf16[144,1024]{1,0:T(8,128)(2,1)S(1)}, u32[]{:S(2)}, u32[]{:S(2)}) %collective-permute-start.8) | collective-permute-done | bytes 294944 | tf_op jit(solution)/shard_map/ppermute | solution.py:91
  72.3 6.2 %collective-permute-done.6.refs_4_ = bf16[144,1024]{1,0:T(8,128)(2,1)S(1)} collective-permute-done((bf16[144,1024]{1,0:T(8,128)(2,1)}, bf16[144,1024]{1,0:T(8,128)(2,1)S(1)}, u32[]{:S(2)}, u32[]{:S(2)}) %collective-permute-start.6) | collective-permute-done | bytes 294944 | tf_op jit(solution)/shard_map/ppermute | solution.py:91
  78.6 1.4 collective-permute-start.5
  80.0 11.0 %collective-permute-done.7.refs_5_ = bf16[144,1024]{1,0:T(8,128)(2,1)S(1)} collective-permute-done((bf16[144,1024]{1,0:T(8,128)(2,1)S(1)}, bf16[144,1024]{1,0:T(8,128)(2,1)S(1)}, u32[]{:S(2)}, u32[]{:S(2)}) %collective-permute-start.7) | collective-permute-done | bytes 294944 | tf_op jit(solution)/shard_map/ppermute | solution.py:91
  91.1 12.6 %collective-permute-done.5.refs_3_ = bf16[144,1024]{1,0:T(8,128)(2,1)S(1)} collective-permute-done((bf16[144,1024]{1,0:T(8,128)(2,1)S(1)}, bf16[144,1024]{1,0:T(8,128)(2,1)S(1)}, u32[]{:S(2)}, u32[]{:S(2)}) %collective-permute-start.5) | collective-permute-done | bytes 294944 | tf_op jit(solution)/shard_map/ppermute | solution.py:91
  104.5 66.1 %assemble.1 = (bf16[1024,768]{1,0:T(8,128)(2,1)}, bf16[1024,256]{1,0:T(8,128)(2,1)}, f32[16,1024]{1,0:T(8,128)}) custom-call(s32[2]{0:T(128)} %pad_add_fusion.ids, bf16[144,1024]{1,0:T(8,128)(2,1)} %early_pack.1.refs_0_, bf16[144,1024]{1,0:T(8,128)(2,1)} %copy-done.25, bf16[144,1024]{1,0:T(8,128)(2,1)} %copy-done.24, bf16[144,1024]{1,0:T(8,128)(2,1)} %copy-done.28, ...), custom_call_target="tpu_custom_call" | custom-call | bytes 4521992 | tf_op jit(solution)/shard_map/assemble/pallas_call | solution.py:54
  171.9 3.5 collective-permute-start
  175.9 5.2 collective-permute-done.14.w2
  181.1 4.1 collective-permute-start.15
  186.2 9.5 %attend.1 = (bf16[2,512,768]{2,1,0:T(8,128)(2,1)}, f32[2,4,512]{2,1,0:T(4,128)}, bf16[2,128,256]{2,1,0:T(8,128)(2,1)}, bf16[2,128,256]{2,1,0:T(8,128)(2,1)}, bf1...) custom-call(s32[2]{0:T(128)} %pad_add_fusion.ids, bf16[2,128,1024]{2,1,0:T(8,128)(2,1)} %x0.3, ...), custom_call_target="tpu_custom_call" | custom-call | flops 2147483648 | bytes 5849096 | tf_op jit(solution)/shard_map/attend/pallas_call | solution.py:54
  197.9 2.8 collective-permute-done.11.m2
  200.7 3.4 collective-permute-done.12.m3
  204.9 4.5 out_project.1
  210.7 12.6 %collective-permute-done.17.f2 = bf16[256,1024]{1,0:T(8,128)(2,1)S(1)} collective-permute-done((bf16[256,1024]{1,0:T(8,128)(2,1)}, bf16[256,1024]{1,0:T(8,128)(2,1)S(1)}, u32[]{:S(2)}, u32[]{:S(2)}) %collective-permute-start.17) | collective-permute-done | bytes 524320 | tf_op jit(solution)/shard_map/ppermute | solution.py:70
  224.0 1.5 collective-permute-done.18.f3
  226.3 18.5 %ffn.1 = (bf16[256,1024]{1,0:T(8,128)(2,1)}, bf16[256,1024]{1,0:T(8,128)(2,1)}, bf16[256,1024]{1,0:T(8,128)(2,1)}, bf16[256,1024]{1,0:T(8,128)(2,1)}, bf16[1024,1024]{1,0:T(8,128)(2,1)}, /*index=5*/f32[1024,1024]{1,0:T(8,128)}) custom-call(s32[2]{0:T(128)} %pad_add_fusion.ids, bf16[256,1024]{1,0:T(8,128)(2,1)} %get-tuple-element.93.f0, ...), custom_call_target="tpu_custom_call" | custom-call | flops 4294967296 | bytes 14745608 | tf_op jit(solution)/shard_map/ffn/pallas_call | solution.py:54
  245.3 1.6 collective-permute-done.20
  249.4 11.9 %collective-permute-done.21.p2 = bf16[256,1024]{1,0:T(8,128)(2,1)S(1)} collective-permute-done((bf16[256,1024]{1,0:T(8,128)(2,1)S(1)}, bf16[256,1024]{1,0:T(8,128)(2,1)S(1)}, u32[]{:S(2)}, u32[]{:S(2)}) %collective-permute-start.21) | collective-permute-done | bytes 524320 | tf_op jit(solution)/shard_map/ppermute | solution.py:70
  262.2 4.1 second_norm.1
  267.5 1.5 collective-permute-start.22
  269.0 9.7 %collective-permute-done.23.d2 = bf16[256,1024]{1,0:T(8,128)(2,1)S(1)} collective-permute-done((bf16[256,1024]{1,0:T(8,128)(2,1)}, bf16[256,1024]{1,0:T(8,128)(2,1)S(1)}, u32[]{:S(2)}, u32[]{:S(2)}) %collective-permute-start.23) | collective-permute-done | bytes 524320 | tf_op jit(solution)/shard_map/ppermute | solution.py:70
  278.7 2.1 collective-permute-start.24
  280.8 1.5 collective-permute-done.24.d3
  283.2 17.8 %ffn_back.1 = (bf16[256,1024]{1,0:T(8,128)(2,1)}, bf16[256,1024]{1,0:T(8,128)(2,1)}, bf16[256,1024]{1,0:T(8,128)(2,1)}, bf16[256,1024]{1,0:T(8,128)(2,1)}, bf16[...) custom-call(bf16[256,1024]{1,0:T(8,128)(2,1)} %get-tuple-element.100.d0, bf16[256,1024]{1,0:T(8,128)(2,1)} %copy-done.52, ...), custom_call_target="tpu_custom_call" | custom-call | flops 4294967296 | bytes 14712832 | tf_op jit(solution)/shard_map/ffn_back/pallas_call | solution.py:54
  301.0 9.4 %ffn_grads.1 = bf16[8,256,1024]{2,1,0:T(8,128)(2,1)} custom-call(bf16[256,1024]{1,0:T(8,128)(2,1)} %get-tuple-element.93.f0, bf16[256,1024]{1,0:T(8,128)(2,1)} %copy-done.47, bf16[256,1024]{1,0:T(8,128)(2,1)} %copy-done.45, bf16[256,1024]{1,0:T(8,128)(2,1)} %copy-done.48, bf16[1024,1024]{1,0:T(8,128)(2,1)} %get-tuple-element.136.up_low, ...), custom_call_target="tpu_custom_call" | custom-call | flops 4294967296 | bytes 12582912 | tf_op jit(solution)/shard_map/ffn_grads/pallas_call | solution.py:54
  314.9 12.0 %collective-permute-done.27.p2 = bf16[256,1024]{1,0:T(8,128)(2,1)S(1)} collective-permute-done((bf16[256,1024]{1,0:T(8,128)(2,1)S(1)}, bf16[256,1024]{1,0:T(8,128)(2,1)S(1)}, u32[]{:S(2)}, u32[]{:S(2)}) %collective-permute-start.27) | collective-permute-done | bytes 524320 | tf_op jit(solution)/shard_map/ppermute | solution.py:70
  327.7 6.5 %first_norm.1 = (f32[256,1024]{1,0:T(8,128)}, f32[8,1024]{1,0:T(8,128)}, bf16[256,256]{1,0:T(8,128)(2,1)}, bf16[256,256]{1,0:T(8,128)(2,1)}, bf16[256,256]{1,0:T...) custom-call(s32[2]{0:T(128)} %pad_add_fusion.ids, ...), custom_call_target="tpu_custom_call" | custom-call | flops 1073741824 | bytes 10059784 | tf_op jit(solution)/shard_map/first_norm/pallas_call | solution.py:54
  335.4 1.7 collective-permute-done.35
  341.8 12.6 %collective-permute-done.29 = bf16[256,256]{1,0:T(8,128)(2,1)S(1)} collective-permute-done((bf16[256,256]{1,0:T(8,128)(2,1)}, bf16[256,256]{1,0:T(8,128)(2,1)S(1)}, u32[]{:S(2)}, u32[]{:S(2)}) %collective-permute-start.29) | collective-permute-done | bytes 131104 | tf_op jit(solution)/shard_map/ppermute | solution.py:70
  354.4 3.6 collective-permute-done.30
  358.6 14.9 %attend_back.1 = (bf16[2,512,768]{2,1,0:T(8,128)(2,1)}, f32[8,768]{1,0:T(8,128)}, bf16[2,128,1024]{2,1,0:T(8,128)(2,1)}, bf16[2,128,1024]{2,1,0:T(8,128)(2,1)}, ...) custom-call(bf16[2,512,768]{2,1,0:T(8,128)(2,1)} %get-tuple-element.109.qkv, ...), custom_call_target="tpu_custom_call" | custom-call | flops 2952790016 | bytes 7380992 | tf_op jit(solution)/shard_map/attend_back/pallas_call | solution.py:54
  374.5 6.2 %qkvo_grads.1.grads = bf16[1024,1024]{1,0:T(8,128)(2,1)} custom-call(bf16[2,128,1024]{2,1,0:T(8,128)(2,1)} %x0.3, bf16[2,128,1024]{2,1,0:T(8,128)(2,1)} %copy-done.7, bf16[2,128,1024]{2,1,0:T(8,128)(2,1)} %copy-done.6, bf16[2,128,1024]{2,1,0:T(8,128)(2,1)} %copy-done.8, bf16[1024,768]{1,0:T(8,128)(2,1)} %bitcast.36, ...), custom_call_target="tpu_custom_call" | custom-call | flops 1610612736 | bytes 7340032 | tf_op jit(solution)/shard_map/qkvo_grads/pallas_call | solution.py:54
  380.7 65.7 %split.1 = (bf16[144,1024]{1,0:T(8,128)(2,1)}, bf16[144,1024]{1,0:T(8,128)(2,1)}, bf16[144,1024]{1,0:T(8,128)(2,1)}, bf16[144,1024]{1,0:T(8,128)(2,1)}, bf16[144...) custom-call(s32[2]{0:T(128)} %pad_add_fusion.ids, ...), custom_call_target="tpu_custom_call" | custom-call | bytes 4579336 | tf_op jit(solution)/shard_map/split/pallas_call | solution.py:54
  446.5 1.5 collective-permute-start.39
  448.1 1.5 collective-permute-start.43
  449.6 6.1 %collective-permute-done.37 = bf16[144,1024]{1,0:T(8,128)(2,1)S(1)} collective-permute-done((bf16[144,1024]{1,0:T(8,128)(2,1)}, bf16[144,1024]{1,0:T(8,128)(2,1)S(1)}, u32[]{:S(2)}, u32[]{:S(2)}) %collective-permute-start.37) | collective-permute-done | bytes 294944 | tf_op jit(solution)/shard_map/ppermute | solution.py:91
  455.7 1.8 add_convert_fusion.6
  457.5 5.0 collective-permute-start.38
  462.5 1.8 add_convert_fusion.5
  464.3 4.3 collective-permute-start.40
  468.6 1.9 add_convert_fusion.4
  470.4 1.8 collective-permute-start.42
  476.3 11.9 %collective-permute-done.40 = bf16[144,1024]{1,0:T(8,128)(2,1)} collective-permute-done((bf16[144,1024]{1,0:T(8,128)(2,1)}, bf16[144,1024]{1,0:T(8,128)(2,1)}, u32[]{:S(2)}, u32[]{:S(2)}) %collective-permute-start.40) | collective-permute-done | bytes 294944 | tf_op jit(solution)/shard_map/ppermute | solution.py:91
  488.2 7.1 %collective-permute-done.42 = bf16[144,1024]{1,0:T(8,128)(2,1)} collective-permute-done((bf16[144,1024]{1,0:T(8,128)(2,1)}, bf16[144,1024]{1,0:T(8,128)(2,1)}, u32[]{:S(2)}, u32[]{:S(2)}) %collective-permute-start.42) | collective-permute-done | bytes 294944 | tf_op jit(solution)/shard_map/ppermute | solution.py:91
  499.2 5.6 %collective-permute-done.45.c2 = bf16[144,1024]{1,0:T(8,128)(2,1)S(1)} collective-permute-done((bf16[144,1024]{1,0:T(8,128)(2,1)S(1)}, bf16[144,1024]{1,0:T(8,128)(2,1)S(1)}, u32[]{:S(2)}, u32[]{:S(2)}) %collective-permute-start.45) | collective-permute-done | bytes 294944 | tf_op jit(solution)/shard_map/ppermute | solution.py:70
  509.3 5.1 finish.1
  (198 shorter events, 47.1 us)
Async XLA Ops:
  7.3 218.2 %all-gather.3.cloned.1.call-start = ((), (), s32[]{:S(2)}) async-start(), calls=%async_computation.2 | async-start | bytes 4718592 | tf_op jit(solution)/shard_map/all_gather | solution.py:832
  25.8 446.4 %reduce-scatter.2.cloned.1.call-start = ((), (), s32[]{:S(2)}) async-start(), calls=%async_computation.1 | async-start | bytes 4718592 | tf_op jit(solution)/shard_map/reduce_scatter | solution.py:848
  36.5 35.5 %collective-permute-start.8 = (bf16[144,1024]{1,0:T(8,128)(2,1)}, bf16[144,1024]{1,0:T(8,128)(2,1)S(1)}, u32[]{:S(2)}, u32[]{:S(2)}) collective-permute-start(bf16[144,1024]{1,0:T(8,128)(2,1)} %early_pack.1.refs_0_), channel_id=1, source_target_pairs={{0,6},{1,7},{2,4},{3,5},{4,2},{5,3},{6,0},{7,1},{8,14},{9,15},{10,... | collective-permute-start | bytes 884744 | tf_op jit(solution)/shard_map/ppermute | solution.py:91
  37.9 40.6 %collective-permute-start.6 = (bf16[144,1024]{1,0:T(8,128)(2,1)}, bf16[144,1024]{1,0:T(8,128)(2,1)S(1)}, u32[]{:S(2)}, u32[]{:S(2)}) collective-permute-start(bf16[144,1024]{1,0:T(8,128)(2,1)} %early_pack.1.refs_0_), channel_id=1, source_target_pairs={{0,4},{1,5},{2,6},{3,7},{4,0},{5,1},{6,2},{7,3},{8,12},{9,13},{10,... | collective-permute-start | bytes 884744 | tf_op jit(solution)/shard_map/ppermute | solution.py:91
  39.0 39.6 %collective-permute-start.4 = (bf16[144,1024]{1,0:T(8,128)(2,1)}, bf16[144,1024]{1,0:T(8,128)(2,1)S(1)}, u32[]{:S(2)}, u32[]{:S(2)}) collective-permute-start(bf16[144,1024]{1,0:T(8,128)(2,1)} %early_pack.1.refs_0_), channel_id=1, source_target_pairs={{0,2},{1,3},{2,0},{3,1},{4,6},{5,7},{6,4},{7,5},{8,10},{9,11},{10,... | collective-permute-start | bytes 884744 | tf_op jit(solution)/shard_map/ppermute | solution.py:91
  40.1 135.3 %collective-permute-start.1 = (bf16[2,128,1024]{2,1,0:T(8,128)(2,1)S(1)}, bf16[2,128,1024]{2,1,0:T(8,128)(2,1)S(1)}, u32[]{:S(2)}, u32[]{:S(2)}) collective-permute-start(bf16[2,128,1024]{2,1,0:T(8,128)(2,1)S(1)} %copy-done), channel_id=1, source_target_pairs={{0,16},{8,24},{16,0},{24,8},{1,17},{9,25},{17,1},{25,9},{2,18},{10... | collective-permute-start | bytes 1572872 | tf_op jit(solution)/shard_map/ppermute | solution.py:70
  41.3 38.7 %collective-permute-start.3 = (bf16[144,1024]{1,0:T(8,128)(2,1)}, bf16[144,1024]{1,0:T(8,128)(2,1)S(1)}, u32[]{:S(2)}, u32[]{:S(2)}) collective-permute-start(bf16[144,1024]{1,0:T(8,128)(2,1)} %early_pack.1.refs_0_), channel_id=1, source_target_pairs={{0,1},{1,0},{2,3},{3,2},{4,5},{5,4},{6,7},{7,6},{8,9},{9,8},{10,11... | collective-permute-start | bytes 884744 | tf_op jit(solution)/shard_map/ppermute | solution.py:91
  72.0 8.0 %collective-permute-start.9 = (bf16[144,1024]{1,0:T(8,128)(2,1)S(1)}, bf16[144,1024]{1,0:T(8,128)(2,1)S(1)}, u32[]{:S(2)}, u32[]{:S(2)}) collective-permute-start(bf16[144,1024]{1,0:T(8,128)(2,1)S(1)} %collective-permute-done.8.refs_6_), channel_id=1, source_target_pairs={{0,1},{1,0},{2,3},{3,2},{4,5},{5,4},{6,7},{7,6},{8,9},{9,8},{10,11... | collective-permute-start | bytes 884744 | tf_op jit(solution)/shard_map/ppermute | solution.py:91
  78.5 12.5 %collective-permute-start.7 = (bf16[144,1024]{1,0:T(8,128)(2,1)S(1)}, bf16[144,1024]{1,0:T(8,128)(2,1)S(1)}, u32[]{:S(2)}, u32[]{:S(2)}) collective-permute-start(bf16[144,1024]{1,0:T(8,128)(2,1)S(1)} %collective-permute-done.6.refs_4_), channel_id=1, source_target_pairs={{0,1},{1,0},{2,3},{3,2},{4,5},{5,4},{6,7},{7,6},{8,9},{9,8},{10,11... | collective-permute-start | bytes 884744 | tf_op jit(solution)/shard_map/ppermute | solution.py:91
  78.6 25.1 %collective-permute-start.5 = (bf16[144,1024]{1,0:T(8,128)(2,1)S(1)}, bf16[144,1024]{1,0:T(8,128)(2,1)S(1)}, u32[]{:S(2)}, u32[]{:S(2)}) collective-permute-start(bf16[144,1024]{1,0:T(8,128)(2,1)S(1)} %collective-permute-done.4.refs_2_), channel_id=1, source_target_pairs={{0,1},{1,0},{2,3},{3,2},{4,5},{5,4},{6,7},{7,6},{8,9},{9,8},{10,11... | collective-permute-start | bytes 884744 | tf_op jit(solution)/shard_map/ppermute | solution.py:91
  170.6 10.5 %collective-permute-start.14 = (bf16[1024,256]{1,0:T(8,128)(2,1)}, bf16[1024,256]{1,0:T(8,128)(2,1)S(1)}, u32[]{:S(2)}, u32[]{:S(2)}) collective-permute-start(bf16[1024,256]{1,0:T(8,128)(2,1)} %get-tuple-element.91.w0), channel_id=1, source_target_pairs={{0,16},{8,24},{16,0},{24,8},{1,17},{9,25},{17,1},{25,9},{2,18},{10... | collective-permute-start | bytes 1572872 | tf_op jit(solution)/shard_map/ppermute | solution.py:70
  171.9 13.3 %collective-permute-start = (bf16[2,128,1024]{2,1,0:T(8,128)(2,1)S(1)}, bf16[2,128,1024]{2,1,0:T(8,128)(2,1)S(1)}, u32[]{:S(2)}, u32[]{:S(2)}) collective-permute-start(bf16[2,128,1024]{2,1,0:T(8,128)(2,1)S(1)} %copy-done), channel_id=1, source_target_pairs={{0,8},{8,0},{16,24},{24,16},{1,9},{9,1},{17,25},{25,17},{2,10},{10... | collective-permute-start | bytes 1572872 | tf_op jit(solution)/shard_map/ppermute | solution.py:70
  175.4 9.9 %collective-permute-start.2 = (bf16[2,128,1024]{2,1,0:T(8,128)(2,1)S(1)}, bf16[2,128,1024]{2,1,0:T(8,128)(2,1)S(1)}, u32[]{:S(2)}, u32[]{:S(2)}) collective-permute-start(bf16[2,128,1024]{2,1,0:T(8,128)(2,1)S(1)} %collective-permute-done.1.x2), channel_id=1, source_target_pairs={{0,8},{8,0},{16,24},{24,16},{1,9},{9,1},{17,25},{25,17},{2,10},{10... | collective-permute-start | bytes 1572872 | tf_op jit(solution)/shard_map/ppermute | solution.py:70
  175.4 22.4 %collective-permute-start.13 = (bf16[1024,256]{1,0:T(8,128)(2,1)}, bf16[1024,256]{1,0:T(8,128)(2,1)S(1)}, u32[]{:S(2)}, u32[]{:S(2)}) collective-permute-start(bf16[1024,256]{1,0:T(8,128)(2,1)} %get-tuple-element.91.w0), channel_id=1, source_target_pairs={{0,8},{8,0},{16,24},{24,16},{1,9},{9,1},{17,25},{25,17},{2,10},{10... | collective-permute-start | bytes 1572872 | tf_op jit(solution)/shard_map/ppermute | solution.py:70
  181.1 23.0 %collective-permute-start.15 = (bf16[1024,256]{1,0:T(8,128)(2,1)S(1)}, bf16[1024,256]{1,0:T(8,128)(2,1)S(1)}, u32[]{:S(2)}, u32[]{:S(2)}) collective-permute-start(bf16[1024,256]{1,0:T(8,128)(2,1)S(1)} %collective-permute-done.14.w2), channel_id=1, source_target_pairs={{0,8},{8,0},{16,24},{24,16},{1,9},{9,1},{17,25},{25,17},{2,10},{10... | collective-permute-start | bytes 1572872 | tf_op jit(solution)/shard_map/ppermute | solution.py:70
  195.8 4.9 collective-permute-start.11
  197.0 7.0 %collective-permute-start.12 = (bf16[256,256]{1,0:T(8,128)(2,1)}, bf16[256,256]{1,0:T(8,128)(2,1)S(1)}, u32[]{:S(2)}, u32[]{:S(2)}) collective-permute-start(bf16[256,256]{1,0:T(8,128)(2,1)} %bitcast.57), channel_id=1, source_target_pairs={{0,24},{8,16},{16,8},{24,0},{1,25},{9,17},{17,9},{25,1},{2,26},{10... | collective-permute-start | bytes 393224 | tf_op jit(solution)/shard_map/ppermute | solution.py:70
  209.4 13.9 %collective-permute-start.17 = (bf16[256,1024]{1,0:T(8,128)(2,1)}, bf16[256,1024]{1,0:T(8,128)(2,1)S(1)}, u32[]{:S(2)}, u32[]{:S(2)}) collective-permute-start(bf16[256,1024]{1,0:T(8,128)(2,1)} %get-tuple-element.93.f0), channel_id=1, source_target_pairs={{0,16},{8,24},{16,0},{24,8},{1,17},{9,25},{17,1},{25,9},{2,18},{10... | collective-permute-start | bytes 1572872 | tf_op jit(solution)/shard_map/ppermute | solution.py:70
  210.6 13.3 %collective-permute-start.16 = (bf16[256,1024]{1,0:T(8,128)(2,1)}, bf16[256,1024]{1,0:T(8,128)(2,1)S(1)}, u32[]{:S(2)}, u32[]{:S(2)}) collective-permute-start(bf16[256,1024]{1,0:T(8,128)(2,1)} %get-tuple-element.93.f0), channel_id=1, source_target_pairs={{0,8},{8,0},{16,24},{24,16},{1,9},{9,1},{17,25},{25,17},{2,10},{10... | collective-permute-start | bytes 1572872 | tf_op jit(solution)/shard_map/ppermute | solution.py:70
  245.2 4.3 collective-permute-start.19
  248.2 13.2 %collective-permute-start.21 = (bf16[256,1024]{1,0:T(8,128)(2,1)S(1)}, bf16[256,1024]{1,0:T(8,128)(2,1)S(1)}, u32[]{:S(2)}, u32[]{:S(2)}) collective-permute-start(bf16[256,1024]{1,0:T(8,128)(2,1)S(1)} %add_convert_fusion.2), channel_id=1, source_target_pairs={{0,16},{8,24},{16,0},{24,8},{1,17},{9,25},{17,1},{25,9},{2,18},{10... | collective-permute-start | bytes 1572872 | tf_op jit(solution)/shard_map/ppermute | solution.py:70
  266.3 12.4 %collective-permute-start.23 = (bf16[256,1024]{1,0:T(8,128)(2,1)}, bf16[256,1024]{1,0:T(8,128)(2,1)S(1)}, u32[]{:S(2)}, u32[]{:S(2)}) collective-permute-start(bf16[256,1024]{1,0:T(8,128)(2,1)} %get-tuple-element.100.d0), channel_id=1, source_target_pairs={{0,16},{8,24},{16,0},{24,8},{1,17},{9,25},{17,1},{25,9},{2,18},{10... | collective-permute-start | bytes 1572872 | tf_op jit(solution)/shard_map/ppermute | solution.py:70
  267.5 13.3 %collective-permute-start.22 = (bf16[256,1024]{1,0:T(8,128)(2,1)}, bf16[256,1024]{1,0:T(8,128)(2,1)S(1)}, u32[]{:S(2)}, u32[]{:S(2)}) collective-permute-start(bf16[256,1024]{1,0:T(8,128)(2,1)} %get-tuple-element.100.d0), channel_id=1, source_target_pairs={{0,8},{8,0},{16,24},{24,16},{1,9},{9,1},{17,25},{25,17},{2,10},{10... | collective-permute-start | bytes 1572872 | tf_op jit(solution)/shard_map/ppermute | solution.py:70
  278.7 3.7 collective-permute-start.24
  311.9 3.0 collective-permute-start.25
  313.6 13.3 %collective-permute-start.27 = (bf16[256,1024]{1,0:T(8,128)(2,1)S(1)}, bf16[256,1024]{1,0:T(8,128)(2,1)S(1)}, u32[]{:S(2)}, u32[]{:S(2)}) collective-permute-start(bf16[256,1024]{1,0:T(8,128)(2,1)S(1)} %add_convert_fusion.1), channel_id=1, source_target_pairs={{0,16},{8,24},{16,0},{24,8},{1,17},{9,25},{17,1},{25,9},{2,18},{10... | collective-permute-start | bytes 1572872 | tf_op jit(solution)/shard_map/ppermute | solution.py:70
  334.2 2.8 collective-permute-start.35
  335.3 38.2 %collective-permute-start.34 = (bf16[1024,256]{1,0:T(8,128)(2,1)}, bf16[1024,256]{1,0:T(8,128)(2,1)S(1)}, u32[]{:S(2)}, u32[]{:S(2)}) collective-permute-start(bf16[1024,256]{1,0:T(8,128)(2,1)} %get-tuple-element.121), channel_id=1, source_target_pairs={{0,8},{8,0},{16,24},{24,16},{1,9},{9,1},{17,25},{25,17},{2,10},{10... | collective-permute-start | bytes 1572872 | tf_op jit(solution)/shard_map/ppermute | solution.py:70
  338.2 35.3 %collective-permute-start.36 = (bf16[1024,256]{1,0:T(8,128)(2,1)S(1)}, bf16[1024,256]{1,0:T(8,128)(2,1)S(1)}, u32[]{:S(2)}, u32[]{:S(2)}) collective-permute-start(bf16[1024,256]{1,0:T(8,128)(2,1)S(1)} %add_convert_fusion), channel_id=1, source_target_pairs={{0,16},{8,24},{16,0},{24,8},{1,17},{9,25},{17,1},{25,9},{2,18},{10... | collective-permute-start | bytes 1572872 | tf_op jit(solution)/shard_map/ppermute | solution.py:70
  339.5 2.3 collective-permute-start.28
  340.1 14.2 %collective-permute-start.29 = (bf16[256,256]{1,0:T(8,128)(2,1)}, bf16[256,256]{1,0:T(8,128)(2,1)S(1)}, u32[]{:S(2)}, u32[]{:S(2)}) collective-permute-start(bf16[256,256]{1,0:T(8,128)(2,1)} %get-tuple-element.113), channel_id=1, source_target_pairs={{0,16},{8,24},{16,0},{24,8},{1,17},{9,25},{17,1},{25,9},{2,18},{10... | collective-permute-start | bytes 393224 | tf_op jit(solution)/shard_map/ppermute | solution.py:70
  340.4 17.6 %collective-permute-start.30 = (bf16[256,256]{1,0:T(8,128)(2,1)}, bf16[256,256]{1,0:T(8,128)(2,1)S(1)}, u32[]{:S(2)}, u32[]{:S(2)}) collective-permute-start(bf16[256,256]{1,0:T(8,128)(2,1)} %get-tuple-element.114), channel_id=1, source_target_pairs={{0,24},{8,16},{16,8},{24,0},{1,25},{9,17},{17,9},{25,1},{2,26},{10... | collective-permute-start | bytes 393224 | tf_op jit(solution)/shard_map/ppermute | solution.py:70
  446.4 9.3 %collective-permute-start.37 = (bf16[144,1024]{1,0:T(8,128)(2,1)}, bf16[144,1024]{1,0:T(8,128)(2,1)S(1)}, u32[]{:S(2)}, u32[]{:S(2)}) collective-permute-start(bf16[144,1024]{1,0:T(8,128)(2,1)} %get-tuple-element.129), channel_id=1, source_target_pairs={{0,1},{1,0},{2,3},{3,2},{4,5},{5,4},{6,7},{7,6},{8,9},{9,8},{10,11... | collective-permute-start | bytes 884744 | tf_op jit(solution)/shard_map/ppermute | solution.py:91
  446.5 16.0 %collective-permute-start.39 = (bf16[144,1024]{1,0:T(8,128)(2,1)}, bf16[144,1024]{1,0:T(8,128)(2,1)S(1)}, u32[]{:S(2)}, u32[]{:S(2)}) collective-permute-start(bf16[144,1024]{1,0:T(8,128)(2,1)} %get-tuple-element.131), channel_id=1, source_target_pairs={{0,1},{1,0},{2,3},{3,2},{4,5},{5,4},{6,7},{7,6},{8,9},{9,8},{10,11... | collective-permute-start | bytes 884744 | tf_op jit(solution)/shard_map/ppermute | solution.py:91
  448.0 24.3 %collective-permute-start.32 = (bf16[256,1024]{1,0:T(8,128)(2,1)S(1)}, bf16[256,1024]{1,0:T(8,128)(2,1)S(1)}, u32[]{:S(2)}, u32[]{:S(2)}) collective-permute-start(bf16[256,1024]{1,0:T(8,128)(2,1)S(1)} %bitcast.53), channel_id=1, source_target_pairs={{0,8},{8,0},{16,24},{24,16},{1,9},{9,1},{17,25},{25,17},{2,10},{10... | collective-permute-start | bytes 1572872 | tf_op jit(solution)/shard_map/ppermute | solution.py:70
  448.1 20.5 %collective-permute-start.41 = (bf16[144,1024]{1,0:T(8,128)(2,1)}, bf16[144,1024]{1,0:T(8,128)(2,1)S(1)}, u32[]{:S(2)}, u32[]{:S(2)}) collective-permute-start(bf16[144,1024]{1,0:T(8,128)(2,1)} %get-tuple-element.133), channel_id=1, source_target_pairs={{0,1},{1,0},{2,3},{3,2},{4,5},{5,4},{6,7},{7,6},{8,9},{9,8},{10,11... | collective-permute-start | bytes 884744 | tf_op jit(solution)/shard_map/ppermute | solution.py:91
  448.1 26.7 %collective-permute-start.43 = (bf16[144,1024]{1,0:T(8,128)(2,1)}, bf16[144,1024]{1,0:T(8,128)(2,1)S(1)}, u32[]{:S(2)}, u32[]{:S(2)}) collective-permute-start(bf16[144,1024]{1,0:T(8,128)(2,1)} %get-tuple-element.135), channel_id=1, source_target_pairs={{0,1},{1,0},{2,3},{3,2},{4,5},{5,4},{6,7},{7,6},{8,9},{9,8},{10,11... | collective-permute-start | bytes 884744 | tf_op jit(solution)/shard_map/ppermute | solution.py:91
  457.5 18.1 %collective-permute-start.38 = (bf16[144,1024]{1,0:T(8,128)(2,1)}, bf16[144,1024]{1,0:T(8,128)(2,1)S(1)}, u32[]{:S(2)}, u32[]{:S(2)}) collective-permute-start(bf16[144,1024]{1,0:T(8,128)(2,1)} %add_convert_fusion.6), channel_id=1, source_target_pairs={{0,2},{1,3},{2,0},{3,1},{4,6},{5,7},{6,4},{7,5},{8,10},{9,11},{10,... | collective-permute-start | bytes 884744 | tf_op jit(solution)/shard_map/ppermute | solution.py:91
  464.3 24.0 %collective-permute-start.40 = (bf16[144,1024]{1,0:T(8,128)(2,1)}, bf16[144,1024]{1,0:T(8,128)(2,1)}, u32[]{:S(2)}, u32[]{:S(2)}) collective-permute-start(bf16[144,1024]{1,0:T(8,128)(2,1)} %add_convert_fusion.5), channel_id=1, source_target_pairs={{0,4},{1,5},{2,6},{3,7},{4,0},{5,1},{6,2},{7,3},{8,12},{9,13},{10,... | collective-permute-start | bytes 884744 | tf_op jit(solution)/shard_map/ppermute | solution.py:91
  470.4 24.9 %collective-permute-start.42 = (bf16[144,1024]{1,0:T(8,128)(2,1)}, bf16[144,1024]{1,0:T(8,128)(2,1)}, u32[]{:S(2)}, u32[]{:S(2)}) collective-permute-start(bf16[144,1024]{1,0:T(8,128)(2,1)} %add_convert_fusion.4), channel_id=1, source_target_pairs={{0,6},{1,7},{2,4},{3,5},{4,2},{5,3},{6,0},{7,1},{8,14},{9,15},{10,... | collective-permute-start | bytes 884744 | tf_op jit(solution)/shard_map/ppermute | solution.py:91
  472.2 26.5 %collective-permute-start.48 = (bf16[256,1024]{1,0:T(8,128)(2,1)}, bf16[256,1024]{1,0:T(8,128)(2,1)S(1)}, u32[]{:S(2)}, u32[]{:S(2)}) collective-permute-start(bf16[256,1024]{1,0:T(8,128)(2,1)} %reduce-scatter.2.cloned.1.call-done.e0), channel_id=1, source_target_pairs={{0,16},{8,24},{16,0},{24,8},{1,17},{9,25},{17,1},{25,9},{2,18},{10... | collective-permute-start | bytes 1572872 | tf_op jit(solution)/shard_map/ppermute | solution.py:70
  474.8 24.0 %collective-permute-start.31 = (bf16[256,1024]{1,0:T(8,128)(2,1)}, bf16[256,1024]{1,0:T(8,128)(2,1)S(1)}, u32[]{:S(2)}, u32[]{:S(2)}) collective-permute-start(bf16[256,1024]{1,0:T(8,128)(2,1)} %bitcast.52), channel_id=1, source_target_pairs={{0,8},{8,0},{16,24},{24,16},{1,9},{9,1},{17,25},{25,17},{2,10},{10... | collective-permute-start | bytes 1572872 | tf_op jit(solution)/shard_map/ppermute | solution.py:70
  475.6 30.6 %collective-permute-start.33 = (bf16[256,1024]{1,0:T(8,128)(2,1)S(1)}, bf16[256,1024]{1,0:T(8,128)(2,1)S(1)}, u32[]{:S(2)}, u32[]{:S(2)}) collective-permute-start(bf16[256,1024]{1,0:T(8,128)(2,1)S(1)} %fusion), channel_id=1, source_target_pairs={{0,16},{8,24},{16,0},{24,8},{1,17},{9,25},{17,1},{25,9},{2,18},{10... | collective-permute-start | bytes 1572872 | tf_op jit(solution)/shard_map/ppermute | solution.py:70
  496.7 8.2 %collective-permute-start.45 = (bf16[144,1024]{1,0:T(8,128)(2,1)S(1)}, bf16[144,1024]{1,0:T(8,128)(2,1)S(1)}, u32[]{:S(2)}, u32[]{:S(2)}) collective-permute-start(bf16[144,1024]{1,0:T(8,128)(2,1)S(1)} %add_convert_fusion.3.c0), channel_id=1, source_target_pairs={{0,16},{8,24},{16,0},{24,8},{1,17},{9,25},{17,1},{25,9},{2,18},{10... | collective-permute-start | bytes 884744 | tf_op jit(solution)/shard_map/ppermute | solution.py:70
  497.9 9.5 %collective-permute-start.47 = (bf16[256,1024]{1,0:T(8,128)(2,1)S(1)}, bf16[256,1024]{1,0:T(8,128)(2,1)S(1)}, u32[]{:S(2)}, u32[]{:S(2)}) collective-permute-start(bf16[256,1024]{1,0:T(8,128)(2,1)S(1)} %copy-done.18), channel_id=1, source_target_pairs={{0,8},{8,0},{16,24},{24,16},{1,9},{9,1},{17,25},{25,17},{2,10},{10... | collective-permute-start | bytes 1572872 | tf_op jit(solution)/shard_map/ppermute | solution.py:70
  498.7 8.8 %collective-permute-start.49 = (bf16[256,1024]{1,0:T(8,128)(2,1)S(1)}, bf16[256,1024]{1,0:T(8,128)(2,1)S(1)}, u32[]{:S(2)}, u32[]{:S(2)}) collective-permute-start(bf16[256,1024]{1,0:T(8,128)(2,1)S(1)} %collective-permute-done.48.e2), channel_id=1, source_target_pairs={{0,8},{8,0},{16,24},{24,16},{1,9},{9,1},{17,25},{25,17},{2,10},{10... | collective-permute-start | bytes 1572872 | tf_op jit(solution)/shard_map/ppermute | solution.py:70
  498.8 8.7 %collective-permute-start.44 = (bf16[144,1024]{1,0:T(8,128)(2,1)S(1)}, bf16[144,1024]{1,0:T(8,128)(2,1)S(1)}, u32[]{:S(2)}, u32[]{:S(2)}) collective-permute-start(bf16[144,1024]{1,0:T(8,128)(2,1)S(1)} %add_convert_fusion.3.c0), channel_id=1, source_target_pairs={{0,8},{8,0},{16,24},{24,16},{1,9},{9,1},{17,25},{25,17},{2,10},{10... | collective-permute-start | bytes 884744 | tf_op jit(solution)/shard_map/ppermute | solution.py:70
  504.8 2.7 collective-permute-start.46
  (61 other events, 785.2 us)
Sparse Core Ops, SparseCore 0:
  26.0 104.9 all-gather.2
  310.6 91.8 reduce-scatter.1

commit v2 on v1

v2 whole, which is shorter than its diff:
```python
import functools
import math

import jax
import jax.numpy as jnp
from jax import lax
from jax.experimental import pallas as pl
from jax.experimental.pallas import tpu as pltpu
from jax.sharding import Mesh, PartitionSpec as P

HD = 64
EPSILON = 1e-05
F32 = jnp.float32
BF16 = jnp.bfloat16
SEQ = ("x", "c")
FSDP = ("z", "y")
SEQ_N = 4
VEC = 16
ROW_QB, ROW_VB, ROW_OB, ROW_DB, ROW_G1, ROW_S1, ROW_G2, ROW_S2, ROW_UB = range(9)
VMEM = pltpu.VMEM
ANY = pl.ANY


def dot(a, b):
    return lax.dot_general(a, b, (((1,), (0,)), ((), ())), preferred_element_type=F32)


def dot_nt(a, b):
    return lax.dot_general(a, b, (((1,), (1,)), ((), ())), preferred_element_type=F32)


def dot_tn(a, b):
    return lax.dot_general(a, b, (((0,), (0,)), ((), ())), preferred_element_type=F32)


def struct(shape, dtype):
    return jax.ShapeDtypeStruct(shape, dtype)


def nbytes(tree):
    return sum(math.prod(a.shape) * a.dtype.itemsize for a in jax.tree.leaves(tree))


def whole(space=VMEM):
    return pl.BlockSpec(memory_space=space)


def call(kernel, outs, args, *, name, grid=None, in_specs=None, out_specs=None, scratch=(), flops=0, trans=0):
    if in_specs is None:
        in_specs = [whole() for _ in args]
    if out_specs is None:
        out_specs = jax.tree.map(lambda _: whole(), outs)
    kwargs = {} if grid is None else {"grid": grid}
    return pl.pallas_call(
        kernel,
        out_shape=outs,
        in_specs=in_specs,
        out_specs=out_specs,
        scratch_shapes=list(scratch),
        compiler_params=pltpu.CompilerParams(vmem_limit_bytes=56 << 20),
        cost_estimate=pl.CostEstimate(
            flops=flops, bytes_accessed=nbytes(args) + nbytes(outs), transcendentals=trans
        ),
        name=name,
        **kwargs,
    )(*args)


def seq_swap(value, k):
    with jax.named_scope(f"seq{k}"):
        return lax.ppermute(value, SEQ, [(i, i ^ k) for i in range(SEQ_N)])


def gather_seq(value, *others):
    far = seq_swap(value, 2)
    near = seq_swap(value, 1)
    return [value, near, far, seq_swap(after(far, *others), 1)]


def reduce_seq(parts):
    near0 = seq_swap(parts[1], 1)
    near2 = seq_swap(parts[3], 1)
    onward = (parts[2].astype(F32) + near2.astype(F32)).astype(BF16)
    return [parts[0], near0, seq_swap(onward, 2)], onward


def exchange_seq(parts):
    return [parts[0]] + [seq_swap(parts[r], r) for r in (1, 2, 3)]


def swap_y(value):
    with jax.named_scope("y"):
        return lax.ppermute(value, "y", [(0, 1), (1, 0)])


def swap_z(value, k, count):
    with jax.named_scope(f"z{k}"):
        return lax.ppermute(value, "z", [(i, i ^ k) for i in range(count)])


def turn_z(value):
    with jax.named_scope("z"):
        return lax.all_to_all(value, "z", split_axis=0, concat_axis=0, tiled=True)


def after(value, *others):
    return lax.optimization_barrier((value, *others))[0] if others else value


def fits(n):
    return n % 128 == 0


def run_copies(copies):
    for copy in copies:
        copy.start()
    for copy in copies:
        copy.wait()


def early_pack_kernel(ids, wq, wk, wv, wo, *refs):
    *vectors, up_bias, out, sems = refs
    s = ids[0]
    n = wq.shape[0]
    c = wq.shape[1] // SEQ_N
    cols = pl.ds(pl.multiple_of(s * c, c), c)
    copies = [
        pltpu.make_async_copy(w.at[:, cols], out.at[pl.ds(0, n), pl.ds(i * c, c)], sems.at[i])
        for i, w in enumerate((wq, wk, wv, wo))
    ]
    for copy in copies:
        copy.start()
    rows = [v[...].astype(F32).reshape(1, n) for v in vectors]
    rows += [up_bias[j * n : (j + 1) * n].astype(F32).reshape(1, n) for j in range(SEQ_N)]
    rows.append(jnp.zeros((VEC - len(rows), n), F32))
    out[n:, 0:n] = jnp.concatenate(rows, 0).astype(BF16)
    out[n:, n:] = jnp.zeros((VEC, out.shape[1] - n), BF16)
    for copy in copies:
        copy.wait()


def late_pack_kernel(fs, ids, up, down, out, sems):
    s = ids[0]
    n = up.shape[0]
    w = up.shape[1] // fs // SEQ_N
    copies = []
    for j in range(fs):
        cols = pl.ds(pl.multiple_of((j * SEQ_N + s) * w, w), w)
        copies.append(
            pltpu.make_async_copy(
                up.at[:, cols], out.at[pl.ds(0, n), pl.ds(j * w, w)], sems.at[j]
            )
        )
    rows = pl.ds(pl.multiple_of(s * w, w), w)
    copies.append(pltpu.make_async_copy(down.at[rows, :], out.at[pl.ds(n, w), :], sems.at[fs]))
    run_copies(copies)


def pack_early(ids, s, wq, wk, wv, wo, vectors, up_bias):
    n, d = wq.shape
    c = d // SEQ_N
    if fits(n):
        return call(
            early_pack_kernel,
            struct((n + VEC, d), BF16),
            (ids, wq, wk, wv, wo, *vectors, up_bias),
            name="early_pack",
            in_specs=[whole(pltpu.SMEM)] + [whole(ANY)] * 4 + [whole()] * (len(vectors) + 1),
            scratch=[pltpu.SemaphoreType.DMA((4,))],
        )
    rows = jnp.concatenate(vectors + [up_bias]).reshape(-1, n)
    vec = jnp.pad(rows, ((0, VEC - rows.shape[0]), (0, d - n)))
    four = [lax.dynamic_slice(m, (0, s * c), (n, c)) for m in (wq, wk, wv, wo)]
    return jnp.concatenate([jnp.concatenate(four, 1), vec], 0)


def pack_late(ids, s, fs, up, down):
    n, d = up.shape[0], down.shape[1]
    w = up.shape[1] // fs // SEQ_N
    if fits(n):
        return call(
            functools.partial(late_pack_kernel, fs),
            struct((n + w, d), BF16),
            (ids, up, down),
            name="late_pack",
            in_specs=[whole(pltpu.SMEM)] + [whole(ANY)] * 2,
            scratch=[pltpu.SemaphoreType.DMA((fs + 1,))],
        )
    mine = lax.dynamic_index_in_dim(up.reshape(n, fs, SEQ_N, w), s, 2, keepdims=False)
    return jnp.concatenate([mine.reshape(n, fs * w), lax.dynamic_slice(down, (s * w, 0), (w, d))], 0)


def gather_early(value, fs, *others):
    zs = fs // 2
    if zs != 4:
        own = turn_z(jnp.broadcast_to(value, (zs,) + value.shape))
        return [own, swap_y(own)]
    own = [value] + [swap_z(value, k, zs) for k in (3, 2, 1)][::-1]
    first = swap_y(value)
    return own + [first] + [swap_y(after(own[k], *others)) for k in (1, 2, 3)]


def load_blocks(pieces, f, first, rows, target, sems):
    zs = target.shape[0] // 2
    y = f & 1
    rows = pl.ds(first, rows)
    cols = pl.ds(0, target.shape[2])
    if len(pieces) == 2:
        return [
            pltpu.make_async_copy(piece.at[j, rows, cols], target.at[2 * j + at], sems.at[i * zs + j])
            for i, (piece, at) in enumerate(zip(pieces, (y, 1 - y)))
            for j in range(zs)
        ]
    return [
        pltpu.make_async_copy(
            piece.at[rows, cols], target.at[f ^ (2 * (i % zs) + i // zs)], sems.at[i]
        )
        for i, piece in enumerate(pieces)
    ]


def attend_kernel(count, ids, x0, x1, x2, x3, *refs):
    pieces = refs[:count]
    qkv, lse, m0, m1, m2, m3, w_out, vec, held, mix, w, small, sems, small_sems = refs[count:]
    fs = w.shape[0]
    n = w.shape[1]
    c = w.shape[2] // 3
    d = fs * n
    heads = c // HD
    block = x0.shape[1]
    f = ids[1]
    out_copy = pltpu.make_async_copy(w, w_out, sems.at[fs])

    @pl.when(pl.program_id(0) == 0)
    def _():
        copies = load_blocks(pieces, f, 0, n, w, sems)
        copies += load_blocks(pieces, f, n, VEC, small, small_sems)
        run_copies(copies)
        for j in range(fs):
            vec[:, j * n : (j + 1) * n] = small[j, :, 0:n].astype(F32)
        out_copy.start()

    for r, x in enumerate((x0, x1, x2, x3)):
        held[r * block : (r + 1) * block, :] = x[0]
    cols = pl.ds(pl.multiple_of(ids[0] * c, c), c)
    for part in range(3):
        acc = dot(held[...], w[:, :, part * c : (part + 1) * c].reshape(d, c))
        if part != 1:
            row = ROW_QB if part == 0 else ROW_VB
            acc = acc + vec[row : row + 1, cols]
        qkv[0, :, part * c : (part + 1) * c] = acc.astype(BF16)
    scale = 1.0 / math.sqrt(HD)
    for h in range(heads):
        at = h * HD
        query = (qkv[0, :, at : at + HD].astype(F32) * scale).astype(BF16)
        key = qkv[0, :, c + at : c + at + HD]
        value = qkv[0, :, 2 * c + at : 2 * c + at + HD]
        scores = dot_nt(key, query)
        highest = jnp.max(scores, 0, keepdims=True)
        raised = jnp.exp(scores - highest)
        summed = jnp.sum(raised, 0, keepdims=True)
        lse[0, h : h + 1, :] = highest + jnp.log(summed)
        low = (raised * (1.0 / summed)).astype(BF16)
        mix[at : at + HD, :] = dot_tn(value, low)
    mixture = mix[...].T.astype(BF16)
    for r, m in enumerate((m0, m1, m2, m3)):
        m[0] = mixture[r * block : (r + 1) * block, :]

    @pl.when(pl.program_id(0) == pl.num_programs(0) - 1)
    def _():
        out_copy.wait()


def attend(ids, blocks, pieces, fs):
    nb, block, d = blocks[0].shape
    c = d // SEQ_N
    n = d // fs
    length = SEQ_N * block
    heads = c // HD
    one = lambda shape: pl.BlockSpec((1,) + shape, lambda b: (b,) + (0,) * len(shape))
    fixed = lambda shape: pl.BlockSpec(shape, lambda b: (0,) * len(shape))
    outs = (
        (struct((nb, length, 3 * c), BF16), struct((nb, heads, length), F32))
        + (struct((nb, block, c), BF16),) * SEQ_N
        + (struct((fs, n, 3 * c), BF16), struct((VEC, d), F32))
    )
    return call(
        functools.partial(attend_kernel, len(pieces)),
        outs,
        (ids, *blocks, *pieces),
        name="attend",
        grid=(nb,),
        in_specs=[whole(pltpu.SMEM)] + [one((block, d))] * SEQ_N + [whole(ANY)] * len(pieces),
        out_specs=(one((length, 3 * c)), one((heads, length)))
        + (one((block, c)),) * SEQ_N
        + (whole(ANY), fixed((VEC, d))),
        scratch=[
            VMEM((length, d), BF16),
            VMEM((c, length), F32),
            VMEM((fs, n, 3 * c), BF16),
            VMEM((fs, VEC, max(n, 128)), BF16),
            pltpu.SemaphoreType.DMA((fs + 1,)),
            pltpu.SemaphoreType.DMA((fs,)),
        ],
        flops=2 * nb * length * (3 * c * d + 2 * length * c),
        trans=nb * heads * length * length,
    )


def attend_back_kernel(qkv, lse, h0, h1, h2, h3, w, back, sums, r0, r1, r2, r3, held, turned):
    c = w.shape[1] // 3
    heads = c // HD
    block = h0.shape[1]
    for r, h in enumerate((h0, h1, h2, h3)):
        held[r * block : (r + 1) * block, :] = h[0]
    scale = 1.0 / math.sqrt(HD)
    for h in range(heads):
        at = h * HD
        query = (qkv[0, :, at : at + HD].astype(F32) * scale).astype(BF16)
        key = qkv[0, :, c + at : c + at + HD]
        value = qkv[0, :, 2 * c + at : 2 * c + at + HD]
        grad = held[:, at : at + HD]
        scores = dot_nt(key, query)
        attention = jnp.exp(scores - lse[0, h : h + 1, :])
        attention_grad = dot_nt(value, grad)
        inner = jnp.sum(attention * attention_grad, 0, keepdims=True)
        low = (attention * (attention_grad - inner)).astype(BF16)
        turned[at : at + HD, :] = dot_tn(key, low) * scale
        back[0, :, c + at : c + at + HD] = dot(low, query).astype(BF16)
        back[0, :, 2 * c + at : 2 * c + at + HD] = dot(attention.astype(BF16), grad).astype(BF16)
    back[0, :, 0:c] = turned[...].T.astype(BF16)
    whole_back = back[0]
    total = jnp.sum(whole_back.astype(F32), 0, keepdims=True)

    @pl.when(pl.program_id(0) == 0)
    def _():
        sums[...] = jnp.zeros_like(sums)

    sums[0:1, :] += total
    for r, out in enumerate((r0, r1, r2, r3)):
        out[0] = dot_nt(back[0, r * block : (r + 1) * block, :], w[...]).astype(BF16)


def attend_back(qkv, lse, grads, wqkv):
    nb, length, c3 = qkv.shape
    d = wqkv.shape[0]
    block = length // SEQ_N
    c = c3 // 3
    heads = c // HD
    one = lambda shape: pl.BlockSpec((1,) + shape, lambda b: (b,) + (0,) * len(shape))
    fixed = lambda shape: pl.BlockSpec(shape, lambda b: (0,) * len(shape))
    outs = (struct((nb, length, c3), BF16), struct((8, c3), F32)) + (
        struct((nb, block, d), BF16),
    ) * SEQ_N
    return call(
        attend_back_kernel,
        outs,
        (qkv, lse, *grads, wqkv),
        name="attend_back",
        grid=(nb,),
        in_specs=[one((length, c3)), one((heads, length))]
        + [one((block, c))] * SEQ_N
        + [fixed(wqkv.shape)],
        out_specs=(one((length, c3)), fixed((8, c3))) + (one((block, d)),) * SEQ_N,
        scratch=[VMEM((length, c), BF16), VMEM((c, length), F32)],
        flops=2 * nb * length * (c3 * d + 5 * length * c),
        trans=nb * heads * length * length,
    )


def row_norm(hidden):
    average = jnp.mean(hidden, -1, keepdims=True)
    centered = hidden - average
    spread = jnp.mean(centered * centered, -1, keepdims=True)
    scale = lax.rsqrt(spread + EPSILON)
    return centered * scale, scale


def norm_back(grad, normed, scale, gain):
    inner = grad * gain
    first = jnp.mean(inner, -1, keepdims=True)
    second = jnp.mean(inner * normed, -1, keepdims=True)
    return scale * (inner - first - normed * second)


def out_kernel(ids, m0, m1, m2, m3, w0, w1, w2, w3, tokens, vec,
               attn_sum, normed, low, mix, w, sems):
    s, f = ids[0], ids[1]
    c = m0.shape[1]
    fs, n, d = w.shape
    places = [pl.ds(pl.multiple_of((s ^ r) * c, c), c) for r in range(SEQ_N)]
    copies = []
    for r, (place, wr) in enumerate(zip(places, (w0, w1, w2, w3))):
        copies += load_blocks([wr.at[i] for i in range(wr.shape[0])], f, 0, n, w.at[:, :, place], sems.at[r])
    for copy in copies:
        copy.start()
    for place, m in zip(places, (m0, m1, m2, m3)):
        mix[:, place] = m[...]
    for copy in copies:
        copy.wait()
    for t in range(d // TILE):
        cols = slice(t * TILE, (t + 1) * TILE)
        product = dot(mix[...], w[:, :, cols].reshape(d, TILE))
        attn_sum[:, cols] = (
            tokens[:, cols].astype(F32) + product + vec[ROW_OB : ROW_OB + 1, cols]
        )
    unit, _ = row_norm(attn_sum[...])
    first = unit * vec[ROW_G1 : ROW_G1 + 1, :] + vec[ROW_S1 : ROW_S1 + 1, :]
    normed[...] = first
    low[...] = first.astype(BF16)


def out_project(ids, mixtures, wo, tokens, vec):
    rows, d = tokens.shape
    n = wo[0].shape[-2]
    fs = d // n
    outs = (
        struct((rows, d), F32),
        struct((rows, d), F32),
        struct((rows, d), BF16),
        struct((rows, d), BF16),
        struct((fs, n, d), BF16),
    )
    args = (ids, *mixtures, *wo, tokens, vec)
    return call(
        out_kernel,
        outs,
        args,
        name="out_project",
        in_specs=[whole(pltpu.SMEM)] + [whole()] * SEQ_N + [whole(ANY)] * SEQ_N + [whole()] * 2,
        scratch=[pltpu.SemaphoreType.DMA((SEQ_N, fs))],
        flops=2 * rows * d * d,
    )


def second_norm_kernel(normed, p0, p1, p2, cotangent, vec, layer_out, ffn_grad, low, sums):
    hidden = (
        normed[...]
        + (p0[...].astype(F32) + p1[...].astype(F32) + p2[...].astype(F32))
        + vec[ROW_DB : ROW_DB + 1, :]
    )
    unit, scale = row_norm(hidden)
    gain = vec[ROW_G2 : ROW_G2 + 1, :]
    layer_out[...] = (unit * gain + vec[ROW_S2 : ROW_S2 + 1, :]).astype(BF16)
    grad = cotangent[...].astype(F32)
    back = norm_back(grad, unit, scale, gain)
    ffn_grad[...] = back
    rounded = back.astype(BF16)
    low[...] = rounded
    sums[...] = jnp.zeros_like(sums)
    sums[0:1, :] = jnp.sum(grad * unit, 0, keepdims=True)
    sums[1:2, :] = jnp.sum(grad, 0, keepdims=True)
    sums[2:3, :] = jnp.sum(rounded.astype(F32), 0, keepdims=True)


def second_norm(normed, parts, cotangent, vec):
    rows, d = normed.shape
    outs = (
        struct((rows, d), BF16),
        struct((rows, d), F32),
        struct((rows, d), BF16),
        struct((8, d), F32),
    )
    return call(
        second_norm_kernel, outs, (normed, *parts, cotangent, vec), name="second_norm", flops=30 * rows * d
    )


def first_norm_kernel(ids, ffn_grad, p0, p1, p2, attn_sum, vec, mix, w,
                      attn_grad, sums, n0, n1, n2, n3, low_out, low, back):
    s = ids[0]
    c = n0.shape[1]
    d = ffn_grad.shape[1]
    grad = ffn_grad[...] + (p0[...].astype(F32) + p1[...].astype(F32) + p2[...].astype(F32))
    unit, scale = row_norm(attn_sum[...])
    gain = vec[ROW_G1 : ROW_G1 + 1, :]
    value = norm_back(grad, unit, scale, gain)
    attn_grad[...] = value
    rounded = value.astype(BF16)
    low[...] = rounded
    low_out[...] = rounded
    sums[...] = jnp.zeros_like(sums)
    sums[0:1, :] = jnp.sum(grad * unit, 0, keepdims=True)
    sums[1:2, :] = jnp.sum(grad, 0, keepdims=True)
    sums[2:3, :] = jnp.sum(rounded.astype(F32), 0, keepdims=True)
    back[...] = dot_nt(low[...], w[...].reshape(d, d)).astype(BF16)
    for r, n in enumerate((n0, n1, n2, n3)):
        n[...] = back[:, pl.ds(pl.multiple_of((s ^ r) * c, c), c)]


def first_norm(ids, ffn_grad, parts, attn_sum, vec, mix, wo):
    rows, d = ffn_grad.shape
    c = d // SEQ_N
    outs = (
        (struct((rows, d), F32), struct((8, d), F32))
        + (struct((rows, c), BF16),) * SEQ_N
        + (struct((rows, d), BF16),)
    )
    args = (ids, ffn_grad, *parts, attn_sum, vec, mix, wo)
    return call(
        first_norm_kernel,
        outs,
        args,
        name="first_norm",
        in_specs=[whole(pltpu.SMEM)] + [whole()] * (len(args) - 1),
        scratch=[VMEM((rows, d), BF16), VMEM((rows, d), BF16)],
        flops=2 * rows * d * d,
    )


def out_grads_kernel(ids, mix, low, d0, d1, d2, d3):
    s = ids[0]
    c = d0.shape[1]
    for r, out in enumerate((d0, d1, d2, d3)):
        place = pl.ds(pl.multiple_of((s ^ r) * c, c), c)
        out[...] = dot_tn(mix[...], low[:, place]).astype(BF16)


def out_grads(ids, mix, low):
    rows, d = mix.shape
    c = d // SEQ_N
    return call(
        out_grads_kernel,
        (struct((d, c), BF16),) * SEQ_N,
        (ids, mix, low),
        name="out_grads",
        in_specs=[whole(pltpu.SMEM)] + [whole()] * 2,
        flops=2 * rows * d * d,
    )


TILE = 256


def gelu_and_slope(u):
    phi = 0.5 * lax.erf(u * (1.0 / math.sqrt(2.0))) + 0.5
    bell = u * (jnp.exp(-0.5 * u * u) * (1.0 / math.sqrt(2.0 * math.pi)))
    return u * phi, phi + bell


def ffn_kernel(ids, f0, f1, f2, f3, vec, packed, p0, p1, p2, p3, gelu, slope,
               held, up, down, sems):
    n = up.shape[1]
    up_copies = [pltpu.make_async_copy(packed.at[:, pl.ds(0, n), :], up, sems.at[0])]
    down_copies = [pltpu.make_async_copy(packed.at[:, pl.ds(n, down.shape[1]), :], down, sems.at[1])]
    for copy in up_copies + down_copies:
        copy.start()
    rows, d = f0.shape
    hidden = gelu.shape[1]
    half = 2 * rows
    for i, f in enumerate((f1, f3, f0, f2)):
        held[i * rows : (i + 1) * rows, :] = f[...]
    bias = vec[pl.ds(ROW_UB + ids[0], 1), :]
    outs = (p1, p3, p0, p2)
    for copy in up_copies:
        copy.wait()
    for part in range(2):
        at = slice(part * half, (part + 1) * half)
        for t in range(hidden // TILE):
            cols = slice(t * TILE, (t + 1) * TILE)
            u = dot(held[at, :], up[:, :, cols].reshape(d, TILE)) + bias[:, cols]
            g, b = gelu_and_slope(u)
            gelu[at, cols] = g.astype(BF16)
            slope[at, cols] = b.astype(BF16)
        if part == 0:
            for copy in down_copies:
                copy.wait()
        for t in range(d // TILE):
            cols = slice(t * TILE, (t + 1) * TILE)
            y = dot(gelu[at, :], down[:, :, cols].reshape(hidden, TILE)).astype(BF16)
            outs[2 * part][:, cols] = y[0:rows]
            outs[2 * part + 1][:, cols] = y[rows:]


def weight_scratch(fs, d, hidden):
    return [
        VMEM((fs, d // fs, hidden), BF16),
        VMEM((fs, hidden // fs, d), BF16),
        pltpu.SemaphoreType.DMA((2,)),
    ]


def ffn(ids, blocks, packed, vec, hidden, fs):
    rows, d = blocks[0].shape
    total = SEQ_N * rows
    outs = (struct((rows, d), BF16),) * SEQ_N + (struct((total, hidden), BF16),) * 2
    return call(
        ffn_kernel,
        outs,
        (ids, *blocks, vec, packed),
        name="ffn",
        in_specs=[whole(pltpu.SMEM)] + [whole()] * (SEQ_N + 1) + [whole(ANY)],
        scratch=[VMEM((total, d), BF16)] + weight_scratch(fs, d, hidden),
        flops=4 * total * d * hidden,
        trans=2 * total * hidden,
    )


def ffn_back_kernel(ids, d0, d1, d2, d3, slope, packed, q0, q1, q2, q3, up_low, sums,
                    held, up, down, sems):
    n = up.shape[1]
    up_copies = [pltpu.make_async_copy(packed.at[:, pl.ds(0, n), :], up, sems.at[0])]
    down_copies = [pltpu.make_async_copy(packed.at[:, pl.ds(n, down.shape[1]), :], down, sems.at[1])]
    for copy in down_copies + up_copies:
        copy.start()
    rows, d = d0.shape
    hidden = up_low.shape[1]
    half = 2 * rows
    per = TILE // up.shape[1]
    for i, x in enumerate((d1, d3, d0, d2)):
        held[i * rows : (i + 1) * rows, :] = x[...]
    sums[...] = jnp.zeros_like(sums)
    outs = (q1, q3, q0, q2)
    for copy in down_copies:
        copy.wait()
    for part in range(2):
        at = slice(part * half, (part + 1) * half)
        for t in range(hidden // TILE):
            cols = slice(t * TILE, (t + 1) * TILE)
            rhs = down[t * per : (t + 1) * per].reshape(TILE, d)
            u = (dot_nt(held[at, :], rhs) * slope[at, cols].astype(F32)).astype(BF16)
            up_low[at, cols] = u
            sums[0:1, cols] += jnp.sum(u.astype(F32), 0, keepdims=True)
        if part == 0:
            for copy in up_copies:
                copy.wait()
        for t in range(d // TILE):
            cols = slice(t * TILE, (t + 1) * TILE)
            rhs = up[t * per : (t + 1) * per].reshape(TILE, hidden)
            y = dot_nt(up_low[at, :], rhs).astype(BF16)
            outs[2 * part][:, cols] = y[0:rows]
            outs[2 * part + 1][:, cols] = y[rows:]


def ffn_back(ids, blocks, packed, slope, fs):
    rows, d = blocks[0].shape
    total, hidden = slope.shape
    outs = (struct((rows, d), BF16),) * SEQ_N + (
        struct((total, hidden), BF16),
        struct((8, hidden), F32),
    )
    return call(
        ffn_back_kernel,
        outs,
        (ids, *blocks, slope, packed),
        name="ffn_back",
        in_specs=[whole(pltpu.SMEM)] + [whole()] * (SEQ_N + 1) + [whole(ANY)],
        scratch=[VMEM((total, d), BF16)] + weight_scratch(fs, d, hidden),
        flops=4 * total * d * hidden,
    )


def put_rows(f, tile, value, keep, send, turn):
    n = keep.shape[1]
    per = TILE // (2 * n)
    y = f & 1
    turn[...] = value
    for j in range(per):
        z = tile * per + j
        own = pl.multiple_of((2 * j + y) * n, n)
        other = pl.multiple_of((2 * j + 1 - y) * n, n)
        keep[z, 0:n, :] = turn[pl.ds(own, n), :]
        send[z, 0:n, :] = turn[pl.ds(other, n), :]


def outer_kernel(lefts, ids, *refs):
    left, right = refs[:lefts], refs[lefts:5]
    keep, send, held, turn = refs[5:]
    many = left if lefts > 1 else right
    rows = many[0].shape[0]
    for i, x in enumerate(many):
        held[i * rows : (i + 1) * rows, :] = x[...]
    a, b = (held, right[0]) if lefts > 1 else (left[0], held)
    for t in range(a.shape[1] // TILE):
        value = dot_tn(a[:, t * TILE : (t + 1) * TILE], b[...]).astype(BF16)
        put_rows(ids[1], t, value, keep, send, turn)


def outer(ids, lefts, rights, fs, name):
    rows = lefts[0].shape[0] if len(lefts) > 1 else rights[0].shape[0]
    d, e = lefts[0].shape[1], rights[0].shape[1]
    total = SEQ_N * rows
    return call(
        functools.partial(outer_kernel, len(lefts)),
        (struct((fs // 2, d // fs, e), BF16),) * 2,
        (ids, *lefts, *rights),
        name=name,
        in_specs=[whole(pltpu.SMEM)] + [whole()] * 5,
        scratch=[VMEM((total, d if len(lefts) > 1 else e), BF16), VMEM((TILE, e), BF16)],
        flops=2 * total * d * e,
    )


def add(a, b):
    return (a.astype(F32) + b.astype(F32)).astype(BF16)


def scatter_fsdp(keep, came, *others):
    if isinstance(keep, (list, tuple)):
        total = None
        for k in (1, 2, 3, 0):
            here = keep[k].astype(F32) + came[k].astype(F32)
            if k:
                here = swap_z(here.astype(BF16), k, len(keep)).astype(F32)
            total = here if total is None else total + here
        return total.astype(BF16)
    came = turn_z(after(add(keep, came), *others))
    return jnp.sum(came.astype(F32), 0).astype(BF16)


def fill_vectors(s, vec, back_sums, first_sums, second_sums, up_sums):
    c = vec.shape[1] // SEQ_N
    vec[...] = jnp.zeros_like(vec)
    cols = pl.ds(pl.multiple_of(s * c, c), c)
    vec[ROW_QB : ROW_QB + 1, cols] = back_sums[0:1, 0:c]
    vec[ROW_VB : ROW_VB + 1, cols] = back_sums[0:1, 2 * c : 3 * c]
    vec[ROW_OB : ROW_OB + 1, :] = first_sums[2:3, :]
    vec[ROW_DB : ROW_DB + 1, :] = second_sums[2:3, :]
    vec[ROW_G1 : ROW_G1 + 1, :] = first_sums[0:1, :]
    vec[ROW_S1 : ROW_S1 + 1, :] = first_sums[1:2, :]
    vec[ROW_G2 : ROW_G2 + 1, :] = second_sums[0:1, :]
    vec[ROW_S2 : ROW_S2 + 1, :] = second_sums[1:2, :]
    vec[pl.ds(ROW_UB + s, 1), :] = up_sums[0:1, :]


def qkvo_grads_kernel(ids, x0, x1, x2, x3, back, o0, o1, o2, s0, s1, s2, s3, *refs):
    outs, (held, vec, turn) = refs[:-3], refs[-3:]
    s, f = ids[0], ids[1]
    nb, block, d = x0.shape
    length = SEQ_N * block
    e = back.shape[1]
    n = outs[0].shape[-2] - VEC
    zs = d // (2 * n)
    per = TILE // (2 * n)
    y = f & 1
    for b in range(nb):
        for r, x in enumerate((x0, x1, x2, x3)):
            held[b * length + r * block : b * length + (r + 1) * block, :] = x[b]
    fill_vectors(s, vec, s0, s1, s2, s3)
    if len(outs) > 2:
        for k in (1, 2, 3, 0):
            z = (f >> 1) ^ k
            rows = pl.ds(pl.multiple_of(z * TILE, TILE), TILE)
            turn[:, 0:e] = dot_tn(held[:, rows], back[...]).astype(BF16)
            turn[:, e:] = (
                o0[rows, :].astype(F32) + o1[rows, :].astype(F32) + o2[rows, :].astype(F32)
            ).astype(BF16)
            for out, side in ((outs[k], y), (outs[zs + k], 1 - y)):
                out[0:n, :] = turn[pl.ds(pl.multiple_of(side * n, n), n), :]
                out[n:, :] = jnp.zeros((VEC, out.shape[1]), BF16)
                cols = pl.ds(pl.multiple_of((2 * z + side) * n, n), n)
                out[n:, 0:n] = vec[:, cols].astype(BF16)
        return
    keep, send = outs
    for t in range(d // TILE):
        rows = slice(t * TILE, (t + 1) * TILE)
        turn[:, 0:e] = dot_tn(held[:, rows], back[...]).astype(BF16)
        turn[:, e:] = (
            o0[rows, :].astype(F32) + o1[rows, :].astype(F32) + o2[rows, :].astype(F32)
        ).astype(BF16)
        for j in range(per):
            z = t * per + j
            for out, side in ((keep, y), (send, 1 - y)):
                out[z, 0:n, :] = turn[pl.ds(pl.multiple_of((2 * j + side) * n, n), n), :]
    low = vec[...].astype(BF16)
    for z in range(zs):
        first, second = (low[:, (2 * z + i) * n : (2 * z + i + 1) * n] for i in range(2))
        for out, pick in ((keep, y == 0), (send, y != 0)):
            out[z, n:, :] = jnp.zeros((VEC, out.shape[2]), BF16)
            out[z, n:, 0:n] = jnp.where(pick, first, second)


def qkvo_grads(ids, blocks, back, out_parts, sums, fs):
    nb, block, d = blocks[0].shape
    total, e = back.shape
    n = d // fs
    wide = e + out_parts[0].shape[1]
    if fs == 8 and fits(n):
        outs = (struct((n + VEC, wide), BF16),) * 8
    else:
        outs = (struct((fs // 2, n + VEC, wide), BF16),) * 2
    return call(
        qkvo_grads_kernel,
        outs,
        (ids, *blocks, back, *out_parts, *sums),
        name="qkvo_grads",
        in_specs=[whole(pltpu.SMEM)] + [whole()] * 12,
        scratch=[VMEM((total, d), BF16), VMEM((VEC, d), F32), VMEM((TILE, wide), BF16)],
        flops=2 * total * d * e,
    )


def finish_ffn_kernel(fs, ids, *refs):
    ups, downs, (up, down) = refs[:4], refs[4:8], refs[8:]
    s = ids[0]
    w = up.shape[1] // fs // SEQ_N
    for r in range(SEQ_N):
        at = s ^ r
        for j in range(fs):
            place = pl.ds(pl.multiple_of((j * SEQ_N + at) * w, w), w)
            up[:, place] = ups[r][:, j * w : (j + 1) * w].astype(F32)
        down[pl.ds(pl.multiple_of(at * w, w), w), :] = downs[r][...].astype(F32)


def finish_qkvo_kernel(ids, c0, c1, c2, c3, wq, wk, wv, wo, *vectors):
    s = ids[0]
    n = wq.shape[0]
    c = wq.shape[1] // SEQ_N
    total = 0.0
    for r, small in enumerate((c0, c1, c2, c3)):
        cols = pl.ds(pl.multiple_of((s ^ r) * c, c), c)
        for i, out in enumerate((wq, wk, wv, wo)):
            out[:, cols] = small[0:n, i * c : (i + 1) * c].astype(F32)
        total = total + small[n:, 0:n].astype(F32)
    for row, out in enumerate(vectors[:ROW_UB]):
        out[...] = total[row : row + 1, :].reshape(n)
    for j in range(SEQ_N):
        vectors[ROW_UB][j * n : (j + 1) * n] = total[ROW_UB + j : ROW_UB + j + 1, :].reshape(n)


def finish_ffn(ids, s, ups, downs, fs):
    n = ups[0].shape[0]
    w, d = downs[0].shape
    hidden = SEQ_N * fs * w
    if fits(n):
        return call(
            functools.partial(finish_ffn_kernel, fs),
            (struct((n, hidden), F32), struct((SEQ_N * w, d), F32)),
            (ids, *ups, *downs),
            name="finish_ffn",
            in_specs=[whole(pltpu.SMEM)] + [whole()] * 8,
        )
    order = jnp.arange(SEQ_N) ^ s
    up, down = (jnp.stack(v)[order].astype(F32) for v in (ups, downs))
    return (
        up.reshape(SEQ_N, n, fs, w).transpose(1, 2, 0, 3).reshape(n, hidden),
        down.reshape(SEQ_N * w, d),
    )


def finish_qkvo(ids, s, small):
    n = small[0].shape[0] - VEC
    d = small[0].shape[1]
    c = d // SEQ_N
    if fits(n):
        outs = (struct((n, d), F32),) * 4 + (struct((n,), F32),) * ROW_UB + (struct((SEQ_N * n,), F32),)
        done = call(
            finish_qkvo_kernel,
            outs,
            (ids, *small),
            name="finish_qkvo",
            in_specs=[whole(pltpu.SMEM)] + [whole()] * 4,
        )
        return done[:4], done[4:]
    small = jnp.stack(small)[jnp.arange(SEQ_N) ^ s].astype(F32)
    four = small[:, :n].reshape(SEQ_N, n, 4, c).transpose(2, 1, 0, 3).reshape(4, n, d)
    total = jnp.sum(small[:, n:, :n], 0)
    vectors = [total[row] for row in range(ROW_UB)]
    vectors.append(total[ROW_UB : ROW_UB + SEQ_N].reshape(SEQ_N * n))
    return [four[i] for i in range(4)], vectors


def body(fs, tokens_in, cotangent, query_weight, key_weight, value_weight, out_weight, up_weight,
         down_weight, query_bias, value_bias, out_bias, up_bias, down_bias, first_gain, first_shift,
         second_gain, second_shift):
    nb, block, d = tokens_in.shape
    rows = nb * block
    s = lax.axis_index(SEQ)
    f = lax.axis_index(FSDP)
    ids = jnp.stack([s, f]).astype(jnp.int32)
    flat = lambda a: a.reshape(rows, a.shape[-1])
    deep = lambda a: a.reshape(nb, block, a.shape[-1])

    scope = jax.named_scope
    early = pack_early(
        ids, s, query_weight, key_weight, value_weight, out_weight,
        [query_bias, value_bias, out_bias, down_bias, first_gain, first_shift, second_gain, second_shift],
        up_bias,
    )
    packed = pack_late(ids, s, fs, up_weight, down_weight)
    hidden = up_weight.shape[1] // SEQ_N
    with scope("tok"):
        tokens = gather_seq(tokens_in)
    with scope("wqkv"):
        wqkv = gather_early(early, fs, tokens[2])
    with scope("ffnw"):
        packed = lax.all_gather(after(packed, *wqkv[:5], tokens[2]), FSDP)
    with scope("wo"):
        n = d // fs
        wo = jnp.stack([p[..., :n, 3 * (d // SEQ_N) :] for p in wqkv])
        wo = [wo, seq_swap(wo, 1), seq_swap(wo, 2)]
    qkv, lse, *mixtures, wqkv, vec = attend(ids, tokens, wqkv, fs)
    with scope("wo"):
        wo.append(seq_swap(after(wo[2], vec), 1))
    with scope("mix"):
        mixtures = exchange_seq([flat(m) for m in mixtures])
    attn_sum, normed, first_low, mix, wo = out_project(ids, mixtures, wo, flat(tokens_in), vec)
    with scope("first"):
        firsts = gather_seq(first_low)
    *parts, gelu, slope = ffn(ids, firsts, packed, vec, hidden, fs)
    with scope("ffn"):
        parts, _ = reduce_seq(parts)
    layer_out, ffn_grad, down_low, second_sums = second_norm(normed, parts, flat(cotangent), vec)
    with scope("low"):
        lows = gather_seq(down_low)
    *parts, up_low, up_sums = ffn_back(ids, lows, packed, slope, fs)
    with scope("ffnback"):
        parts, onward = reduce_seq(parts)
        gelu = after(gelu, onward)
    turned = lambda blocks: (blocks[1], blocks[3], blocks[0], blocks[2])
    keep_down, send_down = outer(ids, (gelu,), turned(lows), fs, "down_grads")
    with scope("gdown"):
        came_down = swap_y(send_down)
    keep_up, send_up = outer(ids, turned(firsts), (up_low,), fs, "up_grads")
    parts[0] = after(parts[0], keep_down, keep_up)
    attn_grad, first_sums, *pieces, out_low = first_norm(ids, ffn_grad, parts, attn_sum, vec, mix, wo)
    with scope("mixback"):
        grads = exchange_seq(pieces)
    out_parts = out_grads(ids, mix, out_low)
    came_down = after(came_down, out_parts[0])
    with scope("gup"):
        came_up = swap_y(after(send_up, came_down))
    with scope("gdown"):
        down_grad = scatter_fsdp(keep_down, came_down)
    with scope("outs"):
        out_parts, onward = reduce_seq(out_parts)
    grads[0] = after(grads[0], onward)
    back, back_sums, *parts = attend_back(qkv, lse, [deep(g) for g in grads], wqkv.reshape(d, -1))
    came_up = after(came_up, back)
    with scope("gup"):
        up_grad = scatter_fsdp(keep_up, came_up)
    with scope("fdown"):
        down_full = gather_seq(down_grad)
    back = after(back, came_up, down_grad)
    pieces = qkvo_grads(
        ids, tokens, back.reshape(-1, back.shape[-1]), out_parts,
        (back_sums, first_sums, second_sums, up_sums), fs,
    )
    with scope("fup"):
        up_full = gather_seq(up_grad)
    up, down = finish_ffn(ids, s, up_full, down_full, fs)
    with scope("gqkvo"):
        half = len(pieces) // 2
        keep, send = pieces[:half], pieces[half:]
        if half == 1:
            small = scatter_fsdp(keep[0], swap_y(send[0]), up_grad)
        else:
            came = {k: swap_y(send[k]) for k in (1, 2, 3, 0)}
            small = scatter_fsdp(keep, came)
        small = gather_seq(after(small, up))
    with scope("input"):
        terms, _ = reduce_seq([flat(p) for p in parts])
    input_grad = attn_grad + (
        terms[0].astype(F32) + terms[1].astype(F32) + terms[2].astype(F32)
    )
    four, vecs = finish_qkvo(ids, s, small)
    return (
        deep(layer_out), deep(input_grad), *four, up, down,
        vecs[ROW_QB], vecs[ROW_VB], vecs[ROW_OB], vecs[ROW_UB], vecs[ROW_DB],
        vecs[ROW_G1], vecs[ROW_S1], vecs[ROW_G2], vecs[ROW_S2],
    )


def solution(mesh):
    count, fs = mesh.shape["seq"], mesh.shape["fsdp"]
    assert count == SEQ_N and fs % 4 == 0
    inner = Mesh(mesh.devices.reshape(2, 2, fs // 2, 2), SEQ + FSDP)
    rows, matrix, vector = P(FSDP, SEQ, None), P(FSDP, None), P(FSDP)
    in_specs = (rows,) * 2 + (matrix,) * 6 + (vector,) * 9
    return jax.shard_map(
        functools.partial(body, fs), mesh=inner, in_specs=in_specs, out_specs=in_specs, check_vma=False
    )
```

time: 525 us -> 342 us (0.65)
  Pallas kernels: 256 us -> 94.8 us
  waiting for transfers between devices: 174 us -> 139 us
  starting transfers between devices: 54.3 us -> 63.9 us
    pallas_call x14 -> x15, Pallas kernels: 256 us -> 94.8 us  [call(): pl.pallas_call(kernel, out_shape=outs, in_specs=in_specs, out_specs=out_s...]
    ppermute x36 -> x39, waiting for transfers between devices: 87.2 us -> 66.3 us  [seq_swap(): return lax.ppermute(value, SEQ, [(i, i ^ k) for i in range(SEQ_N)])]
    ppermute x14 -> x16, waiting for transfers between devices: 86.8 us -> 71.6 us  [the longest x10 38.6 us: swap_y(): return lax.ppermute(value, 'y', [(0, 1), (1, 0)])]
    all_to_all x0 -> x2, starting transfers between devices: none -> 9.23 us  [turn_z(): return lax.all_to_all(value, 'z', split_axis=0, concat_axis=0, tiled=True)]
    ppermute x36 -> x39, starting transfers between devices: 34.6 us -> 41.3 us  [seq_swap(): return lax.ppermute(value, SEQ, [(i, i ^ k) for i in range(SEQ_N)])]
    ppermute x14 -> x16, starting transfers between devices: 19.6 us -> 13.3 us  [the longest x10 7.18 us: swap_y(): return lax.ppermute(value, 'y', [(0, 1), (1, 0)])]
  transfers between devices with their start and end apart: 52 -> 58, of which waited for: 23 -> 26; matrix products, arithmetic and copies ran while one was open for 2% -> 4% of each run, Pallas kernels for 35% -> 18%
where the time goes in v2:
time: 342 us; the launch traced here: 337 us
  waiting for transfers between devices  139 us (41%)
  Pallas kernels  94.8 us (28%)
  starting transfers between devices  63.9 us (19%)
  between operations  15.1 us (4%)
  other arithmetic  14.5 us (4%)
  local copies, waits for them, and re-layouts  10.2 us (3%)
    pallas_call x15, Pallas kernels, call(): pl.pallas_call(kernel, out_shape=outs, in_specs=in_specs, out_specs=out_s...  94.8 us
    ppermute x39, waiting for transfers between devices, seq_swap(): return lax.ppermute(value, SEQ, [(i, i ^ k) for i in range(SEQ_N)])  66.3 us
    ppermute x39, starting transfers between devices, seq_swap(): return lax.ppermute(value, SEQ, [(i, i ^ k) for i in range(SEQ_N)])  41.3 us
    ppermute x10, waiting for transfers between devices, swap_y(): return lax.ppermute(value, 'y', [(0, 1), (1, 0)])  38.6 us
    ppermute x6, waiting for transfers between devices, swap_z(): return lax.ppermute(value, 'z', [(i, i ^ k) for i in range(count)])  33.1 us
    unnamed x119, local copies, waits for them, and re-layouts  10.2 us
    all_to_all x2, starting transfers between devices, turn_z(): return lax.all_to_all(value, 'z', split_axis=0, concat_axis=0, tiled=True)  9.23 us
    ppermute x10, starting transfers between devices, swap_y(): return lax.ppermute(value, 'y', [(0, 1), (1, 0)])  7.18 us
  transfers between devices with their start and end apart: 58, of which 26 were waited for; matrix products, arithmetic and copies ran while one was open for 4% of the time, Pallas kernels for 18%

profile of v2, /device:TPU:13, one launch (start us, length us, event | category | flops | bytes accessed | tf_op | source)
XLA Modules:
  0.0 337.1 jit_solution(14829239935276820362)
XLA Ops:
  9.1 2.6 early_pack.1.refs_0_
  15.5 2.6 late_pack.1
  19.5 13.3 %collective-permute-done.5.refs_3_ = bf16[144,1024]{1,0:T(8,128)(2,1)S(1)} collective-permute-done((bf16[144,1024]{1,0:T(8,128)(2,1)}, bf16[144,1024]{1,0:T(8,128)(2,1)S(1)}, u32[]{:S(2)}, u32[]{:S(2)}) %collective-permute-start.5) | collective-permute-done | bytes 294944 | tf_op jit(solution)/shard_map/wqkv/z3/ppermute | solution.py:98
  32.8 4.8 %collective-permute-done.4.refs_2_ = bf16[144,1024]{1,0:T(8,128)(2,1)S(1)} collective-permute-done((bf16[144,1024]{1,0:T(8,128)(2,1)}, bf16[144,1024]{1,0:T(8,128)(2,1)S(1)}, u32[]{:S(2)}, u32[]{:S(2)}) %collective-permute-start.4) | collective-permute-done | bytes 294944 | tf_op jit(solution)/shard_map/wqkv/z2/ppermute | solution.py:98
  37.7 2.2 collective-permute-start
  44.6 4.8 %collective-permute-done.7.refs_5_ = bf16[144,1024]{1,0:T(8,128)(2,1)S(1)} collective-permute-done((bf16[144,1024]{1,0:T(8,128)(2,1)S(1)}, bf16[144,1024]{1,0:T(8,128)(2,1)S(1)}, u32[]{:S(2)}, u32[]{:S(2)}) %collective-permute-start.7) | collective-permute-done | bytes 294944 | tf_op jit(solution)/shard_map/wqkv/y/ppermute | solution.py:93
  49.4 11.6 %collective-permute-done.8.refs_6_ = bf16[144,1024]{1,0:T(8,128)(2,1)S(1)} collective-permute-done((bf16[144,1024]{1,0:T(8,128)(2,1)S(1)}, bf16[144,1024]{1,0:T(8,128)(2,1)S(1)}, u32[]{:S(2)}, u32[]{:S(2)}) %collective-permute-start.8) | collective-permute-done | bytes 294944 | tf_op jit(solution)/shard_map/wqkv/y/ppermute | solution.py:93
  61.1 6.7 %collective-permute-done.9.refs_7_ = bf16[144,1024]{1,0:T(8,128)(2,1)S(1)} collective-permute-done((bf16[144,1024]{1,0:T(8,128)(2,1)S(1)}, bf16[144,1024]{1,0:T(8,128)(2,1)S(1)}, u32[]{:S(2)}, u32[]{:S(2)}) %collective-permute-start.9) | collective-permute-done | bytes 294944 | tf_op jit(solution)/shard_map/wqkv/y/ppermute | solution.py:93
  70.8 10.8 %attend.1 = (bf16[2,512,768]{2,1,0:T(8,128)(2,1)}, f32[2,4,512]{2,1,0:T(4,128)}, bf16[2,128,256]{2,1,0:T(8,128)(2,1)}, bf16[2,128,256]{2,1,0:T(8,128)(2,1)}, bf1...) custom-call(s32[2]{0:T(128)} %pad_add_fusion.ids, ...), custom_call_target="tpu_custom_call" | custom-call | flops 2147483648 | bytes 8208392 | tf_op jit(solution)/shard_map/attend/pallas_call | solution.py:54
  84.4 2.7 collective-permute-done.11.m2
  87.1 3.8 %collective-permute-done.12.m3 = bf16[256,256]{1,0:T(8,128)(2,1)S(1)} collective-permute-done((bf16[256,256]{1,0:T(8,128)(2,1)}, bf16[256,256]{1,0:T(8,128)(2,1)S(1)}, u32[]{:S(2)}, u32[]{:S(2)}) %collective-permute-start.12) | collective-permute-done | bytes 131104 | tf_op jit(solution)/shard_map/mix/seq3/ppermute | solution.py:71
  91.9 5.5 %out_project.1 = (f32[256,1024]{1,0:T(8,128)}, f32[256,1024]{1,0:T(8,128)}, bf16[256,1024]{1,0:T(8,128)(2,1)}, bf16[256,1024]{1,0:T(8,128)(2,1)}, bf16[8,128,1024]{2,1,0:T(8,128)(2,1)}) custom-call(s32[2]{0:T(128)} %pad_add_fusion.ids, bf16[256,256]{1,0:T(8,128)(2,1)} %bitcast.60, bf16[256,256]{1,0:T(8,128)(2,1)} %copy-done.27, bf16[256,256]{1,0:T(8,128)(2,1)} %copy-done.28, ...), custom_call_target="tpu_custom_call" | custom-call | flops 536870912 | bytes 8454152 | tf_op jit(solution)/shard_map/out_project/pallas_call | solution.py:54
  98.7 12.8 %collective-permute-done.17.f2.refs_3_ = bf16[256,1024]{1,0:T(8,128)(2,1)S(1)} collective-permute-done((bf16[256,1024]{1,0:T(8,128)(2,1)}, bf16[256,1024]{1,0:T(8,128)(2,1)S(1)}, u32[]{:S(2)}, u32[]{:S(2)}) %collective-permute-start.17) | collective-permute-done | bytes 524320 | tf_op jit(solution)/shard_map/first/seq2/ppermute | solution.py:71
  111.7 1.8 collective-permute-done.18.f3.refs_1_
  114.3 10.5 %ffn.1 = (bf16[256,1024]{1,0:T(8,128)(2,1)}, bf16[256,1024]{1,0:T(8,128)(2,1)}, bf16[256,1024]{1,0:T(8,128)(2,1)}, bf16[256,1024]{1,0:T(8,128)(2,1)}, bf16[1024,...) custom-call(s32[2]{0:T(128)} %pad_add_fusion.ids, bf16[256,1024]{1,0:T(8,128)(2,1)} %get-tuple-element.113.f0.refs_2_, ...), custom_call_target="tpu_custom_call" | custom-call | flops 4294967296 | bytes 12648456 | tf_op jit(solution)/shard_map/ffn/pallas_call | solution.py:54
  124.8 1.7 collective-permute-start.20
  130.7 11.9 %collective-permute-done.21.p2 = bf16[256,1024]{1,0:T(8,128)(2,1)S(1)} collective-permute-done((bf16[256,1024]{1,0:T(8,128)(2,1)S(1)}, bf16[256,1024]{1,0:T(8,128)(2,1)S(1)}, u32[]{:S(2)}, u32[]{:S(2)}) %collective-permute-start.21) | collective-permute-done | bytes 524320 | tf_op jit(solution)/shard_map/ffn/seq2/ppermute | solution.py:71
  143.5 4.1 %second_norm.1 = (bf16[256,1024]{1,0:T(8,128)(2,1)}, f32[256,1024]{1,0:T(8,128)}, bf16[256,1024]{1,0:T(8,128)(2,1)}, f32[8,1024]{1,0:T(8,128)}) custom-call(f32[256,1024]{1,0:T(8,128)} %get-tuple-element.112.normed, bf16[256,1024]{1,0:T(8,128)(2,1)} %get-tuple-element.115.p0, bf16[256,1024]{1,0:T(8,128)(2,1)} %copy-done.12, bf16[256,1024]{1,0:T(8,128)(2,1)} %copy-done.13, ...), custom_call_target="tpu_custom_call" | custom-call | flops 7864320 | bytes 5341184 | tf_op jit(solution)/shard_map/second_norm/pallas_call | solution.py:54
  150.3 9.8 %collective-permute-done.23.d2.refs_4_ = bf16[256,1024]{1,0:T(8,128)(2,1)S(1)} collective-permute-done((bf16[256,1024]{1,0:T(8,128)(2,1)}, bf16[256,1024]{1,0:T(8,128)(2,1)S(1)}, u32[]{:S(2)}, u32[]{:S(2)}) %collective-permute-start.23) | collective-permute-done | bytes 524320 | tf_op jit(solution)/shard_map/low/seq2/ppermute | solution.py:71
  160.0 2.1 collective-permute-start.24
  164.5 9.9 %ffn_back.1 = (bf16[256,1024]{1,0:T(8,128)(2,1)}, bf16[256,1024]{1,0:T(8,128)(2,1)}, bf16[256,1024]{1,0:T(8,128)(2,1)}, bf16[256,1024]{1,0:T(8,128)(2,1)}, bf16[...) custom-call(s32[2]{0:T(128)} %pad_add_fusion.ids, bf16[256,1024]{1,0:T(8,128)(2,1)} %get-tuple-element.121.d0.refs_3_, ...), custom_call_target="tpu_custom_call" | custom-call | flops 4294967296 | bytes 12615688 | tf_op jit(solution)/shard_map/ffn_back/pallas_call | solution.py:54
  174.8 1.7 collective-permute-done.25
  177.8 6.1 %down_grads.1 = (bf16[4,128,1024]{2,1,0:T(8,128)(2,1)}, bf16[4,128,1024]{2,1,0:T(8,128)(2,1)}) custom-call(s32[2]{0:T(128)} %pad_add_fusion.ids, bf16[1024,1024]{1,0:T(8,128)(2,1)} %get-tuple-element.127.refs_0_, bf16[256,1024]{1,0:T(8,128)(2,1)} %copy-done.47, bf16[256,1024]{1,0:T(8,128)(2,1)} %copy-done.49, ...), custom_call_target="tpu_custom_call" | custom-call | flops 2147483648 | bytes 6291464 | tf_op jit(solution)/shard_map/down_grads/pallas_call | solution.py:54
  187.0 6.2 %up_grads.1 = (bf16[4,128,1024]{2,1,0:T(8,128)(2,1)}, bf16[4,128,1024]{2,1,0:T(8,128)(2,1)}) custom-call(s32[2]{0:T(128)} %pad_add_fusion.ids, bf16[256,1024]{1,0:T(8,128)(2,1)} %copy-done.41, bf16[256,1024]{1,0:T(8,128)(2,1)} %copy-done.42, bf16[256,1024]{1,0:T(8,128)(2,1)} %get-tuple-element.113.f0.refs_2_, bf16[256,1024]{1,0:T(8,128)(2,1)} %copy-done.40, ...), custom_call_target="tpu_custom_call" | custom-call | flops 2147483648 | bytes 6291464 | tf_op jit(solution)/shard_map/up_grads/pallas_call | solution.py:54
  193.2 6.1 %collective-permute-done.27.p2 = bf16[256,1024]{1,0:T(8,128)(2,1)S(1)} collective-permute-done((bf16[256,1024]{1,0:T(8,128)(2,1)S(1)}, bf16[256,1024]{1,0:T(8,128)(2,1)S(1)}, u32[]{:S(2)}, u32[]{:S(2)}) %collective-permute-start.27) | collective-permute-done | bytes 524320 | tf_op jit(solution)/shard_map/ffnback/seq2/ppermute | solution.py:71
  200.1 5.4 %first_norm.1 = (f32[256,1024]{1,0:T(8,128)}, f32[8,1024]{1,0:T(8,128)}, bf16[256,256]{1,0:T(8,128)(2,1)}, bf16[256,256]{1,0:T(8,128)(2,1)}, bf16[256,256]{1,0:T...) custom-call(s32[2]{0:T(128)} %pad_add_fusion.ids, f32[256,1024]{1,0:T(8,128)} %get-tuple-element.120.ffn_grad, ...), custom_call_target="tpu_custom_call" | custom-call | flops 536870912 | bytes 8486920 | tf_op jit(solution)/shard_map/first_norm/pallas_call | solution.py:54
  205.6 3.1 out_grads.1
  210.1 4.7 %all-to-all-start = ((bf16[4,128,1024]{2,1,0:T(8,128)(2,1)}), bf16[4,128,1024]{2,1,0:T(8,128)(2,1)S(1)}, u32[]{:S(2)}, u32[]{:S(2)}) async-start(bf16[4,128,1024]{2,1,0:T(8,128)(2,1)} %add_convert_fusion.1), calls=%async_computation | async-start | bytes 2097152 | tf_op jit(solution)/shard_map/gdown/z/all_to_all | solution.py:103
  221.2 1.8 collective-permute-done.30
  223.0 4.0 %collective-permute-done.31 = bf16[256,256]{1,0:T(8,128)(2,1)S(1)} collective-permute-done((bf16[256,256]{1,0:T(8,128)(2,1)S(1)}, bf16[256,256]{1,0:T(8,128)(2,1)S(1)}, u32[]{:S(2)}, u32[]{:S(2)}) %collective-permute-start.31) | collective-permute-done | bytes 131104 | tf_op jit(solution)/shard_map/mixback/seq3/ppermute | solution.py:71
  227.6 14.9 %attend_back.1 = (bf16[2,512,768]{2,1,0:T(8,128)(2,1)}, f32[8,768]{1,0:T(8,128)}, bf16[2,128,1024]{2,1,0:T(8,128)(2,1)}, bf16[2,128,1024]{2,1,0:T(8,128)(2,1)}, ...) custom-call(bf16[2,512,768]{2,1,0:T(8,128)(2,1)} %get-tuple-element.137.qkv, ...), custom_call_target="tpu_custom_call" | custom-call | flops 2952790016 | bytes 7380992 | tf_op jit(solution)/shard_map/attend_back/pallas_call | solution.py:54
  244.0 4.5 %all-to-all-start.1 = ((bf16[4,128,1024]{2,1,0:T(8,128)(2,1)}), bf16[4,128,1024]{2,1,0:T(8,128)(2,1)S(1)}, u32[]{:S(2)}, u32[]{:S(2)}) async-start(bf16[4,128,1024]{2,1,0:T(8,128)(2,1)} %add_convert_fusion), calls=%async_computation.1 | async-start | bytes 2097152 | tf_op jit(solution)/shard_map/gup/z/all_to_all | solution.py:103
  248.7 6.3 %qkvo_grads.1 = (bf16[144,1024]{1,0:T(8,128)(2,1)}, bf16[144,1024]{1,0:T(8,128)(2,1)}, bf16[144,1024]{1,0:T(8,128)(2,1)}, bf16[144,1024]{1,0:T(8,128)(2,1)}, bf1...) custom-call(s32[2]{0:T(128)} %pad_add_fusion.ids, ...), custom_call_target="tpu_custom_call" | custom-call | flops 1610612736 | bytes 7725064 | tf_op jit(solution)/shard_map/qkvo_grads/pallas_call | solution.py:54
  258.7 5.0 %collective-permute-done.39 = bf16[144,1024]{1,0:T(8,128)(2,1)S(1)} collective-permute-done((bf16[144,1024]{1,0:T(8,128)(2,1)}, bf16[144,1024]{1,0:T(8,128)(2,1)S(1)}, u32[]{:S(2)}, u32[]{:S(2)}) %collective-permute-start.39) | collective-permute-done | bytes 294944 | tf_op jit(solution)/shard_map/gqkvo/y/ppermute | solution.py:93
  263.7 1.8 add_convert_fusion.8
  265.4 4.6 %collective-permute-done.41 = bf16[144,1024]{1,0:T(8,128)(2,1)S(1)} collective-permute-done((bf16[144,1024]{1,0:T(8,128)(2,1)}, bf16[144,1024]{1,0:T(8,128)(2,1)S(1)}, u32[]{:S(2)}, u32[]{:S(2)}) %collective-permute-start.41) | collective-permute-done | bytes 294944 | tf_op jit(solution)/shard_map/gqkvo/y/ppermute | solution.py:93
  270.0 1.8 add_convert_fusion.7
  271.8 4.6 %collective-permute-done.43 = bf16[144,1024]{1,0:T(8,128)(2,1)S(1)} collective-permute-done((bf16[144,1024]{1,0:T(8,128)(2,1)}, bf16[144,1024]{1,0:T(8,128)(2,1)S(1)}, u32[]{:S(2)}, u32[]{:S(2)}) %collective-permute-start.43) | collective-permute-done | bytes 294944 | tf_op jit(solution)/shard_map/gqkvo/y/ppermute | solution.py:93
  276.6 1.8 add_convert_fusion.6
  278.4 2.1 collective-permute-start.42
  283.0 3.0 collective-permute-start.32
  286.4 12.1 %collective-permute-done.42 = bf16[144,1024]{1,0:T(8,128)(2,1)} collective-permute-done((bf16[144,1024]{1,0:T(8,128)(2,1)}, bf16[144,1024]{1,0:T(8,128)(2,1)}, u32[]{:S(2)}, u32[]{:S(2)}) %collective-permute-start.42) | collective-permute-done | bytes 294944 | tf_op jit(solution)/shard_map/gqkvo/z2/ppermute | solution.py:98
  298.5 4.0 %collective-permute-start.51 = (bf16[128,1024]{1,0:T(8,128)(2,1)}, bf16[128,1024]{1,0:T(8,128)(2,1)S(1)}, u32[]{:S(2)}, u32[]{:S(2)}) collective-permute-start(bf16[128,1024]{1,0:T(8,128)(2,1)} %copy-done.22), channel_id=1, source_target_pairs={{0,8},{8,0},{16,24},{24,16},{1,9},{9,1},{17,25},{25,17},{2,10},{10... | collective-permute-start | bytes 786440 | tf_op jit(solution)/shard_map/fdown/seq1/ppermute | solution.py:71
  302.5 2.8 collective-permute-done.44
  305.3 2.7 collective-permute-start.46
  311.0 3.9 %finish_ffn.1 = (f32[128,4096]{1,0:T(8,128)}, f32[512,1024]{1,0:T(8,128)}) custom-call(s32[2]{0:T(128)} %pad_add_fusion.ids, bf16[128,1024]{1,0:T(8,128)(2,1)} %copy-done.5, bf16[128,1024]{1,0:T(8,128)(2,1)} %copy-done.25, bf16[128,1024]{1,0:T(8,128)(2,1)} %copy-done.23, bf16[128,1024]{1,0:T(8,128)(2,1)} %copy-done.26, bf16[128,1024]{1,0:T(8,128)(2,1)} %copy-done.4, ...), custom_call_target="tpu_custom_call" | custom-call | bytes 6291464 | tf_op jit(solution)/shard_map/finish_ffn/pallas_call | solution.py:54
  316.6 6.5 %collective-permute-done.53.c2 = bf16[144,1024]{1,0:T(8,128)(2,1)S(1)} collective-permute-done((bf16[144,1024]{1,0:T(8,128)(2,1)S(1)}, bf16[144,1024]{1,0:T(8,128)(2,1)S(1)}, u32[]{:S(2)}, u32[]{:S(2)}) %collective-permute-start.53) | collective-permute-done | bytes 294944 | tf_op jit(solution)/shard_map/gqkvo/seq2/ppermute | solution.py:71
  327.1 2.7 finish_qkvo.1
  (218 shorter events, 61.8 us)
Async XLA Ops:
  7.2 107.0 %all-gather.3.cloned.1.call-start = ((), (), s32[]{:S(2)}) async-start(), calls=%async_computation.2 | async-start | bytes 4718592 | tf_op jit(solution)/shard_map/ffnw/all_gather | solution.py:887
  7.2 30.4 %collective-permute-start.1 = (bf16[2,128,1024]{2,1,0:T(8,128)(2,1)}, bf16[2,128,1024]{2,1,0:T(8,128)(2,1)S(1)}, u32[]{:S(2)}, u32[]{:S(2)}) collective-permute-start(bf16[2,128,1024]{2,1,0:T(8,128)(2,1)} %x0.3), channel_id=1, source_target_pairs={{0,16},{8,24},{16,0},{24,8},{1,17},{9,25},{17,1},{25,9},{2,18},{10... | collective-permute-start | bytes 1572872 | tf_op jit(solution)/shard_map/tok/seq2/ppermute | solution.py:71
  11.7 7.8 %collective-permute-start.6 = (bf16[144,1024]{1,0:T(8,128)(2,1)}, bf16[144,1024]{1,0:T(8,128)(2,1)S(1)}, u32[]{:S(2)}, u32[]{:S(2)}) collective-permute-start(bf16[144,1024]{1,0:T(8,128)(2,1)} %early_pack.1.refs_0_), channel_id=1, source_target_pairs={{0,1},{1,0},{2,3},{3,2},{4,5},{5,4},{6,7},{7,6},{8,9},{9,8},{10,11... | collective-permute-start | bytes 884744 | tf_op jit(solution)/shard_map/wqkv/y/ppermute | solution.py:93
  12.0 20.8 %collective-permute-start.5 = (bf16[144,1024]{1,0:T(8,128)(2,1)}, bf16[144,1024]{1,0:T(8,128)(2,1)S(1)}, u32[]{:S(2)}, u32[]{:S(2)}) collective-permute-start(bf16[144,1024]{1,0:T(8,128)(2,1)} %early_pack.1.refs_0_), channel_id=1, source_target_pairs={{0,6},{2,4},{4,2},{6,0},{1,7},{3,5},{5,3},{7,1},{8,14},{10,12},{12... | collective-permute-start | bytes 884744 | tf_op jit(solution)/shard_map/wqkv/z3/ppermute | solution.py:98
  13.3 24.3 %collective-permute-start.4 = (bf16[144,1024]{1,0:T(8,128)(2,1)}, bf16[144,1024]{1,0:T(8,128)(2,1)S(1)}, u32[]{:S(2)}, u32[]{:S(2)}) collective-permute-start(bf16[144,1024]{1,0:T(8,128)(2,1)} %early_pack.1.refs_0_), channel_id=1, source_target_pairs={{0,4},{2,6},{4,0},{6,2},{1,5},{3,7},{5,1},{7,3},{8,12},{10,14},{12... | collective-permute-start | bytes 884744 | tf_op jit(solution)/shard_map/wqkv/z2/ppermute | solution.py:98
  14.3 23.3 %collective-permute-start.3 = (bf16[144,1024]{1,0:T(8,128)(2,1)}, bf16[144,1024]{1,0:T(8,128)(2,1)S(1)}, u32[]{:S(2)}, u32[]{:S(2)}) collective-permute-start(bf16[144,1024]{1,0:T(8,128)(2,1)} %early_pack.1.refs_0_), channel_id=1, source_target_pairs={{0,2},{2,0},{4,6},{6,4},{1,3},{3,1},{5,7},{7,5},{8,10},{10,8},{12,... | collective-permute-start | bytes 884744 | tf_op jit(solution)/shard_map/wqkv/z1/ppermute | solution.py:98
  37.7 31.5 %collective-permute-start = (bf16[2,128,1024]{2,1,0:T(8,128)(2,1)S(1)}, bf16[2,128,1024]{2,1,0:T(8,128)(2,1)S(1)}, u32[]{:S(2)}, u32[]{:S(2)}) collective-permute-start(bf16[2,128,1024]{2,1,0:T(8,128)(2,1)S(1)} %copy-done.14), channel_id=1, source_target_pairs={{0,8},{8,0},{16,24},{24,16},{1,9},{9,1},{17,25},{25,17},{2,10},{10... | collective-permute-start | bytes 1572872 | tf_op jit(solution)/shard_map/tok/seq1/ppermute | solution.py:71
  40.8 8.6 %collective-permute-start.7 = (bf16[144,1024]{1,0:T(8,128)(2,1)S(1)}, bf16[144,1024]{1,0:T(8,128)(2,1)S(1)}, u32[]{:S(2)}, u32[]{:S(2)}) collective-permute-start(bf16[144,1024]{1,0:T(8,128)(2,1)S(1)} %collective-permute-done.3.refs_1_), channel_id=1, source_target_pairs={{0,1},{1,0},{2,3},{3,2},{4,5},{5,4},{6,7},{7,6},{8,9},{9,8},{10,11... | collective-permute-start | bytes 884744 | tf_op jit(solution)/shard_map/wqkv/y/ppermute | solution.py:93
  42.1 18.9 %collective-permute-start.8 = (bf16[144,1024]{1,0:T(8,128)(2,1)S(1)}, bf16[144,1024]{1,0:T(8,128)(2,1)S(1)}, u32[]{:S(2)}, u32[]{:S(2)}) collective-permute-start(bf16[144,1024]{1,0:T(8,128)(2,1)S(1)} %collective-permute-done.4.refs_2_), channel_id=1, source_target_pairs={{0,1},{1,0},{2,3},{3,2},{4,5},{5,4},{6,7},{7,6},{8,9},{9,8},{10,11... | collective-permute-start | bytes 884744 | tf_op jit(solution)/shard_map/wqkv/y/ppermute | solution.py:93
  42.4 25.4 %collective-permute-start.9 = (bf16[144,1024]{1,0:T(8,128)(2,1)S(1)}, bf16[144,1024]{1,0:T(8,128)(2,1)S(1)}, u32[]{:S(2)}, u32[]{:S(2)}) collective-permute-start(bf16[144,1024]{1,0:T(8,128)(2,1)S(1)} %collective-permute-done.5.refs_3_), channel_id=1, source_target_pairs={{0,1},{1,0},{2,3},{3,2},{4,5},{5,4},{6,7},{7,6},{8,9},{9,8},{10,11... | collective-permute-start | bytes 884744 | tf_op jit(solution)/shard_map/wqkv/y/ppermute | solution.py:93
  43.7 25.5 %collective-permute-start.2 = (bf16[2,128,1024]{2,1,0:T(8,128)(2,1)S(1)}, bf16[2,128,1024]{2,1,0:T(8,128)(2,1)S(1)}, u32[]{:S(2)}, u32[]{:S(2)}) collective-permute-start(bf16[2,128,1024]{2,1,0:T(8,128)(2,1)S(1)} %collective-permute-done.1.x2), channel_id=1, source_target_pairs={{0,8},{8,0},{16,24},{24,16},{1,9},{9,1},{17,25},{25,17},{2,10},{10... | collective-permute-start | bytes 1572872 | tf_op jit(solution)/shard_map/tok/seq1/ppermute | solution.py:71
  67.8 13.7 %collective-permute-start.14 = (bf16[8,128,256]{2,1,0:T(8,128)(2,1)S(1)}, bf16[8,128,256]{2,1,0:T(8,128)(2,1)S(1)}, u32[]{:S(2)}, u32[]{:S(2)}) collective-permute-start(bf16[8,128,256]{2,1,0:T(8,128)(2,1)S(1)} %fusion.3.w0), channel_id=1, source_target_pairs={{0,16},{8,24},{16,0},{24,8},{1,17},{9,25},{17,1},{25,9},{2,18},{10... | collective-permute-start | bytes 1572872 | tf_op jit(solution)/shard_map/wo/seq2/ppermute | solution.py:71
  68.1 22.7 %collective-permute-start.13 = (bf16[8,128,256]{2,1,0:T(8,128)(2,1)S(1)}, bf16[8,128,256]{2,1,0:T(8,128)(2,1)S(1)}, u32[]{:S(2)}, u32[]{:S(2)}) collective-permute-start(bf16[8,128,256]{2,1,0:T(8,128)(2,1)S(1)} %fusion.3.w0), channel_id=1, source_target_pairs={{0,8},{8,0},{16,24},{24,16},{1,9},{9,1},{17,25},{25,17},{2,10},{10... | collective-permute-start | bytes 1572872 | tf_op jit(solution)/shard_map/wo/seq1/ppermute | solution.py:71
  81.6 9.3 %collective-permute-start.15 = (bf16[8,128,256]{2,1,0:T(8,128)(2,1)S(1)}, bf16[8,128,256]{2,1,0:T(8,128)(2,1)S(1)}, u32[]{:S(2)}, u32[]{:S(2)}) collective-permute-start(bf16[8,128,256]{2,1,0:T(8,128)(2,1)S(1)} %collective-permute-done.14.w2), channel_id=1, source_target_pairs={{0,8},{8,0},{16,24},{24,16},{1,9},{9,1},{17,25},{25,17},{2,10},{10... | collective-permute-start | bytes 1572872 | tf_op jit(solution)/shard_map/wo/seq1/ppermute | solution.py:71
  82.2 4.9 %collective-permute-start.11 = (bf16[256,256]{1,0:T(8,128)(2,1)}, bf16[256,256]{1,0:T(8,128)(2,1)S(1)}, u32[]{:S(2)}, u32[]{:S(2)}) collective-permute-start(bf16[256,256]{1,0:T(8,128)(2,1)} %bitcast.71), channel_id=1, source_target_pairs={{0,16},{8,24},{16,0},{24,8},{1,17},{9,25},{17,1},{25,9},{2,18},{10... | collective-permute-start | bytes 393224 | tf_op jit(solution)/shard_map/mix/seq2/ppermute | solution.py:71
  83.4 7.5 %collective-permute-start.12 = (bf16[256,256]{1,0:T(8,128)(2,1)}, bf16[256,256]{1,0:T(8,128)(2,1)S(1)}, u32[]{:S(2)}, u32[]{:S(2)}) collective-permute-start(bf16[256,256]{1,0:T(8,128)(2,1)} %bitcast.70), channel_id=1, source_target_pairs={{0,24},{8,16},{16,8},{24,0},{1,25},{9,17},{17,9},{25,1},{2,26},{10... | collective-permute-start | bytes 393224 | tf_op jit(solution)/shard_map/mix/seq3/ppermute | solution.py:71
  97.4 14.1 %collective-permute-start.17 = (bf16[256,1024]{1,0:T(8,128)(2,1)}, bf16[256,1024]{1,0:T(8,128)(2,1)S(1)}, u32[]{:S(2)}, u32[]{:S(2)}) collective-permute-start(bf16[256,1024]{1,0:T(8,128)(2,1)} %get-tuple-element.113.f0.refs_2_), channel_id=1, source_target_pairs={{0,16},{8,24},{16,0},{24,8},{1,17},{9,25},{17,1},{25,9},{2,18},{10... | collective-permute-start | bytes 1572872 | tf_op jit(solution)/shard_map/first/seq2/ppermute | solution.py:71
  98.6 13.0 %collective-permute-start.16 = (bf16[256,1024]{1,0:T(8,128)(2,1)}, bf16[256,1024]{1,0:T(8,128)(2,1)S(1)}, u32[]{:S(2)}, u32[]{:S(2)}) collective-permute-start(bf16[256,1024]{1,0:T(8,128)(2,1)} %get-tuple-element.113.f0.refs_2_), channel_id=1, source_target_pairs={{0,8},{8,0},{16,24},{24,16},{1,9},{9,1},{17,25},{25,17},{2,10},{10... | collective-permute-start | bytes 1572872 | tf_op jit(solution)/shard_map/first/seq1/ppermute | solution.py:71
  129.5 13.2 %collective-permute-start.21 = (bf16[256,1024]{1,0:T(8,128)(2,1)S(1)}, bf16[256,1024]{1,0:T(8,128)(2,1)S(1)}, u32[]{:S(2)}, u32[]{:S(2)}) collective-permute-start(bf16[256,1024]{1,0:T(8,128)(2,1)S(1)} %add_convert_fusion.4), channel_id=1, source_target_pairs={{0,16},{8,24},{16,0},{24,8},{1,17},{9,25},{17,1},{25,9},{2,18},{10... | collective-permute-start | bytes 1572872 | tf_op jit(solution)/shard_map/ffn/seq2/ppermute | solution.py:71
  147.6 12.4 %collective-permute-start.23 = (bf16[256,1024]{1,0:T(8,128)(2,1)}, bf16[256,1024]{1,0:T(8,128)(2,1)S(1)}, u32[]{:S(2)}, u32[]{:S(2)}) collective-permute-start(bf16[256,1024]{1,0:T(8,128)(2,1)} %get-tuple-element.121.d0.refs_3_), channel_id=1, source_target_pairs={{0,16},{8,24},{16,0},{24,8},{1,17},{9,25},{17,1},{25,9},{2,18},{10... | collective-permute-start | bytes 1572872 | tf_op jit(solution)/shard_map/low/seq2/ppermute | solution.py:71
  148.8 13.4 %collective-permute-start.22 = (bf16[256,1024]{1,0:T(8,128)(2,1)}, bf16[256,1024]{1,0:T(8,128)(2,1)S(1)}, u32[]{:S(2)}, u32[]{:S(2)}) collective-permute-start(bf16[256,1024]{1,0:T(8,128)(2,1)} %get-tuple-element.121.d0.refs_3_), channel_id=1, source_target_pairs={{0,8},{8,0},{16,24},{24,16},{1,9},{9,1},{17,25},{25,17},{2,10},{10... | collective-permute-start | bytes 1572872 | tf_op jit(solution)/shard_map/low/seq1/ppermute | solution.py:71
  184.0 24.7 %collective-permute-start.35 = (bf16[4,128,1024]{2,1,0:T(8,128)(2,1)}, bf16[4,128,1024]{2,1,0:T(8,128)(2,1)S(1)}, u32[]{:S(2)}, u32[]{:S(2)}) collective-permute-start(bf16[4,128,1024]{2,1,0:T(8,128)(2,1)} %get-tuple-element.154), channel_id=1, source_target_pairs={{0,1},{1,0},{2,3},{3,2},{4,5},{5,4},{6,7},{7,6},{8,9},{9,8},{10,11... | collective-permute-start | bytes 3145736 | tf_op jit(solution)/shard_map/gdown/y/ppermute | solution.py:93
  185.1 8.1 %collective-permute-start.26 = (bf16[256,1024]{1,0:T(8,128)(2,1)S(1)}, bf16[256,1024]{1,0:T(8,128)(2,1)S(1)}, u32[]{:S(2)}, u32[]{:S(2)}) collective-permute-start(bf16[256,1024]{1,0:T(8,128)(2,1)S(1)} %copy-done.45), channel_id=1, source_target_pairs={{0,8},{8,0},{16,24},{24,16},{1,9},{9,1},{17,25},{25,17},{2,10},{10... | collective-permute-start | bytes 1572872 | tf_op jit(solution)/shard_map/ffnback/seq1/ppermute | solution.py:71
  185.8 13.6 %collective-permute-start.27 = (bf16[256,1024]{1,0:T(8,128)(2,1)S(1)}, bf16[256,1024]{1,0:T(8,128)(2,1)S(1)}, u32[]{:S(2)}, u32[]{:S(2)}) collective-permute-start(bf16[256,1024]{1,0:T(8,128)(2,1)S(1)} %add_convert_fusion.3), channel_id=1, source_target_pairs={{0,16},{8,24},{16,0},{24,8},{1,17},{9,25},{17,1},{25,9},{2,18},{10... | collective-permute-start | bytes 1572872 | tf_op jit(solution)/shard_map/ffnback/seq2/ppermute | solution.py:71
  210.1 33.8 %all-to-all-start = ((bf16[4,128,1024]{2,1,0:T(8,128)(2,1)}), bf16[4,128,1024]{2,1,0:T(8,128)(2,1)S(1)}, u32[]{:S(2)}, u32[]{:S(2)}) async-start(bf16[4,128,1024]{2,1,0:T(8,128)(2,1)} %add_convert_fusion.1), calls=%async_computation | async-start | bytes 2097152 | tf_op jit(solution)/shard_map/gdown/z/all_to_all | solution.py:103
  214.9 5.0 %collective-permute-start.28 = (bf16[1024,256]{1,0:T(8,128)(2,1)S(1)}, bf16[1024,256]{1,0:T(8,128)(2,1)S(1)}, u32[]{:S(2)}, u32[]{:S(2)}) collective-permute-start(bf16[1024,256]{1,0:T(8,128)(2,1)S(1)} %copy-done.48), channel_id=1, source_target_pairs={{0,8},{8,0},{16,24},{24,16},{1,9},{9,1},{17,25},{25,17},{2,10},{10... | collective-permute-start | bytes 1572872 | tf_op jit(solution)/shard_map/outs/seq1/ppermute | solution.py:71
  216.5 26.1 %collective-permute-start.36 = (bf16[4,128,1024]{2,1,0:T(8,128)(2,1)}, bf16[4,128,1024]{2,1,0:T(8,128)(2,1)S(1)}, u32[]{:S(2)}, u32[]{:S(2)}) collective-permute-start(bf16[4,128,1024]{2,1,0:T(8,128)(2,1)} %get-tuple-element.157), channel_id=1, source_target_pairs={{0,1},{1,0},{2,3},{3,2},{4,5},{5,4},{6,7},{7,6},{8,9},{9,8},{10,11... | collective-permute-start | bytes 3145736 | tf_op jit(solution)/shard_map/gup/y/ppermute | solution.py:93
  218.1 4.9 %collective-permute-start.30 = (bf16[256,256]{1,0:T(8,128)(2,1)S(1)}, bf16[256,256]{1,0:T(8,128)(2,1)S(1)}, u32[]{:S(2)}, u32[]{:S(2)}) collective-permute-start(bf16[256,256]{1,0:T(8,128)(2,1)S(1)} %copy-done.51), channel_id=1, source_target_pairs={{0,16},{8,24},{16,0},{24,8},{1,17},{9,25},{17,1},{25,9},{2,18},{10... | collective-permute-start | bytes 393224 | tf_op jit(solution)/shard_map/mixback/seq2/ppermute | solution.py:71
  219.1 7.9 %collective-permute-start.31 = (bf16[256,256]{1,0:T(8,128)(2,1)S(1)}, bf16[256,256]{1,0:T(8,128)(2,1)S(1)}, u32[]{:S(2)}, u32[]{:S(2)}) collective-permute-start(bf16[256,256]{1,0:T(8,128)(2,1)S(1)} %copy-done.50), channel_id=1, source_target_pairs={{0,24},{8,16},{16,8},{24,0},{1,25},{9,17},{17,9},{25,1},{2,26},{10... | collective-permute-start | bytes 393224 | tf_op jit(solution)/shard_map/mixback/seq3/ppermute | solution.py:71
  219.9 28.8 %collective-permute-start.37 = (bf16[1024,256]{1,0:T(8,128)(2,1)S(1)}, bf16[1024,256]{1,0:T(8,128)(2,1)}, u32[]{:S(2)}, u32[]{:S(2)}) collective-permute-start(bf16[1024,256]{1,0:T(8,128)(2,1)S(1)} %copy-done.44), channel_id=1, source_target_pairs={{0,8},{8,0},{16,24},{24,16},{1,9},{9,1},{17,25},{25,17},{2,10},{10... | collective-permute-start | bytes 1572872 | tf_op jit(solution)/shard_map/outs/seq1/ppermute | solution.py:71
  220.1 28.6 %collective-permute-start.38 = (bf16[1024,256]{1,0:T(8,128)(2,1)S(1)}, bf16[1024,256]{1,0:T(8,128)(2,1)}, u32[]{:S(2)}, u32[]{:S(2)}) collective-permute-start(bf16[1024,256]{1,0:T(8,128)(2,1)S(1)} %add_convert_fusion.2), channel_id=1, source_target_pairs={{0,16},{8,24},{16,0},{24,8},{1,17},{9,25},{17,1},{25,9},{2,18},{10... | collective-permute-start | bytes 1572872 | tf_op jit(solution)/shard_map/outs/seq2/ppermute | solution.py:71
  244.0 37.5 %all-to-all-start.1 = ((bf16[4,128,1024]{2,1,0:T(8,128)(2,1)}), bf16[4,128,1024]{2,1,0:T(8,128)(2,1)S(1)}, u32[]{:S(2)}, u32[]{:S(2)}) async-start(bf16[4,128,1024]{2,1,0:T(8,128)(2,1)} %add_convert_fusion), calls=%async_computation.1 | async-start | bytes 2097152 | tf_op jit(solution)/shard_map/gup/z/all_to_all | solution.py:103
  255.0 8.6 %collective-permute-start.39 = (bf16[144,1024]{1,0:T(8,128)(2,1)}, bf16[144,1024]{1,0:T(8,128)(2,1)S(1)}, u32[]{:S(2)}, u32[]{:S(2)}) collective-permute-start(bf16[144,1024]{1,0:T(8,128)(2,1)} %get-tuple-element.166), channel_id=1, source_target_pairs={{0,1},{1,0},{2,3},{3,2},{4,5},{5,4},{6,7},{7,6},{8,9},{9,8},{10,11... | collective-permute-start | bytes 884744 | tf_op jit(solution)/shard_map/gqkvo/y/ppermute | solution.py:93
  255.3 14.7 %collective-permute-start.41 = (bf16[144,1024]{1,0:T(8,128)(2,1)}, bf16[144,1024]{1,0:T(8,128)(2,1)S(1)}, u32[]{:S(2)}, u32[]{:S(2)}) collective-permute-start(bf16[144,1024]{1,0:T(8,128)(2,1)} %get-tuple-element.168), channel_id=1, source_target_pairs={{0,1},{1,0},{2,3},{3,2},{4,5},{5,4},{6,7},{7,6},{8,9},{9,8},{10,11... | collective-permute-start | bytes 884744 | tf_op jit(solution)/shard_map/gqkvo/y/ppermute | solution.py:93
  256.6 21.8 %collective-permute-start.33 = (bf16[256,1024]{1,0:T(8,128)(2,1)S(1)}, bf16[256,1024]{1,0:T(8,128)(2,1)S(1)}, u32[]{:S(2)}, u32[]{:S(2)}) collective-permute-start(bf16[256,1024]{1,0:T(8,128)(2,1)S(1)} %bitcast.65), channel_id=1, source_target_pairs={{0,8},{8,0},{16,24},{24,16},{1,9},{9,1},{17,25},{25,17},{2,10},{10... | collective-permute-start | bytes 1572872 | tf_op jit(solution)/shard_map/input/seq1/ppermute | solution.py:71
  257.4 23.1 %collective-permute-start.50 = (bf16[128,1024]{1,0:T(8,128)(2,1)S(1)}, bf16[128,1024]{1,0:T(8,128)(2,1)S(1)}, u32[]{:S(2)}, u32[]{:S(2)}) collective-permute-start(bf16[128,1024]{1,0:T(8,128)(2,1)S(1)} %reduce_sum.24.refs_4_), channel_id=1, source_target_pairs={{0,16},{8,24},{16,0},{24,8},{1,17},{9,25},{17,1},{25,9},{2,18},{10... | collective-permute-start | bytes 786440 | tf_op jit(solution)/shard_map/fdown/seq2/ppermute | solution.py:71
  258.4 23.2 %collective-permute-start.49 = (bf16[128,1024]{1,0:T(8,128)(2,1)S(1)}, bf16[128,1024]{1,0:T(8,128)(2,1)}, u32[]{:S(2)}, u32[]{:S(2)}) collective-permute-start(bf16[128,1024]{1,0:T(8,128)(2,1)S(1)} %reduce_sum.24.refs_4_), channel_id=1, source_target_pairs={{0,8},{8,0},{16,24},{24,16},{1,9},{9,1},{17,25},{25,17},{2,10},{10... | collective-permute-start | bytes 786440 | tf_op jit(solution)/shard_map/fdown/seq1/ppermute | solution.py:71
  263.7 12.6 %collective-permute-start.43 = (bf16[144,1024]{1,0:T(8,128)(2,1)}, bf16[144,1024]{1,0:T(8,128)(2,1)S(1)}, u32[]{:S(2)}, u32[]{:S(2)}) collective-permute-start(bf16[144,1024]{1,0:T(8,128)(2,1)} %get-tuple-element.170), channel_id=1, source_target_pairs={{0,1},{1,0},{2,3},{3,2},{4,5},{5,4},{6,7},{7,6},{8,9},{9,8},{10,11... | collective-permute-start | bytes 884744 | tf_op jit(solution)/shard_map/gqkvo/y/ppermute | solution.py:93
  270.0 13.0 %collective-permute-start.45 = (bf16[144,1024]{1,0:T(8,128)(2,1)}, bf16[144,1024]{1,0:T(8,128)(2,1)S(1)}, u32[]{:S(2)}, u32[]{:S(2)}) collective-permute-start(bf16[144,1024]{1,0:T(8,128)(2,1)} %get-tuple-element.172), channel_id=1, source_target_pairs={{0,1},{1,0},{2,3},{3,2},{4,5},{5,4},{6,7},{7,6},{8,9},{9,8},{10,11... | collective-permute-start | bytes 884744 | tf_op jit(solution)/shard_map/gqkvo/y/ppermute | solution.py:93
  276.3 9.6 %collective-permute-start.40 = (bf16[144,1024]{1,0:T(8,128)(2,1)}, bf16[144,1024]{1,0:T(8,128)(2,1)S(1)}, u32[]{:S(2)}, u32[]{:S(2)}) collective-permute-start(bf16[144,1024]{1,0:T(8,128)(2,1)} %add_convert_fusion.8), channel_id=1, source_target_pairs={{0,2},{2,0},{4,6},{6,4},{1,3},{3,1},{5,7},{7,5},{8,10},{10,8},{12,... | collective-permute-start | bytes 884744 | tf_op jit(solution)/shard_map/gqkvo/z1/ppermute | solution.py:98
  278.4 20.1 %collective-permute-start.42 = (bf16[144,1024]{1,0:T(8,128)(2,1)}, bf16[144,1024]{1,0:T(8,128)(2,1)}, u32[]{:S(2)}, u32[]{:S(2)}) collective-permute-start(bf16[144,1024]{1,0:T(8,128)(2,1)} %add_convert_fusion.7), channel_id=1, source_target_pairs={{0,4},{2,6},{4,0},{6,2},{1,5},{3,7},{5,1},{7,3},{8,12},{10,14},{12... | collective-permute-start | bytes 884744 | tf_op jit(solution)/shard_map/gqkvo/z2/ppermute | solution.py:98
  281.2 24.1 %collective-permute-start.44 = (bf16[144,1024]{1,0:T(8,128)(2,1)}, bf16[144,1024]{1,0:T(8,128)(2,1)}, u32[]{:S(2)}, u32[]{:S(2)}) collective-permute-start(bf16[144,1024]{1,0:T(8,128)(2,1)} %add_convert_fusion.6), channel_id=1, source_target_pairs={{0,6},{2,4},{4,2},{6,0},{1,7},{3,5},{5,3},{7,1},{8,14},{10,12},{12... | collective-permute-start | bytes 884744 | tf_op jit(solution)/shard_map/gqkvo/z3/ppermute | solution.py:98
  281.7 26.3 %collective-permute-start.47 = (bf16[128,1024]{1,0:T(8,128)(2,1)S(1)}, bf16[128,1024]{1,0:T(8,128)(2,1)S(1)}, u32[]{:S(2)}, u32[]{:S(2)}) collective-permute-start(bf16[128,1024]{1,0:T(8,128)(2,1)S(1)} %reduce_sum.25.refs_0_), channel_id=1, source_target_pairs={{0,16},{8,24},{16,0},{24,8},{1,17},{9,25},{17,1},{25,9},{2,18},{10... | collective-permute-start | bytes 786440 | tf_op jit(solution)/shard_map/fup/seq2/ppermute | solution.py:71
  283.0 41.3 %collective-permute-start.32 = (bf16[256,1024]{1,0:T(8,128)(2,1)}, bf16[256,1024]{1,0:T(8,128)(2,1)S(1)}, u32[]{:S(2)}, u32[]{:S(2)}) collective-permute-start(bf16[256,1024]{1,0:T(8,128)(2,1)} %bitcast.64), channel_id=1, source_target_pairs={{0,8},{8,0},{16,24},{24,16},{1,9},{9,1},{17,25},{25,17},{2,10},{10... | collective-permute-start | bytes 1572872 | tf_op jit(solution)/shard_map/input/seq1/ppermute | solution.py:71
  285.9 38.4 %collective-permute-start.34 = (bf16[256,1024]{1,0:T(8,128)(2,1)S(1)}, bf16[256,1024]{1,0:T(8,128)(2,1)S(1)}, u32[]{:S(2)}, u32[]{:S(2)}) collective-permute-start(bf16[256,1024]{1,0:T(8,128)(2,1)S(1)} %fusion), channel_id=1, source_target_pairs={{0,16},{8,24},{16,0},{24,8},{1,17},{9,25},{17,1},{25,9},{2,18},{10... | collective-permute-start | bytes 1572872 | tf_op jit(solution)/shard_map/input/seq2/ppermute | solution.py:71
  298.5 10.9 %collective-permute-start.51 = (bf16[128,1024]{1,0:T(8,128)(2,1)}, bf16[128,1024]{1,0:T(8,128)(2,1)S(1)}, u32[]{:S(2)}, u32[]{:S(2)}) collective-permute-start(bf16[128,1024]{1,0:T(8,128)(2,1)} %copy-done.22), channel_id=1, source_target_pairs={{0,8},{8,0},{16,24},{24,16},{1,9},{9,1},{17,25},{25,17},{2,10},{10... | collective-permute-start | bytes 786440 | tf_op jit(solution)/shard_map/fdown/seq1/ppermute | solution.py:71
  314.9 8.2 %collective-permute-start.53 = (bf16[144,1024]{1,0:T(8,128)(2,1)S(1)}, bf16[144,1024]{1,0:T(8,128)(2,1)S(1)}, u32[]{:S(2)}, u32[]{:S(2)}) collective-permute-start(bf16[144,1024]{1,0:T(8,128)(2,1)S(1)} %add_convert_fusion.5.c0), channel_id=1, source_target_pairs={{0,16},{8,24},{16,0},{24,8},{1,17},{9,25},{17,1},{25,9},{2,18},{10... | collective-permute-start | bytes 884744 | tf_op jit(solution)/shard_map/gqkvo/seq2/ppermute | solution.py:71
  315.9 9.8 %collective-permute-start.52 = (bf16[144,1024]{1,0:T(8,128)(2,1)S(1)}, bf16[144,1024]{1,0:T(8,128)(2,1)S(1)}, u32[]{:S(2)}, u32[]{:S(2)}) collective-permute-start(bf16[144,1024]{1,0:T(8,128)(2,1)S(1)} %add_convert_fusion.5.c0), channel_id=1, source_target_pairs={{0,8},{8,0},{16,24},{24,16},{1,9},{9,1},{17,25},{25,17},{2,10},{10... | collective-permute-start | bytes 884744 | tf_op jit(solution)/shard_map/gqkvo/seq1/ppermute | solution.py:71
  (66 other events, 647.5 us)
Sparse Core Ops, SparseCore 0:
  37.8 76.3 all-gather.2

commit v3 on v2

--- a/solution.py
+++ b/solution.py
@@ -19,6 +19,8 @@
 ROW_QB, ROW_VB, ROW_OB, ROW_DB, ROW_G1, ROW_S1, ROW_G2, ROW_S2, ROW_UB = range(9)
 VMEM = pltpu.VMEM
 ANY = pl.ANY
+HBM = pltpu.HBM
+LIMITS = {"early_pack": 56, "late_pack": 56}
 
 
 def dot(a, b):
@@ -45,7 +47,7 @@
     return pl.BlockSpec(memory_space=space)
 
 
-def call(kernel, outs, args, *, name, grid=None, in_specs=None, out_specs=None, scratch=(), flops=0, trans=0):
+def call(kernel, outs, args, *, name, grid=None, in_specs=None, out_specs=None, scratch=(), flops=0, trans=0, light=1):
     if in_specs is None:
         in_specs = [whole() for _ in args]
     if out_specs is None:
@@ -57,9 +59,11 @@
         in_specs=in_specs,
         out_specs=out_specs,
         scratch_shapes=list(scratch),
-        compiler_params=pltpu.CompilerParams(vmem_limit_bytes=56 << 20),
+        compiler_params=pltpu.CompilerParams(vmem_limit_bytes=LIMITS.get(name, 20) << 20),
         cost_estimate=pl.CostEstimate(
-            flops=flops, bytes_accessed=nbytes(args) + nbytes(outs), transcendentals=trans
+            flops=flops // light,
+            bytes_accessed=(nbytes(args) + nbytes(outs)) // light,
+            transcendentals=trans,
         ),
         name=name,
         **kwargs,
@@ -77,11 +81,11 @@
     return [value, near, far, seq_swap(after(far, *others), 1)]
 
 
-def reduce_seq(parts):
-    near0 = seq_swap(parts[1], 1)
+def reduce_seq(parts, *others):
     near2 = seq_swap(parts[3], 1)
     onward = (parts[2].astype(F32) + near2.astype(F32)).astype(BF16)
-    return [parts[0], near0, seq_swap(onward, 2)], onward
+    near0 = seq_swap(after(parts[1], onward), 1)
+    return [parts[0], near0, seq_swap(after(onward, *others), 2)], onward
 
 
 def exchange_seq(parts):
@@ -109,6 +113,19 @@
 
 def fits(n):
     return n % 128 == 0
+
+
+def row_copies(blocks, target, sems):
+    rows = blocks[0].shape[0]
+    return [
+        pltpu.make_async_copy(x, target.at[pl.ds(i * rows, rows), :], sems.at[i])
+        for i, x in enumerate(blocks)
+        if x is not None
+    ]
+
+
+def hbm(value):
+    return pltpu.with_memory_space_constraint(value, HBM)
 
 
 def run_copies(copies):
@@ -165,7 +182,7 @@
             struct((n + VEC, d), BF16),
             (ids, wq, wk, wv, wo, *vectors, up_bias),
             name="early_pack",
-            in_specs=[whole(pltpu.SMEM)] + [whole(ANY)] * 4 + [whole()] * (len(vectors) + 1),
+            in_specs=[whole(pltpu.SMEM)] + [whole(HBM)] * 4 + [whole()] * (len(vectors) + 1),
             scratch=[pltpu.SemaphoreType.DMA((4,))],
         )
     rows = jnp.concatenate(vectors + [up_bias]).reshape(-1, n)
@@ -183,21 +200,20 @@
             struct((n + w, d), BF16),
             (ids, up, down),
             name="late_pack",
-            in_specs=[whole(pltpu.SMEM)] + [whole(ANY)] * 2,
+            in_specs=[whole(pltpu.SMEM)] + [whole(HBM)] * 2,
             scratch=[pltpu.SemaphoreType.DMA((fs + 1,))],
         )
     mine = lax.dynamic_index_in_dim(up.reshape(n, fs, SEQ_N, w), s, 2, keepdims=False)
     return jnp.concatenate([mine.reshape(n, fs * w), lax.dynamic_slice(down, (s * w, 0), (w, d))], 0)
 
 
-def gather_early(value, fs, *others):
+def gather_early(value, fs):
     zs = fs // 2
     if zs != 4:
         own = turn_z(jnp.broadcast_to(value, (zs,) + value.shape))
         return [own, swap_y(own)]
     own = [value] + [swap_z(value, k, zs) for k in (3, 2, 1)][::-1]
-    first = swap_y(value)
-    return own + [first] + [swap_y(after(own[k], *others)) for k in (1, 2, 3)]
+    return own + [swap_y(own[k]) for k in range(zs)]
 
 
 def load_blocks(pieces, f, first, rows, target, sems):
@@ -221,18 +237,22 @@
 
 def attend_kernel(count, ids, x0, x1, x2, x3, *refs):
     pieces = refs[:count]
-    qkv, lse, m0, m1, m2, m3, w_out, vec, held, mix, w, small, sems, small_sems = refs[count:]
+    qkv, lse, m0, m1, m2, m3, w_out, vec, held, mix, w, small, sems, small_sems, x_sems = refs[count:]
     fs = w.shape[0]
     n = w.shape[1]
     c = w.shape[2] // 3
     d = fs * n
     heads = c // HD
-    block = x0.shape[1]
+    nb, block, _ = x0.shape
     f = ids[1]
+    b = pl.program_id(0)
     out_copy = pltpu.make_async_copy(w, w_out, sems.at[fs])
 
     @pl.when(pl.program_id(0) == 0)
     def _():
+        for i in range(nb):
+            for copy in row_copies([x.at[i] for x in (x0, x1, x2, x3)], held.at[i], x_sems.at[i]):
+                copy.start()
         copies = load_blocks(pieces, f, 0, n, w, sems)
         copies += load_blocks(pieces, f, n, VEC, small, small_sems)
         run_copies(copies)
@@ -240,11 +260,11 @@
             vec[:, j * n : (j + 1) * n] = small[j, :, 0:n].astype(F32)
         out_copy.start()
 
-    for r, x in enumerate((x0, x1, x2, x3)):
-        held[r * block : (r + 1) * block, :] = x[0]
+    for copy in row_copies([x.at[b] for x in (x0, x1, x2, x3)], held.at[b], x_sems.at[b]):
+        copy.wait()
     cols = pl.ds(pl.multiple_of(ids[0] * c, c), c)
     for part in range(3):
-        acc = dot(held[...], w[:, :, part * c : (part + 1) * c].reshape(d, c))
+        acc = dot(held[b], w[:, :, part * c : (part + 1) * c].reshape(d, c))
         if part != 1:
             row = ROW_QB if part == 0 else ROW_VB
             acc = acc + vec[row : row + 1, cols]
@@ -290,17 +310,18 @@
         (ids, *blocks, *pieces),
         name="attend",
         grid=(nb,),
-        in_specs=[whole(pltpu.SMEM)] + [one((block, d))] * SEQ_N + [whole(ANY)] * len(pieces),
+        in_specs=[whole(pltpu.SMEM)] + [whole(HBM)] * (SEQ_N + len(pieces)),
         out_specs=(one((length, 3 * c)), one((heads, length)))
         + (one((block, c)),) * SEQ_N
         + (whole(ANY), fixed((VEC, d))),
         scratch=[
-            VMEM((length, d), BF16),
+            VMEM((nb, length, d), BF16),
             VMEM((c, length), F32),
             VMEM((fs, n, 3 * c), BF16),
             VMEM((fs, VEC, max(n, 128)), BF16),
             pltpu.SemaphoreType.DMA((fs + 1,)),
             pltpu.SemaphoreType.DMA((fs,)),
+            pltpu.SemaphoreType.DMA((nb, SEQ_N)),
         ],
         flops=2 * nb * length * (3 * c * d + 2 * length * c),
         trans=nb * heads * length * length,
@@ -427,7 +448,7 @@
         outs,
         args,
         name="out_project",
-        in_specs=[whole(pltpu.SMEM)] + [whole()] * SEQ_N + [whole(ANY)] * SEQ_N + [whole()] * 2,
+        in_specs=[whole(pltpu.SMEM)] + [whole()] * SEQ_N + [whole(HBM)] * SEQ_N + [whole()] * 2,
         scratch=[pltpu.SemaphoreType.DMA((SEQ_N, fs))],
         flops=2 * rows * d * d,
     )
@@ -466,7 +487,7 @@
     )
 
 
-def first_norm_kernel(ids, ffn_grad, p0, p1, p2, attn_sum, vec, mix, w,
+def first_norm_kernel(ids, ffn_grad, p0, p1, p2, attn_sum, vec, w,
                       attn_grad, sums, n0, n1, n2, n3, low_out, low, back):
     s = ids[0]
     c = n0.shape[1]
@@ -488,7 +509,7 @@
         n[...] = back[:, pl.ds(pl.multiple_of((s ^ r) * c, c), c)]
 
 
-def first_norm(ids, ffn_grad, parts, attn_sum, vec, mix, wo):
+def first_norm(ids, ffn_grad, parts, attn_sum, vec, wo):
     rows, d = ffn_grad.shape
     c = d // SEQ_N
     outs = (
@@ -496,7 +517,7 @@
         + (struct((rows, c), BF16),) * SEQ_N
         + (struct((rows, d), BF16),)
     )
-    args = (ids, ffn_grad, *parts, attn_sum, vec, mix, wo)
+    args = (ids, ffn_grad, *parts, attn_sum, vec, wo)
     return call(
         first_norm_kernel,
         outs,
@@ -539,37 +560,37 @@
 
 
 def ffn_kernel(ids, f0, f1, f2, f3, vec, packed, p0, p1, p2, p3, gelu, slope,
-               held, up, down, sems):
+               held, made, up, down, sems, row_sems):
+    rows, d = f0.shape
+    held[2 * rows : 3 * rows, :] = f0[...]
+    blocks = row_copies((f1, f3, None, f2), held, row_sems)
     n = up.shape[1]
     up_copies = [pltpu.make_async_copy(packed.at[:, pl.ds(0, n), :], up, sems.at[0])]
     down_copies = [pltpu.make_async_copy(packed.at[:, pl.ds(n, down.shape[1]), :], down, sems.at[1])]
-    for copy in up_copies + down_copies:
+    for copy in blocks + up_copies + down_copies:
         copy.start()
-    rows, d = f0.shape
     hidden = gelu.shape[1]
     half = 2 * rows
-    for i, f in enumerate((f1, f3, f0, f2)):
-        held[i * rows : (i + 1) * rows, :] = f[...]
     bias = vec[pl.ds(ROW_UB + ids[0], 1), :]
-    outs = (p1, p3, p0, p2)
-    for copy in up_copies:
+    for copy in blocks + up_copies + down_copies:
         copy.wait()
-    for part in range(2):
-        at = slice(part * half, (part + 1) * half)
+
+    def step(part, carry):
+        at = pl.ds(pl.multiple_of(part * half, half), half)
         for t in range(hidden // TILE):
             cols = slice(t * TILE, (t + 1) * TILE)
             u = dot(held[at, :], up[:, :, cols].reshape(d, TILE)) + bias[:, cols]
             g, b = gelu_and_slope(u)
             gelu[at, cols] = g.astype(BF16)
             slope[at, cols] = b.astype(BF16)
-        if part == 0:
-            for copy in down_copies:
-                copy.wait()
         for t in range(d // TILE):
             cols = slice(t * TILE, (t + 1) * TILE)
-            y = dot(gelu[at, :], down[:, :, cols].reshape(hidden, TILE)).astype(BF16)
-            outs[2 * part][:, cols] = y[0:rows]
-            outs[2 * part + 1][:, cols] = y[rows:]
+            made[at, cols] = dot(gelu[at, :], down[:, :, cols].reshape(hidden, TILE)).astype(BF16)
+        return carry
+
+    lax.fori_loop(0, 2, step, 0)
+    for i, out in enumerate((p1, p3, p0, p2)):
+        out[...] = made[i * rows : (i + 1) * rows, :]
 
 
 def weight_scratch(fs, d, hidden):
@@ -577,6 +598,7 @@
         VMEM((fs, d // fs, hidden), BF16),
         VMEM((fs, hidden // fs, d), BF16),
         pltpu.SemaphoreType.DMA((2,)),
+        pltpu.SemaphoreType.DMA((SEQ_N,)),
     ]
 
 
@@ -587,49 +609,49 @@
     return call(
         ffn_kernel,
         outs,
-        (ids, *blocks, vec, packed),
+        (ids, blocks[0], *(hbm(b) for b in blocks[1:]), vec, hbm(packed)),
         name="ffn",
-        in_specs=[whole(pltpu.SMEM)] + [whole()] * (SEQ_N + 1) + [whole(ANY)],
-        scratch=[VMEM((total, d), BF16)] + weight_scratch(fs, d, hidden),
+        in_specs=[whole(pltpu.SMEM), whole()] + [whole(HBM)] * 3 + [whole(), whole(HBM)],
+        scratch=[VMEM((total, d), BF16)] * 2 + weight_scratch(fs, d, hidden),
         flops=4 * total * d * hidden,
         trans=2 * total * hidden,
     )
 
 
 def ffn_back_kernel(ids, d0, d1, d2, d3, slope, packed, q0, q1, q2, q3, up_low, sums,
-                    held, up, down, sems):
+                    held, made, up, down, sems, row_sems):
+    rows, d = d0.shape
+    held[2 * rows : 3 * rows, :] = d0[...]
+    blocks = row_copies((d1, d3, None, d2), held, row_sems)
     n = up.shape[1]
     up_copies = [pltpu.make_async_copy(packed.at[:, pl.ds(0, n), :], up, sems.at[0])]
     down_copies = [pltpu.make_async_copy(packed.at[:, pl.ds(n, down.shape[1]), :], down, sems.at[1])]
-    for copy in down_copies + up_copies:
+    for copy in blocks + down_copies + up_copies:
         copy.start()
-    rows, d = d0.shape
     hidden = up_low.shape[1]
     half = 2 * rows
     per = TILE // up.shape[1]
-    for i, x in enumerate((d1, d3, d0, d2)):
-        held[i * rows : (i + 1) * rows, :] = x[...]
     sums[...] = jnp.zeros_like(sums)
-    outs = (q1, q3, q0, q2)
-    for copy in down_copies:
+    for copy in blocks + down_copies + up_copies:
         copy.wait()
-    for part in range(2):
-        at = slice(part * half, (part + 1) * half)
+
+    def step(part, carry):
+        at = pl.ds(pl.multiple_of(part * half, half), half)
         for t in range(hidden // TILE):
             cols = slice(t * TILE, (t + 1) * TILE)
             rhs = down[t * per : (t + 1) * per].reshape(TILE, d)
             u = (dot_nt(held[at, :], rhs) * slope[at, cols].astype(F32)).astype(BF16)
             up_low[at, cols] = u
             sums[0:1, cols] += jnp.sum(u.astype(F32), 0, keepdims=True)
-        if part == 0:
-            for copy in up_copies:
-                copy.wait()
         for t in range(d // TILE):
             cols = slice(t * TILE, (t + 1) * TILE)
             rhs = up[t * per : (t + 1) * per].reshape(TILE, hidden)
-            y = dot_nt(up_low[at, :], rhs).astype(BF16)
-            outs[2 * part][:, cols] = y[0:rows]
-            outs[2 * part + 1][:, cols] = y[rows:]
+            made[at, cols] = dot_nt(up_low[at, :], rhs).astype(BF16)
+        return carry
+
+    lax.fori_loop(0, 2, step, 0)
+    for i, out in enumerate((q1, q3, q0, q2)):
+        out[...] = made[i * rows : (i + 1) * rows, :]
 
 
 def ffn_back(ids, blocks, packed, slope, fs):
@@ -644,55 +666,90 @@
         outs,
         (ids, *blocks, slope, packed),
         name="ffn_back",
-        in_specs=[whole(pltpu.SMEM)] + [whole()] * (SEQ_N + 1) + [whole(ANY)],
-        scratch=[VMEM((total, d), BF16)] + weight_scratch(fs, d, hidden),
+        in_specs=[whole(pltpu.SMEM), whole()] + [whole(HBM)] * 3 + [whole(), whole(HBM)],
+        scratch=[VMEM((total, d), BF16)] * 2 + weight_scratch(fs, d, hidden),
         flops=4 * total * d * hidden,
     )
 
 
-def put_rows(f, tile, value, keep, send, turn):
+def down_grads_kernel(gelu, d0, d1, d2, d3, out, right, made, sems, out_sems):
+    rows, e = d0.shape
+    copies = row_copies((d1, d3, None, d2), right, sems)
+    for copy in copies:
+        copy.start()
+    right[2 * rows : 3 * rows, :] = d0[...]
+    for copy in copies:
+        copy.wait()
+    results = []
+    for t in range(gelu.shape[1] // TILE):
+        at = slice(t * TILE, (t + 1) * TILE)
+        made[at, :] = dot_tn(gelu[:, at], right[...]).astype(BF16)
+        at = pl.ds(t * TILE, TILE)
+        copy = pltpu.make_async_copy(made.at[at, :], out.at[at, :], out_sems.at[t])
+        copy.start()
+        results.append(copy)
+    for copy in results:
+        copy.wait()
+
+
+def down_grads(gelu, lows):
+    rows, d = lows[0].shape
+    total, hidden = gelu.shape
+    return call(
+        down_grads_kernel,
+        struct((hidden, d), BF16),
+        (gelu, *lows),
+        name="down_grads",
+        light=32,
+        in_specs=[whole()] * 2 + [whole(HBM)] * 3,
+        out_specs=whole(HBM),
+        scratch=[
+            VMEM((total, d), BF16),
+            VMEM((hidden, d), BF16),
+            pltpu.SemaphoreType.DMA((SEQ_N,)),
+            pltpu.SemaphoreType.DMA((hidden // TILE,)),
+        ],
+        flops=2 * total * d * hidden,
+    )
+
+
+def up_grads_kernel(ids, f0, f1, f2, f3, up_low, keep, send, left, turn, sems):
+    copies = row_copies((f1, f3, f0, f2), left, sems)
+    for copy in copies:
+        copy.start()
     n = keep.shape[1]
     per = TILE // (2 * n)
-    y = f & 1
-    turn[...] = value
-    for j in range(per):
-        z = tile * per + j
-        own = pl.multiple_of((2 * j + y) * n, n)
-        other = pl.multiple_of((2 * j + 1 - y) * n, n)
-        keep[z, 0:n, :] = turn[pl.ds(own, n), :]
-        send[z, 0:n, :] = turn[pl.ds(other, n), :]
-
-
-def outer_kernel(lefts, ids, *refs):
-    left, right = refs[:lefts], refs[lefts:5]
-    keep, send, held, turn = refs[5:]
-    many = left if lefts > 1 else right
-    rows = many[0].shape[0]
-    for i, x in enumerate(many):
-        held[i * rows : (i + 1) * rows, :] = x[...]
-    a, b = (held, right[0]) if lefts > 1 else (left[0], held)
-    for t in range(a.shape[1] // TILE):
-        value = dot_tn(a[:, t * TILE : (t + 1) * TILE], b[...]).astype(BF16)
-        put_rows(ids[1], t, value, keep, send, turn)
-
-
-def outer(ids, lefts, rights, fs, name):
-    rows = lefts[0].shape[0] if len(lefts) > 1 else rights[0].shape[0]
-    d, e = lefts[0].shape[1], rights[0].shape[1]
-    total = SEQ_N * rows
+    y = ids[1] & 1
+    for copy in copies:
+        copy.wait()
+    for t in range(left.shape[1] // TILE):
+        turn[...] = dot_tn(left[:, t * TILE : (t + 1) * TILE], up_low[...]).astype(BF16)
+        for j in range(per):
+            for out, side in ((keep, y), (send, 1 - y)):
+                out[t * per + j] = turn[pl.ds(pl.multiple_of((2 * j + side) * n, n), n), :]
+
+
+def up_grads(ids, firsts, up_low, fs):
+    rows, d = firsts[0].shape
+    total, hidden = up_low.shape
     return call(
-        functools.partial(outer_kernel, len(lefts)),
-        (struct((fs // 2, d // fs, e), BF16),) * 2,
-        (ids, *lefts, *rights),
-        name=name,
-        in_specs=[whole(pltpu.SMEM)] + [whole()] * 5,
-        scratch=[VMEM((total, d if len(lefts) > 1 else e), BF16), VMEM((TILE, e), BF16)],
-        flops=2 * total * d * e,
+        up_grads_kernel,
+        (struct((fs // 2, d // fs, hidden), BF16),) * 2,
+        (ids, *(hbm(f) for f in firsts), up_low),
+        name="up_grads",
+        light=32,
+        in_specs=[whole(pltpu.SMEM)] + [whole(HBM)] * SEQ_N + [whole()],
+        scratch=[VMEM((total, d), BF16), VMEM((TILE, hidden), BF16), pltpu.SemaphoreType.DMA((SEQ_N,))],
+        flops=2 * total * d * hidden,
     )
 
 
 def add(a, b):
     return (a.astype(F32) + b.astype(F32)).astype(BF16)
+
+
+def sum_z(terms):
+    return jnp.sum(turn_z(terms).astype(F32), 0).astype(BF16)
 
 
 def scatter_fsdp(keep, came, *others):
@@ -704,8 +761,7 @@
                 here = swap_z(here.astype(BF16), k, len(keep)).astype(F32)
             total = here if total is None else total + here
         return total.astype(BF16)
-    came = turn_z(after(add(keep, came), *others))
-    return jnp.sum(came.astype(F32), 0).astype(BF16)
+    return sum_z(after(add(keep, came), *others))
 
 
 def fill_vectors(s, vec, back_sums, first_sums, second_sums, up_sums):
@@ -724,19 +780,20 @@
 
 
 def qkvo_grads_kernel(ids, x0, x1, x2, x3, back, o0, o1, o2, s0, s1, s2, s3, *refs):
-    outs, (held, vec, turn) = refs[:-3], refs[-3:]
+    outs, (held, vec, turn, sems) = refs[:-4], refs[-4:]
     s, f = ids[0], ids[1]
     nb, block, d = x0.shape
-    length = SEQ_N * block
     e = back.shape[1]
     n = outs[0].shape[-2] - VEC
     zs = d // (2 * n)
     per = TILE // (2 * n)
     y = f & 1
-    for b in range(nb):
-        for r, x in enumerate((x0, x1, x2, x3)):
-            held[b * length + r * block : b * length + (r + 1) * block, :] = x[b]
+    copies = row_copies([x.at[b] for b in range(nb) for x in (x0, x1, x2, x3)], held, sems)
+    for copy in copies:
+        copy.start()
     fill_vectors(s, vec, s0, s1, s2, s3)
+    for copy in copies:
+        copy.wait()
     if len(outs) > 2:
         for k in (1, 2, 3, 0):
             z = (f >> 1) ^ k
@@ -782,10 +839,15 @@
     return call(
         qkvo_grads_kernel,
         outs,
-        (ids, *blocks, back, *out_parts, *sums),
+        (ids, *(hbm(b) for b in blocks), back, *out_parts, *sums),
         name="qkvo_grads",
-        in_specs=[whole(pltpu.SMEM)] + [whole()] * 12,
-        scratch=[VMEM((total, d), BF16), VMEM((VEC, d), F32), VMEM((TILE, wide), BF16)],
+        in_specs=[whole(pltpu.SMEM)] + [whole(HBM)] * SEQ_N + [whole()] * 8,
+        scratch=[
+            VMEM((total, d), BF16),
+            VMEM((VEC, d), F32),
+            VMEM((TILE, wide), BF16),
+            pltpu.SemaphoreType.DMA((nb * SEQ_N,)),
+        ],
         flops=2 * total * d * e,
     )
 
@@ -882,9 +944,9 @@
     with scope("tok"):
         tokens = gather_seq(tokens_in)
     with scope("wqkv"):
-        wqkv = gather_early(early, fs, tokens[2])
+        wqkv = gather_early(early, fs)
     with scope("ffnw"):
-        packed = lax.all_gather(after(packed, *wqkv[:5], tokens[2]), FSDP)
+        packed = lax.all_gather(after(packed, wqkv[0], *wqkv[3:5]), FSDP)
     with scope("wo"):
         n = d // fs
         wo = jnp.stack([p[..., :n, 3 * (d // SEQ_N) :] for p in wqkv])
@@ -903,56 +965,52 @@
     layer_out, ffn_grad, down_low, second_sums = second_norm(normed, parts, flat(cotangent), vec)
     with scope("low"):
         lows = gather_seq(down_low)
+    down_full = down_grads(gelu, lows)
+    with scope("gdown"):
+        down_grad = lax.psum_scatter(down_full, FSDP, scatter_dimension=0, tiled=True)
+    slope = after(slope, down_full)
     *parts, up_low, up_sums = ffn_back(ids, lows, packed, slope, fs)
     with scope("ffnback"):
         parts, onward = reduce_seq(parts)
-        gelu = after(gelu, onward)
-    turned = lambda blocks: (blocks[1], blocks[3], blocks[0], blocks[2])
-    keep_down, send_down = outer(ids, (gelu,), turned(lows), fs, "down_grads")
-    with scope("gdown"):
-        came_down = swap_y(send_down)
-    keep_up, send_up = outer(ids, turned(firsts), (up_low,), fs, "up_grads")
-    parts[0] = after(parts[0], keep_down, keep_up)
-    attn_grad, first_sums, *pieces, out_low = first_norm(ids, ffn_grad, parts, attn_sum, vec, mix, wo)
+    attn_grad, first_sums, *pieces, out_low = first_norm(ids, ffn_grad, parts, attn_sum, vec, wo)
     with scope("mixback"):
         grads = exchange_seq(pieces)
+    keep_up, send_up = up_grads(ids, firsts, after(up_low, grads[1]), fs)
+    with scope("gup"):
+        came_up = swap_y(send_up)
     out_parts = out_grads(ids, mix, out_low)
-    came_down = after(came_down, out_parts[0])
+    with scope("outs"):
+        out_parts, onward = reduce_seq(out_parts, *grads[2:])
+    grads[0] = after(grads[0], onward, keep_up)
+    back, back_sums, *parts = attend_back(qkv, lse, [deep(g) for g in grads], wqkv.reshape(d, -1))
     with scope("gup"):
-        came_up = swap_y(after(send_up, came_down))
-    with scope("gdown"):
-        down_grad = scatter_fsdp(keep_down, came_down)
-    with scope("outs"):
-        out_parts, onward = reduce_seq(out_parts)
-    grads[0] = after(grads[0], onward)
-    back, back_sums, *parts = attend_back(qkv, lse, [deep(g) for g in grads], wqkv.reshape(d, -1))
-    came_up = after(came_up, back)
-    with scope("gup"):
-        up_grad = scatter_fsdp(keep_up, came_up)
-    with scope("fdown"):
-        down_full = gather_seq(down_grad)
-    back = after(back, came_up, down_grad)
+        up_terms = add(keep_up, after(came_up, back))
+        up_grad = sum_z(up_terms)
+    back = after(back, up_terms)
     pieces = qkvo_grads(
         ids, tokens, back.reshape(-1, back.shape[-1]), out_parts,
         (back_sums, first_sums, second_sums, up_sums), fs,
     )
-    with scope("fup"):
-        up_full = gather_seq(up_grad)
-    up, down = finish_ffn(ids, s, up_full, down_full, fs)
     with scope("gqkvo"):
         half = len(pieces) // 2
         keep, send = pieces[:half], pieces[half:]
         if half == 1:
-            small = scatter_fsdp(keep[0], swap_y(send[0]), up_grad)
+            small = scatter_fsdp(keep[0], swap_y(send[0]))
         else:
             came = {k: swap_y(send[k]) for k in (1, 2, 3, 0)}
             small = scatter_fsdp(keep, came)
-        small = gather_seq(after(small, up))
     with scope("input"):
         terms, _ = reduce_seq([flat(p) for p in parts])
     input_grad = attn_grad + (
         terms[0].astype(F32) + terms[1].astype(F32) + terms[2].astype(F32)
     )
+    with scope("fdown"):
+        downs = gather_seq(after(down_grad, terms[2]))
+    with scope("fup"):
+        ups = gather_seq(after(up_grad, downs[2]))
+    up, down = finish_ffn(ids, s, ups, downs, fs)
+    with scope("small"):
+        small = gather_seq(small, up)
     four, vecs = finish_qkvo(ids, s, small)
     return (
         deep(layer_out), deep(input_grad), *four, up, down,

time: 342 us -> 300 us (0.88)
  waiting for transfers between devices: 139 us -> 112 us
  Pallas kernels: 94.8 us -> 69.2 us
  local copies, waits for them, and re-layouts: 10.2 us -> 19.6 us
  starting transfers between devices: 63.9 us -> 71.7 us
    pallas_call x15, Pallas kernels: 94.8 us -> 69.2 us  [call(): pl.pallas_call(kernel, out_shape=outs, in_specs=in_specs, out_specs=out_s...]
    ppermute x10 -> x9, waiting for transfers between devices: 38.6 us -> 21.1 us  [swap_y(): return lax.ppermute(value, 'y', [(0, 1), (1, 0)])]
    ppermute x6, waiting for transfers between devices: 33.1 us -> 21.8 us  [swap_z(): return lax.ppermute(value, 'z', [(i, i ^ k) for i in range(count)])]
    unnamed x119 -> x83, local copies, waits for them, and re-layouts: 10.2 us -> 19.6 us
    ppermute x39, starting transfers between devices: 41.3 us -> 48.2 us  [seq_swap(): return lax.ppermute(value, SEQ, [(i, i ^ k) for i in range(SEQ_N)])]
    all_to_all x2 -> x1, starting transfers between devices: 9.23 us -> 5.55 us  [turn_z(): return lax.all_to_all(value, 'z', split_axis=0, concat_axis=0, tiled=True)]
    ppermute x10 -> x9, starting transfers between devices: 7.18 us -> 10.8 us  [swap_y(): return lax.ppermute(value, 'y', [(0, 1), (1, 0)])]
  transfers between devices with their start and end apart: 58 -> 57, of which waited for: 26 -> 29; matrix products, arithmetic and copies ran while one was open for 4% -> 4% of each run, Pallas kernels for 18% -> 17%
where the time goes in v3:
time: 300 us; the launch traced here: 298 us
  waiting for transfers between devices  112 us (37%)
  starting transfers between devices  71.7 us (24%)
  Pallas kernels  69.2 us (23%)
  local copies, waits for them, and re-layouts  19.6 us (7%)
  between operations  14.5 us (5%)
  other arithmetic  11.1 us (4%)
    pallas_call x15, Pallas kernels, call(): pl.pallas_call(kernel, out_shape=outs, in_specs=in_specs, out_specs=out_s...  69.2 us
    ppermute x39, waiting for transfers between devices, seq_swap(): return lax.ppermute(value, SEQ, [(i, i ^ k) for i in range(SEQ_N)])  67.3 us
    ppermute x39, starting transfers between devices, seq_swap(): return lax.ppermute(value, SEQ, [(i, i ^ k) for i in range(SEQ_N)])  48.2 us
    ppermute x6, waiting for transfers between devices, swap_z(): return lax.ppermute(value, 'z', [(i, i ^ k) for i in range(count)])  21.8 us
    ppermute x9, waiting for transfers between devices, swap_y(): return lax.ppermute(value, 'y', [(0, 1), (1, 0)])  21.1 us
    unnamed x83, local copies, waits for them, and re-layouts  19.6 us
    ppermute x9, starting transfers between devices, swap_y(): return lax.ppermute(value, 'y', [(0, 1), (1, 0)])  10.8 us
    ppermute x6, starting transfers between devices, swap_z(): return lax.ppermute(value, 'z', [(i, i ^ k) for i in range(count)])  7.11 us
  transfers between devices with their start and end apart: 57, of which 29 were waited for; matrix products, arithmetic and copies ran while one was open for 4% of the time, Pallas kernels for 17%

profile of v3, /device:TPU:13, one launch (start us, length us, event | category | flops | bytes accessed | tf_op | source)
XLA Modules:
  0.0 298.1 jit_solution(4043469228343424261)
XLA Ops:
  7.8 2.6 early_pack.1.refs_0_
  12.0 2.6 late_pack.1
  14.7 3.9 %collective-permute-done.6.refs_4_ = bf16[144,1024]{1,0:T(8,128)(2,1)S(1)} collective-permute-done((bf16[144,1024]{1,0:T(8,128)(2,1)}, bf16[144,1024]{1,0:T(8,128)(2,1)S(1)}, u32[]{:S(2)}, u32[]{:S(2)}) %collective-permute-start.6) | collective-permute-done | bytes 294944 | tf_op jit(solution)/shard_map/wqkv/y/ppermute | solution.py:97
  18.6 6.7 %collective-permute-done.5.refs_3_ = bf16[144,1024]{1,0:T(8,128)(2,1)S(1)} collective-permute-done((bf16[144,1024]{1,0:T(8,128)(2,1)}, bf16[144,1024]{1,0:T(8,128)(2,1)S(1)}, u32[]{:S(2)}, u32[]{:S(2)}) %collective-permute-start.5) | collective-permute-done | bytes 294944 | tf_op jit(solution)/shard_map/wqkv/z3/ppermute | solution.py:102
  25.4 2.0 collective-permute-start.3
  28.6 2.7 collective-permute-start
  32.7 5.0 %collective-permute-done.4.refs_2_ = bf16[144,1024]{1,0:T(8,128)(2,1)S(1)} collective-permute-done((bf16[144,1024]{1,0:T(8,128)(2,1)S(1)}, bf16[144,1024]{1,0:T(8,128)(2,1)S(1)}, u32[]{:S(2)}, u32[]{:S(2)}) %collective-permute-start.4) | collective-permute-done | bytes 294944 | tf_op jit(solution)/shard_map/wqkv/z2/ppermute | solution.py:102
  37.7 2.3 collective-permute-start.8
  41.3 2.4 collective-permute-start.7
  43.8 7.7 %collective-permute-start.2 = (bf16[2,128,1024]{2,1,0:T(8,128)(2,1)S(1)}, bf16[2,128,1024]{2,1,0:T(8,128)(2,1)S(1)}, u32[]{:S(2)}, u32[]{:S(2)}) collective-permute-start(bf16[2,128,1024]{2,1,0:T(8,128)(2,1)S(1)} %collective-permute-done.1.x2), channel_id=1, source_target_pairs={{0,8},{8,0},{16,24},{24,16},{1,9},{9,1},{17,25},{25,17},{2,10},{10... | collective-permute-start | bytes 1572872 | tf_op jit(solution)/shard_map/tok/seq1/ppermute | solution.py:75
  51.5 4.0 %collective-permute-done.7.refs_5_ = bf16[144,1024]{1,0:T(8,128)(2,1)S(1)} collective-permute-done((bf16[144,1024]{1,0:T(8,128)(2,1)S(1)}, bf16[144,1024]{1,0:T(8,128)(2,1)S(1)}, u32[]{:S(2)}, u32[]{:S(2)}) %collective-permute-start.7) | collective-permute-done | bytes 294944 | tf_op jit(solution)/shard_map/wqkv/y/ppermute | solution.py:97
  55.7 4.1 %collective-permute-start.13 = (bf16[8,128,256]{2,1,0:T(8,128)(2,1)S(1)}, bf16[8,128,256]{2,1,0:T(8,128)(2,1)S(1)}, u32[]{:S(2)}, u32[]{:S(2)}) collective-permute-start(bf16[8,128,256]{2,1,0:T(8,128)(2,1)S(1)} %fusion.3.w0), channel_id=1, source_target_pairs={{0,8},{8,0},{16,24},{24,16},{1,9},{9,1},{17,25},{25,17},{2,10},{10... | collective-permute-start | bytes 1572872 | tf_op jit(solution)/shard_map/wo/seq1/ppermute | solution.py:75
  59.8 8.2 %attend.1 = (bf16[2,512,768]{2,1,0:T(8,128)(2,1)S(1)}, f32[2,4,512]{2,1,0:T(4,128)S(1)}, bf16[2,128,256]{2,1,0:T(8,128)(2,1)S(1)}, bf16[2,128,256]{2,1,0:T(8,128...) custom-call(s32[2]{0:T(128)S(1)} %copy-done.17, ...), custom_call_target="tpu_custom_call" | custom-call | flops 2147483648 | bytes 8208392 | tf_op jit(solution)/shard_map/attend/pallas_call | solution.py:56
  72.2 2.5 collective-permute-done.11.m2
  74.7 3.8 %collective-permute-done.12.m3 = bf16[256,256]{1,0:T(8,128)(2,1)S(1)} collective-permute-done((bf16[256,256]{1,0:T(8,128)(2,1)S(1)}, bf16[256,256]{1,0:T(8,128)(2,1)S(1)}, u32[]{:S(2)}, u32[]{:S(2)}) %collective-permute-start.12) | collective-permute-done | bytes 131104 | tf_op jit(solution)/shard_map/mix/seq3/ppermute | solution.py:75
  78.4 2.3 out_project.1
  84.4 11.9 %collective-permute-done.17.f2 = bf16[256,1024]{1,0:T(8,128)(2,1)S(1)} collective-permute-done((bf16[256,1024]{1,0:T(8,128)(2,1)S(1)}, bf16[256,1024]{1,0:T(8,128)(2,1)S(1)}, u32[]{:S(2)}, u32[]{:S(2)}) %collective-permute-start.17) | collective-permute-done | bytes 524320 | tf_op jit(solution)/shard_map/first/seq2/ppermute | solution.py:75
  98.4 1.9 all-gather.3.cloned.1.call-done
  101.3 9.6 %ffn.1 = (bf16[256,1024]{1,0:T(8,128)(2,1)S(1)}, bf16[256,1024]{1,0:T(8,128)(2,1)S(1)}, bf16[256,1024]{1,0:T(8,128)(2,1)S(1)}, bf16[256,1024]{1,0:T(8,128)(2,1)S...) custom-call(s32[2]{0:T(128)S(1)} %copy-done.17, bf16[256,1024]{1,0:T(8,128)(2,1)S(1)} %copy-done.6, ...), custom_call_target="tpu_custom_call" | custom-call | flops 4294967296 | bytes 12648456 | tf_op jit(solution)/shard_map/ffn/pallas_call | solution.py:56
  110.9 1.8 collective-permute-start.19
  116.4 11.8 %collective-permute-done.21.p2 = bf16[256,1024]{1,0:T(8,128)(2,1)S(1)} collective-permute-done((bf16[256,1024]{1,0:T(8,128)(2,1)S(1)}, bf16[256,1024]{1,0:T(8,128)(2,1)S(1)}, u32[]{:S(2)}, u32[]{:S(2)}) %collective-permute-start.21) | collective-permute-done | bytes 524320 | tf_op jit(solution)/shard_map/ffn/seq2/ppermute | solution.py:75
  128.3 1.7 second_norm.1
  133.3 10.1 %collective-permute-done.23.d2 = bf16[256,1024]{1,0:T(8,128)(2,1)S(1)} collective-permute-done((bf16[256,1024]{1,0:T(8,128)(2,1)S(1)}, bf16[256,1024]{1,0:T(8,128)(2,1)S(1)}, u32[]{:S(2)}, u32[]{:S(2)}) %collective-permute-start.23) | collective-permute-done | bytes 524320 | tf_op jit(solution)/shard_map/low/seq2/ppermute | solution.py:75
  143.4 1.9 collective-permute-start.24
  146.8 3.4 %down_grads.1 = bf16[1024,1024]{1,0:T(8,128)(2,1)} custom-call(bf16[1024,1024]{1,0:T(8,128)(2,1)S(1)} %get-tuple-element.121.gelu, bf16[256,1024]{1,0:T(8,128)(2,1)S(1)} %get-tuple-element.119.d0, bf16[256,1024]{1,0:T(8,128)(2,1)S(1)} %collective-permute-done.22.d1, bf16[256,1024]{1,0:T(8,128)(2,1)S(1)} %collective-permute-done.23.d2, ...), custom_call_target="tpu_custom_call" | custom-call | flops 67108864 | bytes 196608 | tf_op jit(solution)/shard_map/down_grads/pallas_call | solution.py:56
  155.0 2.2 copy-done.18
  157.2 1.6 copy-done.33
  158.8 6.3 %ffn_back.1 = (bf16[256,1024]{1,0:T(8,128)(2,1)S(1)}, bf16[256,1024]{1,0:T(8,128)(2,1)S(1)}, bf16[256,1024]{1,0:T(8,128)(2,1)S(1)}, bf16[256,1024]{1,0:T(8,128)(...) custom-call(s32[2]{0:T(128)S(1)} %copy-done.17, bf16[256,1024]{1,0:T(8,128)(2,1)S(1)} %copy-done.8, ...), custom_call_target="tpu_custom_call" | custom-call | flops 4294967296 | bytes 12615688 | tf_op jit(solution)/shard_map/ffn_back/pallas_call | solution.py:56
  169.3 12.0 %collective-permute-done.27.p2 = bf16[256,1024]{1,0:T(8,128)(2,1)S(1)} collective-permute-done((bf16[256,1024]{1,0:T(8,128)(2,1)S(1)}, bf16[256,1024]{1,0:T(8,128)(2,1)S(1)}, u32[]{:S(2)}, u32[]{:S(2)}) %collective-permute-start.27) | collective-permute-done | bytes 524320 | tf_op jit(solution)/shard_map/ffnback/seq2/ppermute | solution.py:75
  181.3 2.2 first_norm.1
  185.8 5.2 %up_grads.1 = (bf16[4,128,1024]{2,1,0:T(8,128)(2,1)S(1)}, bf16[4,128,1024]{2,1,0:T(8,128)(2,1)S(1)}) custom-call(s32[2]{0:T(128)S(1)} %copy-done.17, bf16[256,1024]{1,0:T(8,128)(2,1)} %copy-done.5, bf16[256,1024]{1,0:T(8,128)(2,1)} %copy-done.35, bf16[256,1024]{1,0:T(8,128)(2,1)} %copy-done.34, bf16[256,1024]{1,0:T(8,128)(2,1)} %collective-permute-done.18.f3, ...), custom_call_target="tpu_custom_call" | custom-call | flops 67108864 | bytes 196608 | tf_op jit(solution)/shard_map/up_grads/pallas_call | solution.py:56
  196.8 3.9 %collective-permute-done.31 = bf16[256,256]{1,0:T(8,128)(2,1)S(1)} collective-permute-done((bf16[256,256]{1,0:T(8,128)(2,1)S(1)}, bf16[256,256]{1,0:T(8,128)(2,1)S(1)}, u32[]{:S(2)}, u32[]{:S(2)}) %collective-permute-start.31) | collective-permute-done | bytes 131104 | tf_op jit(solution)/shard_map/mixback/seq3/ppermute | solution.py:75
  201.9 13.0 %attend_back.1 = (bf16[2,512,768]{2,1,0:T(8,128)(2,1)S(1)}, f32[8,768]{1,0:T(8,128)S(1)}, bf16[2,128,1024]{2,1,0:T(8,128)(2,1)S(1)}, bf16[2,128,1024]{2,1,0:T(8,...) custom-call(bf16[2,512,768]{2,1,0:T(8,128)(2,1)S(1)} %copy-done.31, ...), custom_call_target="tpu_custom_call" | custom-call | flops 2952790016 | bytes 7380992 | tf_op jit(solution)/shard_map/attend_back/pallas_call | solution.py:56
  216.8 2.3 collective-permute-done.35
  220.5 5.6 %all-to-all-start = ((bf16[4,128,1024]{2,1,0:T(8,128)(2,1)}), bf16[4,128,1024]{2,1,0:T(8,128)(2,1)}, u32[]{:S(2)}, u32[]{:S(2)}) async-start(bf16[4,128,1024]{2,1,0:T(8,128)(2,1)} %add_convert_fusion), calls=%async_computation | async-start | bytes 2097152 | tf_op jit(solution)/shard_map/gup/z/all_to_all | solution.py:107
  228.5 5.9 %qkvo_grads.1 = (bf16[144,1024]{1,0:T(8,128)(2,1)S(1)}, bf16[144,1024]{1,0:T(8,128)(2,1)S(1)}, bf16[144,1024]{1,0:T(8,128)(2,1)S(1)}, bf16[144,1024]{1,0:T(8,128...) custom-call(s32[2]{0:T(128)S(1)} %copy-done.17, ...), custom_call_target="tpu_custom_call" | custom-call | flops 1610612736 | bytes 7725064 | tf_op jit(solution)/shard_map/qkvo_grads/pallas_call | solution.py:56
  239.9 2.3 collective-permute-done.38
  243.3 5.1 %collective-permute-done.40 = bf16[144,1024]{1,0:T(8,128)(2,1)S(1)} collective-permute-done((bf16[144,1024]{1,0:T(8,128)(2,1)S(1)}, bf16[144,1024]{1,0:T(8,128)(2,1)S(1)}, u32[]{:S(2)}, u32[]{:S(2)}) %collective-permute-start.40) | collective-permute-done | bytes 294944 | tf_op jit(solution)/shard_map/gqkvo/y/ppermute | solution.py:97
  249.2 2.2 collective-permute-start.41
  251.4 3.3 %collective-permute-done.42 = bf16[144,1024]{1,0:T(8,128)(2,1)S(1)} collective-permute-done((bf16[144,1024]{1,0:T(8,128)(2,1)S(1)}, bf16[144,1024]{1,0:T(8,128)(2,1)S(1)}, u32[]{:S(2)}, u32[]{:S(2)}) %collective-permute-start.42) | collective-permute-done | bytes 294944 | tf_op jit(solution)/shard_map/gqkvo/y/ppermute | solution.py:97
  259.3 3.2 %collective-permute-done.47.refs_6_ = bf16[128,1024]{1,0:T(8,128)(2,1)S(1)} collective-permute-done((bf16[128,1024]{1,0:T(8,128)(2,1)}, bf16[128,1024]{1,0:T(8,128)(2,1)S(1)}, u32[]{:S(2)}, u32[]{:S(2)}) %collective-permute-start.47) | collective-permute-done | bytes 262176 | tf_op jit(solution)/shard_map/fdown/seq2/ppermute | solution.py:75
  262.5 4.3 %collective-permute-start.33 = (bf16[256,1024]{1,0:T(8,128)(2,1)}, bf16[256,1024]{1,0:T(8,128)(2,1)S(1)}, u32[]{:S(2)}, u32[]{:S(2)}) collective-permute-start(bf16[256,1024]{1,0:T(8,128)(2,1)} %bitcast.24), channel_id=1, source_target_pairs={{0,8},{8,0},{16,24},{24,16},{1,9},{9,1},{17,25},{25,17},{2,10},{10... | collective-permute-start | bytes 1572872 | tf_op jit(solution)/shard_map/input/seq1/ppermute | solution.py:75
  268.1 2.5 collective-permute-done.41
  270.6 6.3 %collective-permute-done.43 = bf16[144,1024]{1,0:T(8,128)(2,1)} collective-permute-done((bf16[144,1024]{1,0:T(8,128)(2,1)}, bf16[144,1024]{1,0:T(8,128)(2,1)}, u32[]{:S(2)}, u32[]{:S(2)}) %collective-permute-start.43) | collective-permute-done | bytes 294944 | tf_op jit(solution)/shard_map/gqkvo/z3/ppermute | solution.py:102
  279.5 1.6 collective-permute-start.48
  283.0 3.0 finish_ffn.1
  286.0 1.9 collective-permute-start.53
  289.3 2.0 finish_qkvo.1
  (179 shorter events, 68.8 us)
Async XLA Ops:
  7.2 93.1 %all-gather.3.cloned.1.call-start = ((), (), s32[]{:S(2)}) async-start(), calls=%async_computation.3 | async-start | bytes 4718592 | tf_op jit(solution)/shard_map/ffnw/all_gather | solution.py:949
  10.4 8.2 %collective-permute-start.6 = (bf16[144,1024]{1,0:T(8,128)(2,1)}, bf16[144,1024]{1,0:T(8,128)(2,1)S(1)}, u32[]{:S(2)}, u32[]{:S(2)}) collective-permute-start(bf16[144,1024]{1,0:T(8,128)(2,1)} %early_pack.1.refs_0_), channel_id=1, source_target_pairs={{0,1},{1,0},{2,3},{3,2},{4,5},{5,4},{6,7},{7,6},{8,9},{9,8},{10,11... | collective-permute-start | bytes 884744 | tf_op jit(solution)/shard_map/wqkv/y/ppermute | solution.py:97
  10.7 14.5 %collective-permute-start.5 = (bf16[144,1024]{1,0:T(8,128)(2,1)}, bf16[144,1024]{1,0:T(8,128)(2,1)S(1)}, u32[]{:S(2)}, u32[]{:S(2)}) collective-permute-start(bf16[144,1024]{1,0:T(8,128)(2,1)} %early_pack.1.refs_0_), channel_id=1, source_target_pairs={{0,6},{2,4},{4,2},{6,0},{1,7},{3,5},{5,3},{7,1},{8,14},{10,12},{12... | collective-permute-start | bytes 884744 | tf_op jit(solution)/shard_map/wqkv/z3/ppermute | solution.py:102
  25.3 231.5 %reduce-scatter.2.cloned.1.call-start = ((), (), s32[]{:S(2)}) async-start(), calls=%async_computation.2 | async-start | bytes 2359296 | tf_op jit(solution)/shard_map/gdown/reduce_scatter | solution.py:970
  25.3 12.4 %collective-permute-start.4 = (bf16[144,1024]{1,0:T(8,128)(2,1)S(1)}, bf16[144,1024]{1,0:T(8,128)(2,1)S(1)}, u32[]{:S(2)}, u32[]{:S(2)}) collective-permute-start(bf16[144,1024]{1,0:T(8,128)(2,1)S(1)} %copy-done.15), channel_id=1, source_target_pairs={{0,4},{2,6},{4,0},{6,2},{1,5},{3,7},{5,1},{7,3},{8,12},{10,14},{12... | collective-permute-start | bytes 884744 | tf_op jit(solution)/shard_map/wqkv/z2/ppermute | solution.py:102
  25.4 15.9 %collective-permute-start.3 = (bf16[144,1024]{1,0:T(8,128)(2,1)S(1)}, bf16[144,1024]{1,0:T(8,128)(2,1)S(1)}, u32[]{:S(2)}, u32[]{:S(2)}) collective-permute-start(bf16[144,1024]{1,0:T(8,128)(2,1)S(1)} %copy-done.15), channel_id=1, source_target_pairs={{0,2},{2,0},{4,6},{6,4},{1,3},{3,1},{5,7},{7,5},{8,10},{10,8},{12,... | collective-permute-start | bytes 884744 | tf_op jit(solution)/shard_map/wqkv/z1/ppermute | solution.py:102
  27.4 16.3 %collective-permute-start.1 = (bf16[2,128,1024]{2,1,0:T(8,128)(2,1)S(1)}, bf16[2,128,1024]{2,1,0:T(8,128)(2,1)S(1)}, u32[]{:S(2)}, u32[]{:S(2)}) collective-permute-start(bf16[2,128,1024]{2,1,0:T(8,128)(2,1)S(1)} %copy-done.13), channel_id=1, source_target_pairs={{0,16},{8,24},{16,0},{24,8},{1,17},{9,25},{17,1},{25,9},{2,18},{10... | collective-permute-start | bytes 1572872 | tf_op jit(solution)/shard_map/tok/seq2/ppermute | solution.py:75
  28.6 31.2 %collective-permute-start = (bf16[2,128,1024]{2,1,0:T(8,128)(2,1)S(1)}, bf16[2,128,1024]{2,1,0:T(8,128)(2,1)S(1)}, u32[]{:S(2)}, u32[]{:S(2)}) collective-permute-start(bf16[2,128,1024]{2,1,0:T(8,128)(2,1)S(1)} %copy-done.13), channel_id=1, source_target_pairs={{0,8},{8,0},{16,24},{24,16},{1,9},{9,1},{17,25},{25,17},{2,10},{10... | collective-permute-start | bytes 1572872 | tf_op jit(solution)/shard_map/tok/seq1/ppermute | solution.py:75
  31.4 24.2 %collective-permute-start.9 = (bf16[144,1024]{1,0:T(8,128)(2,1)S(1)}, bf16[144,1024]{1,0:T(8,128)(2,1)S(1)}, u32[]{:S(2)}, u32[]{:S(2)}) collective-permute-start(bf16[144,1024]{1,0:T(8,128)(2,1)S(1)} %collective-permute-done.5.refs_3_), channel_id=1, source_target_pairs={{0,1},{1,0},{2,3},{3,2},{4,5},{5,4},{6,7},{7,6},{8,9},{9,8},{10,11... | collective-permute-start | bytes 884744 | tf_op jit(solution)/shard_map/wqkv/y/ppermute | solution.py:97
  37.7 17.9 %collective-permute-start.8 = (bf16[144,1024]{1,0:T(8,128)(2,1)S(1)}, bf16[144,1024]{1,0:T(8,128)(2,1)S(1)}, u32[]{:S(2)}, u32[]{:S(2)}) collective-permute-start(bf16[144,1024]{1,0:T(8,128)(2,1)S(1)} %collective-permute-done.4.refs_2_), channel_id=1, source_target_pairs={{0,1},{1,0},{2,3},{3,2},{4,5},{5,4},{6,7},{7,6},{8,9},{9,8},{10,11... | collective-permute-start | bytes 884744 | tf_op jit(solution)/shard_map/wqkv/y/ppermute | solution.py:97
  41.3 14.3 %collective-permute-start.7 = (bf16[144,1024]{1,0:T(8,128)(2,1)S(1)}, bf16[144,1024]{1,0:T(8,128)(2,1)S(1)}, u32[]{:S(2)}, u32[]{:S(2)}) collective-permute-start(bf16[144,1024]{1,0:T(8,128)(2,1)S(1)} %collective-permute-done.3.refs_1_), channel_id=1, source_target_pairs={{0,1},{1,0},{2,3},{3,2},{4,5},{5,4},{6,7},{7,6},{8,9},{9,8},{10,11... | collective-permute-start | bytes 884744 | tf_op jit(solution)/shard_map/wqkv/y/ppermute | solution.py:97
  43.8 16.0 %collective-permute-start.2 = (bf16[2,128,1024]{2,1,0:T(8,128)(2,1)S(1)}, bf16[2,128,1024]{2,1,0:T(8,128)(2,1)S(1)}, u32[]{:S(2)}, u32[]{:S(2)}) collective-permute-start(bf16[2,128,1024]{2,1,0:T(8,128)(2,1)S(1)} %collective-permute-done.1.x2), channel_id=1, source_target_pairs={{0,8},{8,0},{16,24},{24,16},{1,9},{9,1},{17,25},{25,17},{2,10},{10... | collective-permute-start | bytes 1572872 | tf_op jit(solution)/shard_map/tok/seq1/ppermute | solution.py:75
  55.6 13.7 %collective-permute-start.14 = (bf16[8,128,256]{2,1,0:T(8,128)(2,1)S(1)}, bf16[8,128,256]{2,1,0:T(8,128)(2,1)S(1)}, u32[]{:S(2)}, u32[]{:S(2)}) collective-permute-start(bf16[8,128,256]{2,1,0:T(8,128)(2,1)S(1)} %fusion.3.w0), channel_id=1, source_target_pairs={{0,16},{8,24},{16,0},{24,8},{1,17},{9,25},{17,1},{25,9},{2,18},{10... | collective-permute-start | bytes 1572872 | tf_op jit(solution)/shard_map/wo/seq2/ppermute | solution.py:75
  55.7 16.5 %collective-permute-start.13 = (bf16[8,128,256]{2,1,0:T(8,128)(2,1)S(1)}, bf16[8,128,256]{2,1,0:T(8,128)(2,1)S(1)}, u32[]{:S(2)}, u32[]{:S(2)}) collective-permute-start(bf16[8,128,256]{2,1,0:T(8,128)(2,1)S(1)} %fusion.3.w0), channel_id=1, source_target_pairs={{0,8},{8,0},{16,24},{24,16},{1,9},{9,1},{17,25},{25,17},{2,10},{10... | collective-permute-start | bytes 1572872 | tf_op jit(solution)/shard_map/wo/seq1/ppermute | solution.py:75
  69.3 9.1 %collective-permute-start.15 = (bf16[8,128,256]{2,1,0:T(8,128)(2,1)S(1)}, bf16[8,128,256]{2,1,0:T(8,128)(2,1)S(1)}, u32[]{:S(2)}, u32[]{:S(2)}) collective-permute-start(bf16[8,128,256]{2,1,0:T(8,128)(2,1)S(1)} %collective-permute-done.14.w2), channel_id=1, source_target_pairs={{0,8},{8,0},{16,24},{24,16},{1,9},{9,1},{17,25},{25,17},{2,10},{10... | collective-permute-start | bytes 1572872 | tf_op jit(solution)/shard_map/wo/seq1/ppermute | solution.py:75
  70.0 4.7 %collective-permute-start.11 = (bf16[256,256]{1,0:T(8,128)(2,1)S(1)}, bf16[256,256]{1,0:T(8,128)(2,1)S(1)}, u32[]{:S(2)}, u32[]{:S(2)}) collective-permute-start(bf16[256,256]{1,0:T(8,128)(2,1)S(1)} %bitcast.65), channel_id=1, source_target_pairs={{0,16},{8,24},{16,0},{24,8},{1,17},{9,25},{17,1},{25,9},{2,18},{10... | collective-permute-start | bytes 393224 | tf_op jit(solution)/shard_map/mix/seq2/ppermute | solution.py:75
  71.0 7.4 %collective-permute-start.12 = (bf16[256,256]{1,0:T(8,128)(2,1)S(1)}, bf16[256,256]{1,0:T(8,128)(2,1)S(1)}, u32[]{:S(2)}, u32[]{:S(2)}) collective-permute-start(bf16[256,256]{1,0:T(8,128)(2,1)S(1)} %bitcast.64), channel_id=1, source_target_pairs={{0,24},{8,16},{16,8},{24,0},{1,25},{9,17},{17,9},{25,1},{2,26},{10... | collective-permute-start | bytes 393224 | tf_op jit(solution)/shard_map/mix/seq3/ppermute | solution.py:75
  82.5 13.8 %collective-permute-start.17 = (bf16[256,1024]{1,0:T(8,128)(2,1)S(1)}, bf16[256,1024]{1,0:T(8,128)(2,1)S(1)}, u32[]{:S(2)}, u32[]{:S(2)}) collective-permute-start(bf16[256,1024]{1,0:T(8,128)(2,1)S(1)} %get-tuple-element.110.f0), channel_id=1, source_target_pairs={{0,16},{8,24},{16,0},{24,8},{1,17},{9,25},{17,1},{25,9},{2,18},{10... | collective-permute-start | bytes 1572872 | tf_op jit(solution)/shard_map/first/seq2/ppermute | solution.py:75
  83.5 12.9 %collective-permute-start.16 = (bf16[256,1024]{1,0:T(8,128)(2,1)S(1)}, bf16[256,1024]{1,0:T(8,128)(2,1)S(1)}, u32[]{:S(2)}, u32[]{:S(2)}) collective-permute-start(bf16[256,1024]{1,0:T(8,128)(2,1)S(1)} %get-tuple-element.110.f0), channel_id=1, source_target_pairs={{0,8},{8,0},{16,24},{24,16},{1,9},{9,1},{17,25},{25,17},{2,10},{10... | collective-permute-start | bytes 1572872 | tf_op jit(solution)/shard_map/first/seq1/ppermute | solution.py:75
  110.9 3.3 %collective-permute-start.19 = (bf16[256,1024]{1,0:T(8,128)(2,1)S(1)}, bf16[256,1024]{1,0:T(8,128)(2,1)S(1)}, u32[]{:S(2)}, u32[]{:S(2)}) collective-permute-start(bf16[256,1024]{1,0:T(8,128)(2,1)S(1)} %get-tuple-element.115), channel_id=1, source_target_pairs={{0,8},{8,0},{16,24},{24,16},{1,9},{9,1},{17,25},{25,17},{2,10},{10... | collective-permute-start | bytes 1572872 | tf_op jit(solution)/shard_map/ffn/seq1/ppermute | solution.py:75
  114.9 13.4 %collective-permute-start.21 = (bf16[256,1024]{1,0:T(8,128)(2,1)S(1)}, bf16[256,1024]{1,0:T(8,128)(2,1)S(1)}, u32[]{:S(2)}, u32[]{:S(2)}) collective-permute-start(bf16[256,1024]{1,0:T(8,128)(2,1)S(1)} %add_convert_fusion.3), channel_id=1, source_target_pairs={{0,16},{8,24},{16,0},{24,8},{1,17},{9,25},{17,1},{25,9},{2,18},{10... | collective-permute-start | bytes 1572872 | tf_op jit(solution)/shard_map/ffn/seq2/ppermute | solution.py:75
  130.9 12.5 %collective-permute-start.23 = (bf16[256,1024]{1,0:T(8,128)(2,1)S(1)}, bf16[256,1024]{1,0:T(8,128)(2,1)S(1)}, u32[]{:S(2)}, u32[]{:S(2)}) collective-permute-start(bf16[256,1024]{1,0:T(8,128)(2,1)S(1)} %get-tuple-element.119.d0), channel_id=1, source_target_pairs={{0,16},{8,24},{16,0},{24,8},{1,17},{9,25},{17,1},{25,9},{2,18},{10... | collective-permute-start | bytes 1572872 | tf_op jit(solution)/shard_map/low/seq2/ppermute | solution.py:75
  132.1 13.2 %collective-permute-start.22 = (bf16[256,1024]{1,0:T(8,128)(2,1)S(1)}, bf16[256,1024]{1,0:T(8,128)(2,1)S(1)}, u32[]{:S(2)}, u32[]{:S(2)}) collective-permute-start(bf16[256,1024]{1,0:T(8,128)(2,1)S(1)} %get-tuple-element.119.d0), channel_id=1, source_target_pairs={{0,8},{8,0},{16,24},{24,16},{1,9},{9,1},{17,25},{25,17},{2,10},{10... | collective-permute-start | bytes 1572872 | tf_op jit(solution)/shard_map/low/seq1/ppermute | solution.py:75
  143.4 3.4 %collective-permute-start.24 = (bf16[256,1024]{1,0:T(8,128)(2,1)S(1)}, bf16[256,1024]{1,0:T(8,128)(2,1)S(1)}, u32[]{:S(2)}, u32[]{:S(2)}) collective-permute-start(bf16[256,1024]{1,0:T(8,128)(2,1)S(1)} %collective-permute-done.23.d2), channel_id=1, source_target_pairs={{0,8},{8,0},{16,24},{24,16},{1,9},{9,1},{17,25},{25,17},{2,10},{10... | collective-permute-start | bytes 1572872 | tf_op jit(solution)/shard_map/low/seq1/ppermute | solution.py:75
  167.8 13.5 %collective-permute-start.27 = (bf16[256,1024]{1,0:T(8,128)(2,1)S(1)}, bf16[256,1024]{1,0:T(8,128)(2,1)S(1)}, u32[]{:S(2)}, u32[]{:S(2)}) collective-permute-start(bf16[256,1024]{1,0:T(8,128)(2,1)S(1)} %add_convert_fusion.2), channel_id=1, source_target_pairs={{0,16},{8,24},{16,0},{24,8},{1,17},{9,25},{17,1},{25,9},{2,18},{10... | collective-permute-start | bytes 1572872 | tf_op jit(solution)/shard_map/ffnback/seq2/ppermute | solution.py:75
  185.7 8.9 %collective-permute-start.28 = (bf16[1024,256]{1,0:T(8,128)(2,1)S(1)}, bf16[1024,256]{1,0:T(8,128)(2,1)S(1)}, u32[]{:S(2)}, u32[]{:S(2)}) collective-permute-start(bf16[1024,256]{1,0:T(8,128)(2,1)S(1)} %get-tuple-element.137), channel_id=1, source_target_pairs={{0,8},{8,0},{16,24},{24,16},{1,9},{9,1},{17,25},{25,17},{2,10},{10... | collective-permute-start | bytes 1572872 | tf_op jit(solution)/shard_map/outs/seq1/ppermute | solution.py:75
  190.9 28.2 %collective-permute-start.35 = (bf16[4,128,1024]{2,1,0:T(8,128)(2,1)S(1)}, bf16[4,128,1024]{2,1,0:T(8,128)(2,1)S(1)}, u32[]{:S(2)}, u32[]{:S(2)}) collective-permute-start(bf16[4,128,1024]{2,1,0:T(8,128)(2,1)S(1)} %get-tuple-element.152), channel_id=1, source_target_pairs={{0,1},{1,0},{2,3},{3,2},{4,5},{5,4},{6,7},{7,6},{8,9},{9,8},{10,11... | collective-permute-start | bytes 3145736 | tf_op jit(solution)/shard_map/gup/y/ppermute | solution.py:97
  192.3 4.4 %collective-permute-start.30 = (bf16[256,256]{1,0:T(8,128)(2,1)S(1)}, bf16[256,256]{1,0:T(8,128)(2,1)S(1)}, u32[]{:S(2)}, u32[]{:S(2)}) collective-permute-start(bf16[256,256]{1,0:T(8,128)(2,1)S(1)} %get-tuple-element.143), channel_id=1, source_target_pairs={{0,16},{8,24},{16,0},{24,8},{1,17},{9,25},{17,1},{25,9},{2,18},{10... | collective-permute-start | bytes 393224 | tf_op jit(solution)/shard_map/mixback/seq2/ppermute | solution.py:75
  193.5 7.1 %collective-permute-start.31 = (bf16[256,256]{1,0:T(8,128)(2,1)S(1)}, bf16[256,256]{1,0:T(8,128)(2,1)S(1)}, u32[]{:S(2)}, u32[]{:S(2)}) collective-permute-start(bf16[256,256]{1,0:T(8,128)(2,1)S(1)} %get-tuple-element.144), channel_id=1, source_target_pairs={{0,24},{8,16},{16,8},{24,0},{1,25},{9,17},{17,9},{25,1},{2,26},{10... | collective-permute-start | bytes 393224 | tf_op jit(solution)/shard_map/mixback/seq3/ppermute | solution.py:75
  200.7 25.4 %collective-permute-start.36 = (bf16[1024,256]{1,0:T(8,128)(2,1)S(1)}, bf16[1024,256]{1,0:T(8,128)(2,1)}, u32[]{:S(2)}, u32[]{:S(2)}) collective-permute-start(bf16[1024,256]{1,0:T(8,128)(2,1)S(1)} %get-tuple-element.157), channel_id=1, source_target_pairs={{0,8},{8,0},{16,24},{24,16},{1,9},{9,1},{17,25},{25,17},{2,10},{10... | collective-permute-start | bytes 1572872 | tf_op jit(solution)/shard_map/outs/seq1/ppermute | solution.py:75
  200.7 25.4 %collective-permute-start.37 = (bf16[1024,256]{1,0:T(8,128)(2,1)}, bf16[1024,256]{1,0:T(8,128)(2,1)}, u32[]{:S(2)}, u32[]{:S(2)}) collective-permute-start(bf16[1024,256]{1,0:T(8,128)(2,1)} %add_convert_fusion.1), channel_id=1, source_target_pairs={{0,16},{8,24},{16,0},{24,8},{1,17},{9,25},{17,1},{25,9},{2,18},{10... | collective-permute-start | bytes 1572872 | tf_op jit(solution)/shard_map/outs/seq2/ppermute | solution.py:75
  216.0 19.9 %collective-permute-start.32 = (bf16[256,1024]{1,0:T(8,128)(2,1)}, bf16[256,1024]{1,0:T(8,128)(2,1)}, u32[]{:S(2)}, u32[]{:S(2)}) collective-permute-start(bf16[256,1024]{1,0:T(8,128)(2,1)} %bitcast.26), channel_id=1, source_target_pairs={{0,8},{8,0},{16,24},{24,16},{1,9},{9,1},{17,25},{25,17},{2,10},{10... | collective-permute-start | bytes 1572872 | tf_op jit(solution)/shard_map/input/seq1/ppermute | solution.py:75
  220.5 37.4 %all-to-all-start = ((bf16[4,128,1024]{2,1,0:T(8,128)(2,1)}), bf16[4,128,1024]{2,1,0:T(8,128)(2,1)}, u32[]{:S(2)}, u32[]{:S(2)}) async-start(bf16[4,128,1024]{2,1,0:T(8,128)(2,1)} %add_convert_fusion), calls=%async_computation | async-start | bytes 2097152 | tf_op jit(solution)/shard_map/gup/z/all_to_all | solution.py:107
  234.4 7.8 %collective-permute-start.38 = (bf16[144,1024]{1,0:T(8,128)(2,1)S(1)}, bf16[144,1024]{1,0:T(8,128)(2,1)S(1)}, u32[]{:S(2)}, u32[]{:S(2)}) collective-permute-start(bf16[144,1024]{1,0:T(8,128)(2,1)S(1)} %get-tuple-element.164), channel_id=1, source_target_pairs={{0,1},{1,0},{2,3},{3,2},{4,5},{5,4},{6,7},{7,6},{8,9},{9,8},{10,11... | collective-permute-start | bytes 884744 | tf_op jit(solution)/shard_map/gqkvo/y/ppermute | solution.py:97
  234.7 13.8 %collective-permute-start.40 = (bf16[144,1024]{1,0:T(8,128)(2,1)S(1)}, bf16[144,1024]{1,0:T(8,128)(2,1)S(1)}, u32[]{:S(2)}, u32[]{:S(2)}) collective-permute-start(bf16[144,1024]{1,0:T(8,128)(2,1)S(1)} %get-tuple-element.166), channel_id=1, source_target_pairs={{0,1},{1,0},{2,3},{3,2},{4,5},{5,4},{6,7},{7,6},{8,9},{9,8},{10,11... | collective-permute-start | bytes 884744 | tf_op jit(solution)/shard_map/gqkvo/y/ppermute | solution.py:97
  237.2 19.6 %collective-permute-start.34 = (bf16[256,1024]{1,0:T(8,128)(2,1)S(1)}, bf16[256,1024]{1,0:T(8,128)(2,1)S(1)}, u32[]{:S(2)}, u32[]{:S(2)}) collective-permute-start(bf16[256,1024]{1,0:T(8,128)(2,1)S(1)} %fusion), channel_id=1, source_target_pairs={{0,16},{8,24},{16,0},{24,8},{1,17},{9,25},{17,1},{25,9},{2,18},{10... | collective-permute-start | bytes 1572872 | tf_op jit(solution)/shard_map/input/seq2/ppermute | solution.py:75
  238.4 16.4 %collective-permute-start.42 = (bf16[144,1024]{1,0:T(8,128)(2,1)S(1)}, bf16[144,1024]{1,0:T(8,128)(2,1)S(1)}, u32[]{:S(2)}, u32[]{:S(2)}) collective-permute-start(bf16[144,1024]{1,0:T(8,128)(2,1)S(1)} %get-tuple-element.168), channel_id=1, source_target_pairs={{0,1},{1,0},{2,3},{3,2},{4,5},{5,4},{6,7},{7,6},{8,9},{9,8},{10,11... | collective-permute-start | bytes 884744 | tf_op jit(solution)/shard_map/gqkvo/y/ppermute | solution.py:97
  238.5 28.3 %collective-permute-start.44 = (bf16[144,1024]{1,0:T(8,128)(2,1)}, bf16[144,1024]{1,0:T(8,128)(2,1)}, u32[]{:S(2)}, u32[]{:S(2)}) collective-permute-start(bf16[144,1024]{1,0:T(8,128)(2,1)} %get-tuple-element.170), channel_id=1, source_target_pairs={{0,1},{1,0},{2,3},{3,2},{4,5},{5,4},{6,7},{7,6},{8,9},{9,8},{10,11... | collective-permute-start | bytes 884744 | tf_op jit(solution)/shard_map/gqkvo/y/ppermute | solution.py:97
  243.0 23.8 %collective-permute-start.39 = (bf16[144,1024]{1,0:T(8,128)(2,1)}, bf16[144,1024]{1,0:T(8,128)(2,1)}, u32[]{:S(2)}, u32[]{:S(2)}) collective-permute-start(bf16[144,1024]{1,0:T(8,128)(2,1)} %add_convert_fusion.7), channel_id=1, source_target_pairs={{0,2},{2,0},{4,6},{6,4},{1,3},{3,1},{5,7},{7,5},{8,10},{10,8},{12,... | collective-permute-start | bytes 884744 | tf_op jit(solution)/shard_map/gqkvo/z1/ppermute | solution.py:102
  249.2 21.4 %collective-permute-start.41 = (bf16[144,1024]{1,0:T(8,128)(2,1)}, bf16[144,1024]{1,0:T(8,128)(2,1)}, u32[]{:S(2)}, u32[]{:S(2)}) collective-permute-start(bf16[144,1024]{1,0:T(8,128)(2,1)} %add_convert_fusion.6), channel_id=1, source_target_pairs={{0,4},{2,6},{4,0},{6,2},{1,5},{3,7},{5,1},{7,3},{8,12},{10,14},{12... | collective-permute-start | bytes 884744 | tf_op jit(solution)/shard_map/gqkvo/z2/ppermute | solution.py:102
  255.5 21.4 %collective-permute-start.43 = (bf16[144,1024]{1,0:T(8,128)(2,1)}, bf16[144,1024]{1,0:T(8,128)(2,1)}, u32[]{:S(2)}, u32[]{:S(2)}) collective-permute-start(bf16[144,1024]{1,0:T(8,128)(2,1)} %add_convert_fusion.5), channel_id=1, source_target_pairs={{0,6},{2,4},{4,2},{6,0},{1,7},{3,5},{5,3},{7,1},{8,14},{10,12},{12... | collective-permute-start | bytes 884744 | tf_op jit(solution)/shard_map/gqkvo/z3/ppermute | solution.py:102
  256.7 5.8 %collective-permute-start.47 = (bf16[128,1024]{1,0:T(8,128)(2,1)}, bf16[128,1024]{1,0:T(8,128)(2,1)S(1)}, u32[]{:S(2)}, u32[]{:S(2)}) collective-permute-start(bf16[128,1024]{1,0:T(8,128)(2,1)} %reduce-scatter.2.cloned.1.call-done.refs_4_), channel_id=1, source_target_pairs={{0,16},{8,24},{16,0},{24,8},{1,17},{9,25},{17,1},{25,9},{2,18},{10... | collective-permute-start | bytes 786440 | tf_op jit(solution)/shard_map/fdown/seq2/ppermute | solution.py:75
  262.5 25.4 %collective-permute-start.33 = (bf16[256,1024]{1,0:T(8,128)(2,1)}, bf16[256,1024]{1,0:T(8,128)(2,1)S(1)}, u32[]{:S(2)}, u32[]{:S(2)}) collective-permute-start(bf16[256,1024]{1,0:T(8,128)(2,1)} %bitcast.24), channel_id=1, source_target_pairs={{0,8},{8,0},{16,24},{24,16},{1,9},{9,1},{17,25},{25,17},{2,10},{10... | collective-permute-start | bytes 1572872 | tf_op jit(solution)/shard_map/input/seq1/ppermute | solution.py:75
  266.8 14.3 %collective-permute-start.51 = (bf16[128,1024]{1,0:T(8,128)(2,1)}, bf16[128,1024]{1,0:T(8,128)(2,1)S(1)}, u32[]{:S(2)}, u32[]{:S(2)}) collective-permute-start(bf16[128,1024]{1,0:T(8,128)(2,1)} %reduce-scatter.2.cloned.1.call-done.refs_4_), channel_id=1, source_target_pairs={{0,8},{8,0},{16,24},{24,16},{1,9},{9,1},{17,25},{25,17},{2,10},{10... | collective-permute-start | bytes 786440 | tf_op jit(solution)/shard_map/fdown/seq1/ppermute | solution.py:75
  266.8 14.3 %collective-permute-start.49 = (bf16[128,1024]{1,0:T(8,128)(2,1)S(1)}, bf16[128,1024]{1,0:T(8,128)(2,1)S(1)}, u32[]{:S(2)}, u32[]{:S(2)}) collective-permute-start(bf16[128,1024]{1,0:T(8,128)(2,1)S(1)} %reduce_sum.12.refs_0_), channel_id=1, source_target_pairs={{0,16},{8,24},{16,0},{24,8},{1,17},{9,25},{17,1},{25,9},{2,18},{10... | collective-permute-start | bytes 786440 | tf_op jit(solution)/shard_map/fup/seq2/ppermute | solution.py:75
  278.4 7.6 %collective-permute-start.46 = (bf16[144,1024]{1,0:T(8,128)(2,1)S(1)}, bf16[144,1024]{1,0:T(8,128)(2,1)S(1)}, u32[]{:S(2)}, u32[]{:S(2)}) collective-permute-start(bf16[144,1024]{1,0:T(8,128)(2,1)S(1)} %add_convert_fusion.4.c0), channel_id=1, source_target_pairs={{0,16},{8,24},{16,0},{24,8},{1,17},{9,25},{17,1},{25,9},{2,18},{10... | collective-permute-start | bytes 884744 | tf_op jit(solution)/shard_map/small/seq2/ppermute | solution.py:75
  282.3 7.0 %collective-permute-start.45 = (bf16[144,1024]{1,0:T(8,128)(2,1)S(1)}, bf16[144,1024]{1,0:T(8,128)(2,1)S(1)}, u32[]{:S(2)}, u32[]{:S(2)}) collective-permute-start(bf16[144,1024]{1,0:T(8,128)(2,1)S(1)} %add_convert_fusion.4.c0), channel_id=1, source_target_pairs={{0,8},{8,0},{16,24},{24,16},{1,9},{9,1},{17,25},{25,17},{2,10},{10... | collective-permute-start | bytes 884744 | tf_op jit(solution)/shard_map/small/seq1/ppermute | solution.py:75
  286.0 3.3 %collective-permute-start.53 = (bf16[144,1024]{1,0:T(8,128)(2,1)S(1)}, bf16[144,1024]{1,0:T(8,128)(2,1)S(1)}, u32[]{:S(2)}, u32[]{:S(2)}) collective-permute-start(bf16[144,1024]{1,0:T(8,128)(2,1)S(1)} %collective-permute-done.46.c2), channel_id=1, source_target_pairs={{0,8},{8,0},{16,24},{24,16},{1,9},{9,1},{17,25},{25,17},{2,10},{10... | collective-permute-start | bytes 884744 | tf_op jit(solution)/shard_map/small/seq1/ppermute | solution.py:75
  (47 other events, 397.5 us)
Sparse Core Ops, SparseCore 0:
  25.4 74.8 all-gather.2
  152.0 68.6 reduce-scatter.1

commit v4 on v3

--- a/solution.py
+++ b/solution.py
@@ -972,12 +972,13 @@
     *parts, up_low, up_sums = ffn_back(ids, lows, packed, slope, fs)
     with scope("ffnback"):
         parts, onward = reduce_seq(parts)
+    keep_up, send_up = up_grads(ids, firsts, after(up_low, parts[1]), fs)
+    with scope("gup"):
+        came_up = swap_y(send_up)
+    parts[0] = after(parts[0], keep_up)
     attn_grad, first_sums, *pieces, out_low = first_norm(ids, ffn_grad, parts, attn_sum, vec, wo)
     with scope("mixback"):
         grads = exchange_seq(pieces)
-    keep_up, send_up = up_grads(ids, firsts, after(up_low, grads[1]), fs)
-    with scope("gup"):
-        came_up = swap_y(send_up)
     out_parts = out_grads(ids, mix, out_low)
     with scope("outs"):
         out_parts, onward = reduce_seq(out_parts, *grads[2:])
@@ -986,7 +987,7 @@
     with scope("gup"):
         up_terms = add(keep_up, after(came_up, back))
         up_grad = sum_z(up_terms)
-    back = after(back, up_terms)
+    back = after(back, up_terms, down_grad)
     pieces = qkvo_grads(
         ids, tokens, back.reshape(-1, back.shape[-1]), out_parts,
         (back_sums, first_sums, second_sums, up_sums), fs,

time: 300 us -> 297 us (0.990)
    ppermute x39, waiting for transfers between devices: 67.3 us -> 63.2 us  [seq_swap(): return lax.ppermute(value, SEQ, [(i, i ^ k) for i in range(SEQ_N)])]
  transfers between devices with their start and end apart: 57 -> 57, of which waited for: 29 -> 30; matrix products, arithmetic and copies ran while one was open for 4% -> 4% of each run, Pallas kernels for 17% -> 17%
where the time goes in v4:
time: 297 us; the launch traced here: 294 us
  waiting for transfers between devices  110 us (37%)
  starting transfers between devices  69.7 us (23%)
  Pallas kernels  69.2 us (23%)
  local copies, waits for them, and re-layouts  19.6 us (7%)
  between operations  14.6 us (5%)
  other arithmetic  11.2 us (4%)
    pallas_call x15, Pallas kernels, call(): pl.pallas_call(kernel, out_shape=outs, in_specs=in_specs, out_specs=out_s...  69.2 us
    ppermute x39, waiting for transfers between devices, seq_swap(): return lax.ppermute(value, SEQ, [(i, i ^ k) for i in range(SEQ_N)])  63.2 us
    ppermute x39, starting transfers between devices, seq_swap(): return lax.ppermute(value, SEQ, [(i, i ^ k) for i in range(SEQ_N)])  47.3 us
    ppermute x9, waiting for transfers between devices, swap_y(): return lax.ppermute(value, 'y', [(0, 1), (1, 0)])  22.9 us
    ppermute x6, waiting for transfers between devices, swap_z(): return lax.ppermute(value, 'z', [(i, i ^ k) for i in range(count)])  22 us
    unnamed x83, local copies, waits for them, and re-layouts  19.6 us
    ppermute x9, starting transfers between devices, swap_y(): return lax.ppermute(value, 'y', [(0, 1), (1, 0)])  10.7 us
    ppermute x6, starting transfers between devices, swap_z(): return lax.ppermute(value, 'z', [(i, i ^ k) for i in range(count)])  6.81 us
  transfers between devices with their start and end apart: 57, of which 30 were waited for; matrix products, arithmetic and copies ran while one was open for 4% of the time, Pallas kernels for 17%

profile of v4, /device:TPU:13, one launch (start us, length us, event | category | flops | bytes accessed | tf_op | source)
XLA Modules:
  0.0 294.3 jit_solution(17281428776605137548)
XLA Ops:
  7.8 2.6 early_pack.1.refs_0_
  12.0 2.6 late_pack.1
  14.7 3.9 %collective-permute-done.6.refs_4_ = bf16[144,1024]{1,0:T(8,128)(2,1)S(1)} collective-permute-done((bf16[144,1024]{1,0:T(8,128)(2,1)}, bf16[144,1024]{1,0:T(8,128)(2,1)S(1)}, u32[]{:S(2)}, u32[]{:S(2)}) %collective-permute-start.6) | collective-permute-done | bytes 294944 | tf_op jit(solution)/shard_map/wqkv/y/ppermute | solution.py:97
  18.6 6.7 %collective-permute-done.5.refs_3_ = bf16[144,1024]{1,0:T(8,128)(2,1)S(1)} collective-permute-done((bf16[144,1024]{1,0:T(8,128)(2,1)}, bf16[144,1024]{1,0:T(8,128)(2,1)S(1)}, u32[]{:S(2)}, u32[]{:S(2)}) %collective-permute-start.5) | collective-permute-done | bytes 294944 | tf_op jit(solution)/shard_map/wqkv/z3/ppermute | solution.py:102
  25.4 2.0 collective-permute-start.3
  28.6 2.7 collective-permute-start
  32.7 5.0 %collective-permute-done.4.refs_2_ = bf16[144,1024]{1,0:T(8,128)(2,1)S(1)} collective-permute-done((bf16[144,1024]{1,0:T(8,128)(2,1)S(1)}, bf16[144,1024]{1,0:T(8,128)(2,1)S(1)}, u32[]{:S(2)}, u32[]{:S(2)}) %collective-permute-start.4) | collective-permute-done | bytes 294944 | tf_op jit(solution)/shard_map/wqkv/z2/ppermute | solution.py:102
  37.7 2.3 collective-permute-start.8
  41.3 2.4 collective-permute-start.7
  43.8 7.7 %collective-permute-start.2 = (bf16[2,128,1024]{2,1,0:T(8,128)(2,1)S(1)}, bf16[2,128,1024]{2,1,0:T(8,128)(2,1)S(1)}, u32[]{:S(2)}, u32[]{:S(2)}) collective-permute-start(bf16[2,128,1024]{2,1,0:T(8,128)(2,1)S(1)} %collective-permute-done.1.x2), channel_id=1, source_target_pairs={{0,8},{8,0},{16,24},{24,16},{1,9},{9,1},{17,25},{25,17},{2,10},{10... | collective-permute-start | bytes 1572872 | tf_op jit(solution)/shard_map/tok/seq1/ppermute | solution.py:75
  51.5 4.0 %collective-permute-done.7.refs_5_ = bf16[144,1024]{1,0:T(8,128)(2,1)S(1)} collective-permute-done((bf16[144,1024]{1,0:T(8,128)(2,1)S(1)}, bf16[144,1024]{1,0:T(8,128)(2,1)S(1)}, u32[]{:S(2)}, u32[]{:S(2)}) %collective-permute-start.7) | collective-permute-done | bytes 294944 | tf_op jit(solution)/shard_map/wqkv/y/ppermute | solution.py:97
  55.7 4.1 %collective-permute-start.13 = (bf16[8,128,256]{2,1,0:T(8,128)(2,1)S(1)}, bf16[8,128,256]{2,1,0:T(8,128)(2,1)S(1)}, u32[]{:S(2)}, u32[]{:S(2)}) collective-permute-start(bf16[8,128,256]{2,1,0:T(8,128)(2,1)S(1)} %fusion.3.w0), channel_id=1, source_target_pairs={{0,8},{8,0},{16,24},{24,16},{1,9},{9,1},{17,25},{25,17},{2,10},{10... | collective-permute-start | bytes 1572872 | tf_op jit(solution)/shard_map/wo/seq1/ppermute | solution.py:75
  59.8 8.2 %attend.1 = (bf16[2,512,768]{2,1,0:T(8,128)(2,1)S(1)}, f32[2,4,512]{2,1,0:T(4,128)S(1)}, bf16[2,128,256]{2,1,0:T(8,128)(2,1)S(1)}, bf16[2,128,256]{2,1,0:T(8,128...) custom-call(s32[2]{0:T(128)S(1)} %copy-done.17, ...), custom_call_target="tpu_custom_call" | custom-call | flops 2147483648 | bytes 8208392 | tf_op jit(solution)/shard_map/attend/pallas_call | solution.py:56
  72.2 2.5 collective-permute-done.11.m2
  74.7 3.8 %collective-permute-done.12.m3 = bf16[256,256]{1,0:T(8,128)(2,1)S(1)} collective-permute-done((bf16[256,256]{1,0:T(8,128)(2,1)S(1)}, bf16[256,256]{1,0:T(8,128)(2,1)S(1)}, u32[]{:S(2)}, u32[]{:S(2)}) %collective-permute-start.12) | collective-permute-done | bytes 131104 | tf_op jit(solution)/shard_map/mix/seq3/ppermute | solution.py:75
  78.4 2.3 out_project.1
  84.4 11.9 %collective-permute-done.17.f2 = bf16[256,1024]{1,0:T(8,128)(2,1)S(1)} collective-permute-done((bf16[256,1024]{1,0:T(8,128)(2,1)S(1)}, bf16[256,1024]{1,0:T(8,128)(2,1)S(1)}, u32[]{:S(2)}, u32[]{:S(2)}) %collective-permute-start.17) | collective-permute-done | bytes 524320 | tf_op jit(solution)/shard_map/first/seq2/ppermute | solution.py:75
  98.4 1.9 all-gather.3.cloned.1.call-done
  101.3 9.6 %ffn.1 = (bf16[256,1024]{1,0:T(8,128)(2,1)S(1)}, bf16[256,1024]{1,0:T(8,128)(2,1)S(1)}, bf16[256,1024]{1,0:T(8,128)(2,1)S(1)}, bf16[256,1024]{1,0:T(8,128)(2,1)S...) custom-call(s32[2]{0:T(128)S(1)} %copy-done.17, bf16[256,1024]{1,0:T(8,128)(2,1)S(1)} %copy-done.6, ...), custom_call_target="tpu_custom_call" | custom-call | flops 4294967296 | bytes 12648456 | tf_op jit(solution)/shard_map/ffn/pallas_call | solution.py:56
  111.0 1.8 collective-permute-start.19
  116.5 11.8 %collective-permute-done.21.p2 = bf16[256,1024]{1,0:T(8,128)(2,1)S(1)} collective-permute-done((bf16[256,1024]{1,0:T(8,128)(2,1)S(1)}, bf16[256,1024]{1,0:T(8,128)(2,1)S(1)}, u32[]{:S(2)}, u32[]{:S(2)}) %collective-permute-start.21) | collective-permute-done | bytes 524320 | tf_op jit(solution)/shard_map/ffn/seq2/ppermute | solution.py:75
  128.3 1.7 second_norm.1
  133.3 10.1 %collective-permute-done.23.d2 = bf16[256,1024]{1,0:T(8,128)(2,1)S(1)} collective-permute-done((bf16[256,1024]{1,0:T(8,128)(2,1)S(1)}, bf16[256,1024]{1,0:T(8,128)(2,1)S(1)}, u32[]{:S(2)}, u32[]{:S(2)}) %collective-permute-start.23) | collective-permute-done | bytes 524320 | tf_op jit(solution)/shard_map/low/seq2/ppermute | solution.py:75
  143.4 1.9 collective-permute-start.24
  146.8 3.4 %down_grads.1 = bf16[1024,1024]{1,0:T(8,128)(2,1)} custom-call(bf16[1024,1024]{1,0:T(8,128)(2,1)S(1)} %get-tuple-element.122.gelu, bf16[256,1024]{1,0:T(8,128)(2,1)S(1)} %get-tuple-element.120.d0, bf16[256,1024]{1,0:T(8,128)(2,1)S(1)} %collective-permute-done.22.d1, bf16[256,1024]{1,0:T(8,128)(2,1)S(1)} %collective-permute-done.23.d2, ...), custom_call_target="tpu_custom_call" | custom-call | flops 67108864 | bytes 196608 | tf_op jit(solution)/shard_map/down_grads/pallas_call | solution.py:56
  155.0 2.2 copy-done.18
  157.2 1.6 copy-done.33
  158.8 6.3 %ffn_back.1 = (bf16[256,1024]{1,0:T(8,128)(2,1)S(1)}, bf16[256,1024]{1,0:T(8,128)(2,1)S(1)}, bf16[256,1024]{1,0:T(8,128)(2,1)S(1)}, bf16[256,1024]{1,0:T(8,128)(...) custom-call(s32[2]{0:T(128)S(1)} %copy-done.17, bf16[256,1024]{1,0:T(8,128)(2,1)S(1)} %copy-done.8, ...), custom_call_target="tpu_custom_call" | custom-call | flops 4294967296 | bytes 12615688 | tf_op jit(solution)/shard_map/ffn_back/pallas_call | solution.py:56
  169.3 4.9 %up_grads.1 = (bf16[4,128,1024]{2,1,0:T(8,128)(2,1)S(1)}, bf16[4,128,1024]{2,1,0:T(8,128)(2,1)S(1)}) custom-call(s32[2]{0:T(128)S(1)} %copy-done.17, bf16[256,1024]{1,0:T(8,128)(2,1)} %copy-done.5, bf16[256,1024]{1,0:T(8,128)(2,1)} %copy-done.37, bf16[256,1024]{1,0:T(8,128)(2,1)} %copy-done.36, bf16[256,1024]{1,0:T(8,128)(2,1)} %collective-permute-done.18.f3, ...), custom_call_target="tpu_custom_call" | custom-call | flops 67108864 | bytes 196608 | tf_op jit(solution)/shard_map/up_grads/pallas_call | solution.py:56
  174.2 7.0 %collective-permute-done.27.p2 = bf16[256,1024]{1,0:T(8,128)(2,1)S(1)} collective-permute-done((bf16[256,1024]{1,0:T(8,128)(2,1)S(1)}, bf16[256,1024]{1,0:T(8,128)(2,1)S(1)}, u32[]{:S(2)}, u32[]{:S(2)}) %collective-permute-start.27) | collective-permute-done | bytes 524320 | tf_op jit(solution)/shard_map/ffnback/seq2/ppermute | solution.py:75
  181.3 2.2 first_norm.1
  190.1 2.3 collective-permute-done.30
  192.4 3.4 %collective-permute-done.31 = bf16[256,256]{1,0:T(8,128)(2,1)S(1)} collective-permute-done((bf16[256,256]{1,0:T(8,128)(2,1)S(1)}, bf16[256,256]{1,0:T(8,128)(2,1)S(1)}, u32[]{:S(2)}, u32[]{:S(2)}) %collective-permute-start.31) | collective-permute-done | bytes 131104 | tf_op jit(solution)/shard_map/mixback/seq3/ppermute | solution.py:75
  197.0 13.3 %attend_back.1 = (bf16[2,512,768]{2,1,0:T(8,128)(2,1)S(1)}, f32[8,768]{1,0:T(8,128)S(1)}, bf16[2,128,1024]{2,1,0:T(8,128)(2,1)S(1)}, bf16[2,128,1024]{2,1,0:T(8,...) custom-call(bf16[2,512,768]{2,1,0:T(8,128)(2,1)S(1)} %copy-done.31, ...), custom_call_target="tpu_custom_call" | custom-call | flops 2952790016 | bytes 7380992 | tf_op jit(solution)/shard_map/attend_back/pallas_call | solution.py:56
  212.2 3.8 %collective-permute-done.35 = bf16[4,128,1024]{2,1,0:T(8,128)(2,1)S(1)} collective-permute-done((bf16[4,128,1024]{2,1,0:T(8,128)(2,1)S(1)}, bf16[4,128,1024]{2,1,0:T(8,128)(2,1)S(1)}, u32[]{:S(2)}, u32[]{:S(2)}) %collective-permute-start.35) | collective-permute-done | bytes 1048608 | tf_op jit(solution)/shard_map/gup/y/ppermute | solution.py:97
  217.4 4.8 %all-to-all-start = ((bf16[4,128,1024]{2,1,0:T(8,128)(2,1)}), bf16[4,128,1024]{2,1,0:T(8,128)(2,1)}, u32[]{:S(2)}, u32[]{:S(2)}) async-start(bf16[4,128,1024]{2,1,0:T(8,128)(2,1)} %add_convert_fusion), calls=%async_computation.1 | async-start | bytes 2097152 | tf_op jit(solution)/shard_map/gup/z/all_to_all | solution.py:107
  224.7 5.9 %qkvo_grads.1 = (bf16[144,1024]{1,0:T(8,128)(2,1)S(1)}, bf16[144,1024]{1,0:T(8,128)(2,1)S(1)}, bf16[144,1024]{1,0:T(8,128)(2,1)S(1)}, bf16[144,1024]{1,0:T(8,128...) custom-call(s32[2]{0:T(128)S(1)} %copy-done.17, ...), custom_call_target="tpu_custom_call" | custom-call | flops 1610612736 | bytes 7725064 | tf_op jit(solution)/shard_map/qkvo_grads/pallas_call | solution.py:56
  236.0 2.4 collective-permute-done.38
  239.2 5.4 %collective-permute-done.40 = bf16[144,1024]{1,0:T(8,128)(2,1)S(1)} collective-permute-done((bf16[144,1024]{1,0:T(8,128)(2,1)S(1)}, bf16[144,1024]{1,0:T(8,128)(2,1)S(1)}, u32[]{:S(2)}, u32[]{:S(2)}) %collective-permute-start.40) | collective-permute-done | bytes 294944 | tf_op jit(solution)/shard_map/gqkvo/y/ppermute | solution.py:97
  245.4 2.2 collective-permute-start.41
  247.6 3.3 %collective-permute-done.42 = bf16[144,1024]{1,0:T(8,128)(2,1)S(1)} collective-permute-done((bf16[144,1024]{1,0:T(8,128)(2,1)S(1)}, bf16[144,1024]{1,0:T(8,128)(2,1)S(1)}, u32[]{:S(2)}, u32[]{:S(2)}) %collective-permute-start.42) | collective-permute-done | bytes 294944 | tf_op jit(solution)/shard_map/gqkvo/y/ppermute | solution.py:97
  255.6 3.0 %collective-permute-done.47.refs_6_ = bf16[128,1024]{1,0:T(8,128)(2,1)S(1)} collective-permute-done((bf16[128,1024]{1,0:T(8,128)(2,1)S(1)}, bf16[128,1024]{1,0:T(8,128)(2,1)S(1)}, u32[]{:S(2)}, u32[]{:S(2)}) %collective-permute-start.47) | collective-permute-done | bytes 262176 | tf_op jit(solution)/shard_map/fdown/seq2/ppermute | solution.py:75
  258.6 4.2 %collective-permute-start.33 = (bf16[256,1024]{1,0:T(8,128)(2,1)}, bf16[256,1024]{1,0:T(8,128)(2,1)S(1)}, u32[]{:S(2)}, u32[]{:S(2)}) collective-permute-start(bf16[256,1024]{1,0:T(8,128)(2,1)} %bitcast.24), channel_id=1, source_target_pairs={{0,8},{8,0},{16,24},{24,16},{1,9},{9,1},{17,25},{25,17},{2,10},{10... | collective-permute-start | bytes 1572872 | tf_op jit(solution)/shard_map/input/seq1/ppermute | solution.py:75
  264.0 2.8 collective-permute-done.41
  266.8 6.3 %collective-permute-done.43 = bf16[144,1024]{1,0:T(8,128)(2,1)} collective-permute-done((bf16[144,1024]{1,0:T(8,128)(2,1)}, bf16[144,1024]{1,0:T(8,128)(2,1)}, u32[]{:S(2)}, u32[]{:S(2)}) %collective-permute-start.43) | collective-permute-done | bytes 294944 | tf_op jit(solution)/shard_map/gqkvo/z3/ppermute | solution.py:102
  278.9 3.0 %finish_ffn.1 = (f32[128,4096]{1,0:T(8,128)}, f32[512,1024]{1,0:T(8,128)}) custom-call(s32[2]{0:T(128)S(1)} %copy-done.17, bf16[128,1024]{1,0:T(8,128)(2,1)S(1)} %reduce_sum.12.refs_0_, bf16[128,1024]{1,0:T(8,128)(2,1)S(1)} %collective-permute-done.48.refs_1_, bf16[128,1024]{1,0:T(8,128)(2,1)S(1)} %collective-permute-done.49.refs_2_, ...), custom_call_target="tpu_custom_call" | custom-call | bytes 6291464 | tf_op jit(solution)/shard_map/finish_ffn/pallas_call | solution.py:56
  282.2 1.8 collective-permute-start.53
  285.4 2.0 finish_qkvo.1
  (179 shorter events, 68.6 us)
Async XLA Ops:
  7.2 93.1 %all-gather.3.cloned.1.call-start = ((), (), s32[]{:S(2)}) async-start(), calls=%async_computation.3 | async-start | bytes 4718592 | tf_op jit(solution)/shard_map/ffnw/all_gather | solution.py:949
  10.4 8.2 %collective-permute-start.6 = (bf16[144,1024]{1,0:T(8,128)(2,1)}, bf16[144,1024]{1,0:T(8,128)(2,1)S(1)}, u32[]{:S(2)}, u32[]{:S(2)}) collective-permute-start(bf16[144,1024]{1,0:T(8,128)(2,1)} %early_pack.1.refs_0_), channel_id=1, source_target_pairs={{0,1},{1,0},{2,3},{3,2},{4,5},{5,4},{6,7},{7,6},{8,9},{9,8},{10,11... | collective-permute-start | bytes 884744 | tf_op jit(solution)/shard_map/wqkv/y/ppermute | solution.py:97
  10.7 14.5 %collective-permute-start.5 = (bf16[144,1024]{1,0:T(8,128)(2,1)}, bf16[144,1024]{1,0:T(8,128)(2,1)S(1)}, u32[]{:S(2)}, u32[]{:S(2)}) collective-permute-start(bf16[144,1024]{1,0:T(8,128)(2,1)} %early_pack.1.refs_0_), channel_id=1, source_target_pairs={{0,6},{2,4},{4,2},{6,0},{1,7},{3,5},{5,3},{7,1},{8,14},{10,12},{12... | collective-permute-start | bytes 884744 | tf_op jit(solution)/shard_map/wqkv/z3/ppermute | solution.py:102
  25.3 197.0 %reduce-scatter.2.cloned.1.call-start = ((), (), s32[]{:S(2)}) async-start(), calls=%async_computation.2 | async-start | bytes 2359296 | tf_op jit(solution)/shard_map/gdown/reduce_scatter | solution.py:970
  25.3 12.4 %collective-permute-start.4 = (bf16[144,1024]{1,0:T(8,128)(2,1)S(1)}, bf16[144,1024]{1,0:T(8,128)(2,1)S(1)}, u32[]{:S(2)}, u32[]{:S(2)}) collective-permute-start(bf16[144,1024]{1,0:T(8,128)(2,1)S(1)} %copy-done.15), channel_id=1, source_target_pairs={{0,4},{2,6},{4,0},{6,2},{1,5},{3,7},{5,1},{7,3},{8,12},{10,14},{12... | collective-permute-start | bytes 884744 | tf_op jit(solution)/shard_map/wqkv/z2/ppermute | solution.py:102
  25.4 15.9 %collective-permute-start.3 = (bf16[144,1024]{1,0:T(8,128)(2,1)S(1)}, bf16[144,1024]{1,0:T(8,128)(2,1)S(1)}, u32[]{:S(2)}, u32[]{:S(2)}) collective-permute-start(bf16[144,1024]{1,0:T(8,128)(2,1)S(1)} %copy-done.15), channel_id=1, source_target_pairs={{0,2},{2,0},{4,6},{6,4},{1,3},{3,1},{5,7},{7,5},{8,10},{10,8},{12,... | collective-permute-start | bytes 884744 | tf_op jit(solution)/shard_map/wqkv/z1/ppermute | solution.py:102
  27.4 16.3 %collective-permute-start.1 = (bf16[2,128,1024]{2,1,0:T(8,128)(2,1)S(1)}, bf16[2,128,1024]{2,1,0:T(8,128)(2,1)S(1)}, u32[]{:S(2)}, u32[]{:S(2)}) collective-permute-start(bf16[2,128,1024]{2,1,0:T(8,128)(2,1)S(1)} %copy-done.13), channel_id=1, source_target_pairs={{0,16},{8,24},{16,0},{24,8},{1,17},{9,25},{17,1},{25,9},{2,18},{10... | collective-permute-start | bytes 1572872 | tf_op jit(solution)/shard_map/tok/seq2/ppermute | solution.py:75
  28.6 31.2 %collective-permute-start = (bf16[2,128,1024]{2,1,0:T(8,128)(2,1)S(1)}, bf16[2,128,1024]{2,1,0:T(8,128)(2,1)S(1)}, u32[]{:S(2)}, u32[]{:S(2)}) collective-permute-start(bf16[2,128,1024]{2,1,0:T(8,128)(2,1)S(1)} %copy-done.13), channel_id=1, source_target_pairs={{0,8},{8,0},{16,24},{24,16},{1,9},{9,1},{17,25},{25,17},{2,10},{10... | collective-permute-start | bytes 1572872 | tf_op jit(solution)/shard_map/tok/seq1/ppermute | solution.py:75
  31.4 24.2 %collective-permute-start.9 = (bf16[144,1024]{1,0:T(8,128)(2,1)S(1)}, bf16[144,1024]{1,0:T(8,128)(2,1)S(1)}, u32[]{:S(2)}, u32[]{:S(2)}) collective-permute-start(bf16[144,1024]{1,0:T(8,128)(2,1)S(1)} %collective-permute-done.5.refs_3_), channel_id=1, source_target_pairs={{0,1},{1,0},{2,3},{3,2},{4,5},{5,4},{6,7},{7,6},{8,9},{9,8},{10,11... | collective-permute-start | bytes 884744 | tf_op jit(solution)/shard_map/wqkv/y/ppermute | solution.py:97
  37.7 17.9 %collective-permute-start.8 = (bf16[144,1024]{1,0:T(8,128)(2,1)S(1)}, bf16[144,1024]{1,0:T(8,128)(2,1)S(1)}, u32[]{:S(2)}, u32[]{:S(2)}) collective-permute-start(bf16[144,1024]{1,0:T(8,128)(2,1)S(1)} %collective-permute-done.4.refs_2_), channel_id=1, source_target_pairs={{0,1},{1,0},{2,3},{3,2},{4,5},{5,4},{6,7},{7,6},{8,9},{9,8},{10,11... | collective-permute-start | bytes 884744 | tf_op jit(solution)/shard_map/wqkv/y/ppermute | solution.py:97
  41.3 14.3 %collective-permute-start.7 = (bf16[144,1024]{1,0:T(8,128)(2,1)S(1)}, bf16[144,1024]{1,0:T(8,128)(2,1)S(1)}, u32[]{:S(2)}, u32[]{:S(2)}) collective-permute-start(bf16[144,1024]{1,0:T(8,128)(2,1)S(1)} %collective-permute-done.3.refs_1_), channel_id=1, source_target_pairs={{0,1},{1,0},{2,3},{3,2},{4,5},{5,4},{6,7},{7,6},{8,9},{9,8},{10,11... | collective-permute-start | bytes 884744 | tf_op jit(solution)/shard_map/wqkv/y/ppermute | solution.py:97
  43.8 16.0 %collective-permute-start.2 = (bf16[2,128,1024]{2,1,0:T(8,128)(2,1)S(1)}, bf16[2,128,1024]{2,1,0:T(8,128)(2,1)S(1)}, u32[]{:S(2)}, u32[]{:S(2)}) collective-permute-start(bf16[2,128,1024]{2,1,0:T(8,128)(2,1)S(1)} %collective-permute-done.1.x2), channel_id=1, source_target_pairs={{0,8},{8,0},{16,24},{24,16},{1,9},{9,1},{17,25},{25,17},{2,10},{10... | collective-permute-start | bytes 1572872 | tf_op jit(solution)/shard_map/tok/seq1/ppermute | solution.py:75
  55.6 13.7 %collective-permute-start.14 = (bf16[8,128,256]{2,1,0:T(8,128)(2,1)S(1)}, bf16[8,128,256]{2,1,0:T(8,128)(2,1)S(1)}, u32[]{:S(2)}, u32[]{:S(2)}) collective-permute-start(bf16[8,128,256]{2,1,0:T(8,128)(2,1)S(1)} %fusion.3.w0), channel_id=1, source_target_pairs={{0,16},{8,24},{16,0},{24,8},{1,17},{9,25},{17,1},{25,9},{2,18},{10... | collective-permute-start | bytes 1572872 | tf_op jit(solution)/shard_map/wo/seq2/ppermute | solution.py:75
  55.7 16.5 %collective-permute-start.13 = (bf16[8,128,256]{2,1,0:T(8,128)(2,1)S(1)}, bf16[8,128,256]{2,1,0:T(8,128)(2,1)S(1)}, u32[]{:S(2)}, u32[]{:S(2)}) collective-permute-start(bf16[8,128,256]{2,1,0:T(8,128)(2,1)S(1)} %fusion.3.w0), channel_id=1, source_target_pairs={{0,8},{8,0},{16,24},{24,16},{1,9},{9,1},{17,25},{25,17},{2,10},{10... | collective-permute-start | bytes 1572872 | tf_op jit(solution)/shard_map/wo/seq1/ppermute | solution.py:75
  69.3 9.1 %collective-permute-start.15 = (bf16[8,128,256]{2,1,0:T(8,128)(2,1)S(1)}, bf16[8,128,256]{2,1,0:T(8,128)(2,1)S(1)}, u32[]{:S(2)}, u32[]{:S(2)}) collective-permute-start(bf16[8,128,256]{2,1,0:T(8,128)(2,1)S(1)} %collective-permute-done.14.w2), channel_id=1, source_target_pairs={{0,8},{8,0},{16,24},{24,16},{1,9},{9,1},{17,25},{25,17},{2,10},{10... | collective-permute-start | bytes 1572872 | tf_op jit(solution)/shard_map/wo/seq1/ppermute | solution.py:75
  70.0 4.7 %collective-permute-start.11 = (bf16[256,256]{1,0:T(8,128)(2,1)S(1)}, bf16[256,256]{1,0:T(8,128)(2,1)S(1)}, u32[]{:S(2)}, u32[]{:S(2)}) collective-permute-start(bf16[256,256]{1,0:T(8,128)(2,1)S(1)} %bitcast.66), channel_id=1, source_target_pairs={{0,16},{8,24},{16,0},{24,8},{1,17},{9,25},{17,1},{25,9},{2,18},{10... | collective-permute-start | bytes 393224 | tf_op jit(solution)/shard_map/mix/seq2/ppermute | solution.py:75
  71.0 7.4 %collective-permute-start.12 = (bf16[256,256]{1,0:T(8,128)(2,1)S(1)}, bf16[256,256]{1,0:T(8,128)(2,1)S(1)}, u32[]{:S(2)}, u32[]{:S(2)}) collective-permute-start(bf16[256,256]{1,0:T(8,128)(2,1)S(1)} %bitcast.64), channel_id=1, source_target_pairs={{0,24},{8,16},{16,8},{24,0},{1,25},{9,17},{17,9},{25,1},{2,26},{10... | collective-permute-start | bytes 393224 | tf_op jit(solution)/shard_map/mix/seq3/ppermute | solution.py:75
  82.5 13.8 %collective-permute-start.17 = (bf16[256,1024]{1,0:T(8,128)(2,1)S(1)}, bf16[256,1024]{1,0:T(8,128)(2,1)S(1)}, u32[]{:S(2)}, u32[]{:S(2)}) collective-permute-start(bf16[256,1024]{1,0:T(8,128)(2,1)S(1)} %get-tuple-element.111.f0), channel_id=1, source_target_pairs={{0,16},{8,24},{16,0},{24,8},{1,17},{9,25},{17,1},{25,9},{2,18},{10... | collective-permute-start | bytes 1572872 | tf_op jit(solution)/shard_map/first/seq2/ppermute | solution.py:75
  83.5 12.9 %collective-permute-start.16 = (bf16[256,1024]{1,0:T(8,128)(2,1)S(1)}, bf16[256,1024]{1,0:T(8,128)(2,1)S(1)}, u32[]{:S(2)}, u32[]{:S(2)}) collective-permute-start(bf16[256,1024]{1,0:T(8,128)(2,1)S(1)} %get-tuple-element.111.f0), channel_id=1, source_target_pairs={{0,8},{8,0},{16,24},{24,16},{1,9},{9,1},{17,25},{25,17},{2,10},{10... | collective-permute-start | bytes 1572872 | tf_op jit(solution)/shard_map/first/seq1/ppermute | solution.py:75
  111.0 3.3 %collective-permute-start.19 = (bf16[256,1024]{1,0:T(8,128)(2,1)S(1)}, bf16[256,1024]{1,0:T(8,128)(2,1)S(1)}, u32[]{:S(2)}, u32[]{:S(2)}) collective-permute-start(bf16[256,1024]{1,0:T(8,128)(2,1)S(1)} %get-tuple-element.116), channel_id=1, source_target_pairs={{0,8},{8,0},{16,24},{24,16},{1,9},{9,1},{17,25},{25,17},{2,10},{10... | collective-permute-start | bytes 1572872 | tf_op jit(solution)/shard_map/ffn/seq1/ppermute | solution.py:75
  114.9 13.4 %collective-permute-start.21 = (bf16[256,1024]{1,0:T(8,128)(2,1)S(1)}, bf16[256,1024]{1,0:T(8,128)(2,1)S(1)}, u32[]{:S(2)}, u32[]{:S(2)}) collective-permute-start(bf16[256,1024]{1,0:T(8,128)(2,1)S(1)} %add_convert_fusion.3), channel_id=1, source_target_pairs={{0,16},{8,24},{16,0},{24,8},{1,17},{9,25},{17,1},{25,9},{2,18},{10... | collective-permute-start | bytes 1572872 | tf_op jit(solution)/shard_map/ffn/seq2/ppermute | solution.py:75
  131.0 12.5 %collective-permute-start.23 = (bf16[256,1024]{1,0:T(8,128)(2,1)S(1)}, bf16[256,1024]{1,0:T(8,128)(2,1)S(1)}, u32[]{:S(2)}, u32[]{:S(2)}) collective-permute-start(bf16[256,1024]{1,0:T(8,128)(2,1)S(1)} %get-tuple-element.120.d0), channel_id=1, source_target_pairs={{0,16},{8,24},{16,0},{24,8},{1,17},{9,25},{17,1},{25,9},{2,18},{10... | collective-permute-start | bytes 1572872 | tf_op jit(solution)/shard_map/low/seq2/ppermute | solution.py:75
  132.1 13.2 %collective-permute-start.22 = (bf16[256,1024]{1,0:T(8,128)(2,1)S(1)}, bf16[256,1024]{1,0:T(8,128)(2,1)S(1)}, u32[]{:S(2)}, u32[]{:S(2)}) collective-permute-start(bf16[256,1024]{1,0:T(8,128)(2,1)S(1)} %get-tuple-element.120.d0), channel_id=1, source_target_pairs={{0,8},{8,0},{16,24},{24,16},{1,9},{9,1},{17,25},{25,17},{2,10},{10... | collective-permute-start | bytes 1572872 | tf_op jit(solution)/shard_map/low/seq1/ppermute | solution.py:75
  143.4 3.4 %collective-permute-start.24 = (bf16[256,1024]{1,0:T(8,128)(2,1)S(1)}, bf16[256,1024]{1,0:T(8,128)(2,1)S(1)}, u32[]{:S(2)}, u32[]{:S(2)}) collective-permute-start(bf16[256,1024]{1,0:T(8,128)(2,1)S(1)} %collective-permute-done.23.d2), channel_id=1, source_target_pairs={{0,8},{8,0},{16,24},{24,16},{1,9},{9,1},{17,25},{25,17},{2,10},{10... | collective-permute-start | bytes 1572872 | tf_op jit(solution)/shard_map/low/seq1/ppermute | solution.py:75
  167.8 13.5 %collective-permute-start.27 = (bf16[256,1024]{1,0:T(8,128)(2,1)S(1)}, bf16[256,1024]{1,0:T(8,128)(2,1)S(1)}, u32[]{:S(2)}, u32[]{:S(2)}) collective-permute-start(bf16[256,1024]{1,0:T(8,128)(2,1)S(1)} %add_convert_fusion.2), channel_id=1, source_target_pairs={{0,16},{8,24},{16,0},{24,8},{1,17},{9,25},{17,1},{25,9},{2,18},{10... | collective-permute-start | bytes 1572872 | tf_op jit(solution)/shard_map/ffnback/seq2/ppermute | solution.py:75
  184.8 4.4 %collective-permute-start.28 = (bf16[1024,256]{1,0:T(8,128)(2,1)S(1)}, bf16[1024,256]{1,0:T(8,128)(2,1)S(1)}, u32[]{:S(2)}, u32[]{:S(2)}) collective-permute-start(bf16[1024,256]{1,0:T(8,128)(2,1)S(1)} %get-tuple-element.142), channel_id=1, source_target_pairs={{0,8},{8,0},{16,24},{24,16},{1,9},{9,1},{17,25},{25,17},{2,10},{10... | collective-permute-start | bytes 1572872 | tf_op jit(solution)/shard_map/outs/seq1/ppermute | solution.py:75
  185.7 30.3 %collective-permute-start.35 = (bf16[4,128,1024]{2,1,0:T(8,128)(2,1)S(1)}, bf16[4,128,1024]{2,1,0:T(8,128)(2,1)S(1)}, u32[]{:S(2)}, u32[]{:S(2)}) collective-permute-start(bf16[4,128,1024]{2,1,0:T(8,128)(2,1)S(1)} %get-tuple-element.154), channel_id=1, source_target_pairs={{0,1},{1,0},{2,3},{3,2},{4,5},{5,4},{6,7},{7,6},{8,9},{9,8},{10,11... | collective-permute-start | bytes 3145736 | tf_op jit(solution)/shard_map/gup/y/ppermute | solution.py:97
  187.0 10.0 %collective-permute-start.29 = (bf16[256,256]{1,0:T(8,128)(2,1)S(1)}, bf16[256,256]{1,0:T(8,128)(2,1)S(1)}, u32[]{:S(2)}, u32[]{:S(2)}) collective-permute-start(bf16[256,256]{1,0:T(8,128)(2,1)S(1)} %get-tuple-element.144), channel_id=1, source_target_pairs={{0,8},{8,0},{16,24},{24,16},{1,9},{9,1},{17,25},{25,17},{2,10},{10... | collective-permute-start | bytes 393224 | tf_op jit(solution)/shard_map/mixback/seq1/ppermute | solution.py:75
  187.3 5.0 %collective-permute-start.30 = (bf16[256,256]{1,0:T(8,128)(2,1)S(1)}, bf16[256,256]{1,0:T(8,128)(2,1)S(1)}, u32[]{:S(2)}, u32[]{:S(2)}) collective-permute-start(bf16[256,256]{1,0:T(8,128)(2,1)S(1)} %get-tuple-element.145), channel_id=1, source_target_pairs={{0,16},{8,24},{16,0},{24,8},{1,17},{9,25},{17,1},{25,9},{2,18},{10... | collective-permute-start | bytes 393224 | tf_op jit(solution)/shard_map/mixback/seq2/ppermute | solution.py:75
  188.6 7.2 %collective-permute-start.31 = (bf16[256,256]{1,0:T(8,128)(2,1)S(1)}, bf16[256,256]{1,0:T(8,128)(2,1)S(1)}, u32[]{:S(2)}, u32[]{:S(2)}) collective-permute-start(bf16[256,256]{1,0:T(8,128)(2,1)S(1)} %get-tuple-element.146), channel_id=1, source_target_pairs={{0,24},{8,16},{16,8},{24,0},{1,25},{9,17},{17,9},{25,1},{2,26},{10... | collective-permute-start | bytes 393224 | tf_op jit(solution)/shard_map/mixback/seq3/ppermute | solution.py:75
  195.8 26.5 %collective-permute-start.36 = (bf16[1024,256]{1,0:T(8,128)(2,1)S(1)}, bf16[1024,256]{1,0:T(8,128)(2,1)}, u32[]{:S(2)}, u32[]{:S(2)}) collective-permute-start(bf16[1024,256]{1,0:T(8,128)(2,1)S(1)} %get-tuple-element.159), channel_id=1, source_target_pairs={{0,8},{8,0},{16,24},{24,16},{1,9},{9,1},{17,25},{25,17},{2,10},{10... | collective-permute-start | bytes 1572872 | tf_op jit(solution)/shard_map/outs/seq1/ppermute | solution.py:75
  195.8 26.5 %collective-permute-start.37 = (bf16[1024,256]{1,0:T(8,128)(2,1)}, bf16[1024,256]{1,0:T(8,128)(2,1)}, u32[]{:S(2)}, u32[]{:S(2)}) collective-permute-start(bf16[1024,256]{1,0:T(8,128)(2,1)} %add_convert_fusion.1), channel_id=1, source_target_pairs={{0,16},{8,24},{16,0},{24,8},{1,17},{9,25},{17,1},{25,9},{2,18},{10... | collective-permute-start | bytes 1572872 | tf_op jit(solution)/shard_map/outs/seq2/ppermute | solution.py:75
  211.4 20.7 %collective-permute-start.32 = (bf16[256,1024]{1,0:T(8,128)(2,1)}, bf16[256,1024]{1,0:T(8,128)(2,1)}, u32[]{:S(2)}, u32[]{:S(2)}) collective-permute-start(bf16[256,1024]{1,0:T(8,128)(2,1)} %bitcast.26), channel_id=1, source_target_pairs={{0,8},{8,0},{16,24},{24,16},{1,9},{9,1},{17,25},{25,17},{2,10},{10... | collective-permute-start | bytes 1572872 | tf_op jit(solution)/shard_map/input/seq1/ppermute | solution.py:75
  217.4 36.7 %all-to-all-start = ((bf16[4,128,1024]{2,1,0:T(8,128)(2,1)}), bf16[4,128,1024]{2,1,0:T(8,128)(2,1)}, u32[]{:S(2)}, u32[]{:S(2)}) async-start(bf16[4,128,1024]{2,1,0:T(8,128)(2,1)} %add_convert_fusion), calls=%async_computation.1 | async-start | bytes 2097152 | tf_op jit(solution)/shard_map/gup/z/all_to_all | solution.py:107
  230.6 7.8 %collective-permute-start.38 = (bf16[144,1024]{1,0:T(8,128)(2,1)S(1)}, bf16[144,1024]{1,0:T(8,128)(2,1)S(1)}, u32[]{:S(2)}, u32[]{:S(2)}) collective-permute-start(bf16[144,1024]{1,0:T(8,128)(2,1)S(1)} %get-tuple-element.166), channel_id=1, source_target_pairs={{0,1},{1,0},{2,3},{3,2},{4,5},{5,4},{6,7},{7,6},{8,9},{9,8},{10,11... | collective-permute-start | bytes 884744 | tf_op jit(solution)/shard_map/gqkvo/y/ppermute | solution.py:97
  231.7 13.0 %collective-permute-start.40 = (bf16[144,1024]{1,0:T(8,128)(2,1)S(1)}, bf16[144,1024]{1,0:T(8,128)(2,1)S(1)}, u32[]{:S(2)}, u32[]{:S(2)}) collective-permute-start(bf16[144,1024]{1,0:T(8,128)(2,1)S(1)} %get-tuple-element.168), channel_id=1, source_target_pairs={{0,1},{1,0},{2,3},{3,2},{4,5},{5,4},{6,7},{7,6},{8,9},{9,8},{10,11... | collective-permute-start | bytes 884744 | tf_op jit(solution)/shard_map/gqkvo/y/ppermute | solution.py:97
  233.4 19.5 %collective-permute-start.34 = (bf16[256,1024]{1,0:T(8,128)(2,1)S(1)}, bf16[256,1024]{1,0:T(8,128)(2,1)S(1)}, u32[]{:S(2)}, u32[]{:S(2)}) collective-permute-start(bf16[256,1024]{1,0:T(8,128)(2,1)S(1)} %fusion), channel_id=1, source_target_pairs={{0,16},{8,24},{16,0},{24,8},{1,17},{9,25},{17,1},{25,9},{2,18},{10... | collective-permute-start | bytes 1572872 | tf_op jit(solution)/shard_map/input/seq2/ppermute | solution.py:75
  234.6 16.4 %collective-permute-start.42 = (bf16[144,1024]{1,0:T(8,128)(2,1)S(1)}, bf16[144,1024]{1,0:T(8,128)(2,1)S(1)}, u32[]{:S(2)}, u32[]{:S(2)}) collective-permute-start(bf16[144,1024]{1,0:T(8,128)(2,1)S(1)} %get-tuple-element.170), channel_id=1, source_target_pairs={{0,1},{1,0},{2,3},{3,2},{4,5},{5,4},{6,7},{7,6},{8,9},{9,8},{10,11... | collective-permute-start | bytes 884744 | tf_op jit(solution)/shard_map/gqkvo/y/ppermute | solution.py:97
  235.7 27.2 %collective-permute-start.44 = (bf16[144,1024]{1,0:T(8,128)(2,1)}, bf16[144,1024]{1,0:T(8,128)(2,1)}, u32[]{:S(2)}, u32[]{:S(2)}) collective-permute-start(bf16[144,1024]{1,0:T(8,128)(2,1)} %get-tuple-element.172), channel_id=1, source_target_pairs={{0,1},{1,0},{2,3},{3,2},{4,5},{5,4},{6,7},{7,6},{8,9},{9,8},{10,11... | collective-permute-start | bytes 884744 | tf_op jit(solution)/shard_map/gqkvo/y/ppermute | solution.py:97
  239.2 23.6 %collective-permute-start.39 = (bf16[144,1024]{1,0:T(8,128)(2,1)}, bf16[144,1024]{1,0:T(8,128)(2,1)}, u32[]{:S(2)}, u32[]{:S(2)}) collective-permute-start(bf16[144,1024]{1,0:T(8,128)(2,1)} %add_convert_fusion.7), channel_id=1, source_target_pairs={{0,2},{2,0},{4,6},{6,4},{1,3},{3,1},{5,7},{7,5},{8,10},{10,8},{12,... | collective-permute-start | bytes 884744 | tf_op jit(solution)/shard_map/gqkvo/z1/ppermute | solution.py:102
  245.4 21.4 %collective-permute-start.41 = (bf16[144,1024]{1,0:T(8,128)(2,1)}, bf16[144,1024]{1,0:T(8,128)(2,1)}, u32[]{:S(2)}, u32[]{:S(2)}) collective-permute-start(bf16[144,1024]{1,0:T(8,128)(2,1)} %add_convert_fusion.6), channel_id=1, source_target_pairs={{0,4},{2,6},{4,0},{6,2},{1,5},{3,7},{5,1},{7,3},{8,12},{10,14},{12... | collective-permute-start | bytes 884744 | tf_op jit(solution)/shard_map/gqkvo/z2/ppermute | solution.py:102
  251.7 21.4 %collective-permute-start.43 = (bf16[144,1024]{1,0:T(8,128)(2,1)}, bf16[144,1024]{1,0:T(8,128)(2,1)}, u32[]{:S(2)}, u32[]{:S(2)}) collective-permute-start(bf16[144,1024]{1,0:T(8,128)(2,1)} %add_convert_fusion.5), channel_id=1, source_target_pairs={{0,6},{2,4},{4,2},{6,0},{1,7},{3,5},{5,3},{7,1},{8,14},{10,12},{12... | collective-permute-start | bytes 884744 | tf_op jit(solution)/shard_map/gqkvo/z3/ppermute | solution.py:102
  252.9 5.7 %collective-permute-start.47 = (bf16[128,1024]{1,0:T(8,128)(2,1)S(1)}, bf16[128,1024]{1,0:T(8,128)(2,1)S(1)}, u32[]{:S(2)}, u32[]{:S(2)}) collective-permute-start(bf16[128,1024]{1,0:T(8,128)(2,1)S(1)} %copy-done.16), channel_id=1, source_target_pairs={{0,16},{8,24},{16,0},{24,8},{1,17},{9,25},{17,1},{25,9},{2,18},{10... | collective-permute-start | bytes 786440 | tf_op jit(solution)/shard_map/fdown/seq2/ppermute | solution.py:75
  258.6 25.5 %collective-permute-start.33 = (bf16[256,1024]{1,0:T(8,128)(2,1)}, bf16[256,1024]{1,0:T(8,128)(2,1)S(1)}, u32[]{:S(2)}, u32[]{:S(2)}) collective-permute-start(bf16[256,1024]{1,0:T(8,128)(2,1)} %bitcast.24), channel_id=1, source_target_pairs={{0,8},{8,0},{16,24},{24,16},{1,9},{9,1},{17,25},{25,17},{2,10},{10... | collective-permute-start | bytes 1572872 | tf_op jit(solution)/shard_map/input/seq1/ppermute | solution.py:75
  262.8 14.2 %collective-permute-start.51 = (bf16[128,1024]{1,0:T(8,128)(2,1)S(1)}, bf16[128,1024]{1,0:T(8,128)(2,1)S(1)}, u32[]{:S(2)}, u32[]{:S(2)}) collective-permute-start(bf16[128,1024]{1,0:T(8,128)(2,1)S(1)} %copy-done.16), channel_id=1, source_target_pairs={{0,8},{8,0},{16,24},{24,16},{1,9},{9,1},{17,25},{25,17},{2,10},{10... | collective-permute-start | bytes 786440 | tf_op jit(solution)/shard_map/fdown/seq1/ppermute | solution.py:75
  262.8 14.2 %collective-permute-start.49 = (bf16[128,1024]{1,0:T(8,128)(2,1)S(1)}, bf16[128,1024]{1,0:T(8,128)(2,1)S(1)}, u32[]{:S(2)}, u32[]{:S(2)}) collective-permute-start(bf16[128,1024]{1,0:T(8,128)(2,1)S(1)} %reduce_sum.12.refs_0_), channel_id=1, source_target_pairs={{0,16},{8,24},{16,0},{24,8},{1,17},{9,25},{17,1},{25,9},{2,18},{10... | collective-permute-start | bytes 786440 | tf_op jit(solution)/shard_map/fup/seq2/ppermute | solution.py:75
  274.6 7.7 %collective-permute-start.46 = (bf16[144,1024]{1,0:T(8,128)(2,1)S(1)}, bf16[144,1024]{1,0:T(8,128)(2,1)S(1)}, u32[]{:S(2)}, u32[]{:S(2)}) collective-permute-start(bf16[144,1024]{1,0:T(8,128)(2,1)S(1)} %add_convert_fusion.4.c0), channel_id=1, source_target_pairs={{0,16},{8,24},{16,0},{24,8},{1,17},{9,25},{17,1},{25,9},{2,18},{10... | collective-permute-start | bytes 884744 | tf_op jit(solution)/shard_map/small/seq2/ppermute | solution.py:75
  278.1 7.2 %collective-permute-start.45 = (bf16[144,1024]{1,0:T(8,128)(2,1)S(1)}, bf16[144,1024]{1,0:T(8,128)(2,1)S(1)}, u32[]{:S(2)}, u32[]{:S(2)}) collective-permute-start(bf16[144,1024]{1,0:T(8,128)(2,1)S(1)} %add_convert_fusion.4.c0), channel_id=1, source_target_pairs={{0,8},{8,0},{16,24},{24,16},{1,9},{9,1},{17,25},{25,17},{2,10},{10... | collective-permute-start | bytes 884744 | tf_op jit(solution)/shard_map/small/seq1/ppermute | solution.py:75
  (47 other events, 378.5 us)
Sparse Core Ops, SparseCore 0:
  25.4 74.8 all-gather.2
  152.0 69.6 reduce-scatter.1

commit v5 on v4

--- a/solution.py
+++ b/solution.py
@@ -378,6 +378,7 @@
         outs,
         (qkv, lse, *grads, wqkv),
         name="attend_back",
+        light=32,
         grid=(nb,),
         in_specs=[one((length, c3)), one((heads, length))]
         + [one((block, c))] * SEQ_N
@@ -523,6 +524,7 @@
         outs,
         args,
         name="first_norm",
+        light=32,
         in_specs=[whole(pltpu.SMEM)] + [whole()] * (len(args) - 1),
         scratch=[VMEM((rows, d), BF16), VMEM((rows, d), BF16)],
         flops=2 * rows * d * d,
@@ -545,6 +547,7 @@
         (struct((d, c), BF16),) * SEQ_N,
         (ids, mix, low),
         name="out_grads",
+        light=32,
         in_specs=[whole(pltpu.SMEM)] + [whole()] * 2,
         flops=2 * rows * d * d,
     )

time: 297 us -> 292 us (0.983)
  waiting for transfers between devices: 110 us -> 100 us
  starting transfers between devices: 69.7 us -> 76.5 us
    ppermute x6, waiting for transfers between devices: 22 us -> 14.7 us  [swap_z(): return lax.ppermute(value, 'z', [(i, i ^ k) for i in range(count)])]
    ppermute x9, waiting for transfers between devices: 22.9 us -> 16.1 us  [swap_y(): return lax.ppermute(value, 'y', [(0, 1), (1, 0)])]
    ppermute x39, starting transfers between devices: 47.3 us -> 53.9 us  [seq_swap(): return lax.ppermute(value, SEQ, [(i, i ^ k) for i in range(SEQ_N)])]
    reduce_scatter x1, waiting for transfers between devices: 0.01 us -> 5.62 us  [body(): lax.psum_scatter(down_full, FSDP, scatter_dimension=0, tiled=True)]
  transfers between devices with their start and end apart: 57 -> 57, of which waited for: 30 -> 28; matrix products, arithmetic and copies ran while one was open for 4% -> 4% of each run, Pallas kernels for 17% -> 17%
where the time goes in v5:
time: 292 us; the launch traced here: 291 us
  waiting for transfers between devices  100 us (34%)
  starting transfers between devices  76.5 us (26%)
  Pallas kernels  69.2 us (24%)
  local copies, waits for them, and re-layouts  19.5 us (7%)
  between operations  14.6 us (5%)
  other arithmetic  11.2 us (4%)
    pallas_call x15, Pallas kernels, call(): pl.pallas_call(kernel, out_shape=outs, in_specs=in_specs, out_specs=out_s...  69.2 us
    ppermute x39, waiting for transfers between devices, seq_swap(): return lax.ppermute(value, SEQ, [(i, i ^ k) for i in range(SEQ_N)])  61.7 us
    ppermute x39, starting transfers between devices, seq_swap(): return lax.ppermute(value, SEQ, [(i, i ^ k) for i in range(SEQ_N)])  53.9 us
    unnamed x83, local copies, waits for them, and re-layouts  19.5 us
    ppermute x9, waiting for transfers between devices, swap_y(): return lax.ppermute(value, 'y', [(0, 1), (1, 0)])  16.1 us
    ppermute x6, waiting for transfers between devices, swap_z(): return lax.ppermute(value, 'z', [(i, i ^ k) for i in range(count)])  14.7 us
    ppermute x9, starting transfers between devices, swap_y(): return lax.ppermute(value, 'y', [(0, 1), (1, 0)])  10.7 us
    ppermute x6, starting transfers between devices, swap_z(): return lax.ppermute(value, 'z', [(i, i ^ k) for i in range(count)])  6.83 us
  transfers between devices with their start and end apart: 57, of which 28 were waited for; matrix products, arithmetic and copies ran while one was open for 4% of the time, Pallas kernels for 17%

profile of v5, /device:TPU:13, one launch (start us, length us, event | category | flops | bytes accessed | tf_op | source)
XLA Modules:
  0.0 291.0 jit_solution(1733748409427985731)
XLA Ops:
  7.8 2.6 early_pack.1.refs_0_
  12.0 2.6 late_pack.1
  14.7 3.9 %collective-permute-done.6.refs_4_ = bf16[144,1024]{1,0:T(8,128)(2,1)S(1)} collective-permute-done((bf16[144,1024]{1,0:T(8,128)(2,1)}, bf16[144,1024]{1,0:T(8,128)(2,1)S(1)}, u32[]{:S(2)}, u32[]{:S(2)}) %collective-permute-start.6) | collective-permute-done | bytes 294944 | tf_op jit(solution)/shard_map/wqkv/y/ppermute | solution.py:97
  18.6 6.7 %collective-permute-done.5.refs_3_ = bf16[144,1024]{1,0:T(8,128)(2,1)S(1)} collective-permute-done((bf16[144,1024]{1,0:T(8,128)(2,1)}, bf16[144,1024]{1,0:T(8,128)(2,1)S(1)}, u32[]{:S(2)}, u32[]{:S(2)}) %collective-permute-start.5) | collective-permute-done | bytes 294944 | tf_op jit(solution)/shard_map/wqkv/z3/ppermute | solution.py:102
  25.4 2.0 collective-permute-start.3
  28.6 2.7 collective-permute-start
  32.7 5.0 %collective-permute-done.4.refs_2_ = bf16[144,1024]{1,0:T(8,128)(2,1)S(1)} collective-permute-done((bf16[144,1024]{1,0:T(8,128)(2,1)S(1)}, bf16[144,1024]{1,0:T(8,128)(2,1)S(1)}, u32[]{:S(2)}, u32[]{:S(2)}) %collective-permute-start.4) | collective-permute-done | bytes 294944 | tf_op jit(solution)/shard_map/wqkv/z2/ppermute | solution.py:102
  37.7 2.3 collective-permute-start.8
  41.3 2.4 collective-permute-start.7
  43.8 7.7 %collective-permute-start.2 = (bf16[2,128,1024]{2,1,0:T(8,128)(2,1)S(1)}, bf16[2,128,1024]{2,1,0:T(8,128)(2,1)S(1)}, u32[]{:S(2)}, u32[]{:S(2)}) collective-permute-start(bf16[2,128,1024]{2,1,0:T(8,128)(2,1)S(1)} %collective-permute-done.1.x2), channel_id=1, source_target_pairs={{0,8},{8,0},{16,24},{24,16},{1,9},{9,1},{17,25},{25,17},{2,10},{10... | collective-permute-start | bytes 1572872 | tf_op jit(solution)/shard_map/tok/seq1/ppermute | solution.py:75
  51.5 4.0 %collective-permute-done.7.refs_5_ = bf16[144,1024]{1,0:T(8,128)(2,1)S(1)} collective-permute-done((bf16[144,1024]{1,0:T(8,128)(2,1)S(1)}, bf16[144,1024]{1,0:T(8,128)(2,1)S(1)}, u32[]{:S(2)}, u32[]{:S(2)}) %collective-permute-start.7) | collective-permute-done | bytes 294944 | tf_op jit(solution)/shard_map/wqkv/y/ppermute | solution.py:97
  55.7 4.1 %collective-permute-start.13 = (bf16[8,128,256]{2,1,0:T(8,128)(2,1)S(1)}, bf16[8,128,256]{2,1,0:T(8,128)(2,1)S(1)}, u32[]{:S(2)}, u32[]{:S(2)}) collective-permute-start(bf16[8,128,256]{2,1,0:T(8,128)(2,1)S(1)} %fusion.3.w0), channel_id=1, source_target_pairs={{0,8},{8,0},{16,24},{24,16},{1,9},{9,1},{17,25},{25,17},{2,10},{10... | collective-permute-start | bytes 1572872 | tf_op jit(solution)/shard_map/wo/seq1/ppermute | solution.py:75
  59.8 8.2 %attend.1 = (bf16[2,512,768]{2,1,0:T(8,128)(2,1)S(1)}, f32[2,4,512]{2,1,0:T(4,128)S(1)}, bf16[2,128,256]{2,1,0:T(8,128)(2,1)S(1)}, bf16[2,128,256]{2,1,0:T(8,128...) custom-call(s32[2]{0:T(128)S(1)} %copy-done.19, ...), custom_call_target="tpu_custom_call" | custom-call | flops 2147483648 | bytes 8208392 | tf_op jit(solution)/shard_map/attend/pallas_call | solution.py:56
  72.2 2.5 collective-permute-done.11.m2
  74.7 3.8 %collective-permute-done.12.m3 = bf16[256,256]{1,0:T(8,128)(2,1)S(1)} collective-permute-done((bf16[256,256]{1,0:T(8,128)(2,1)S(1)}, bf16[256,256]{1,0:T(8,128)(2,1)S(1)}, u32[]{:S(2)}, u32[]{:S(2)}) %collective-permute-start.12) | collective-permute-done | bytes 131104 | tf_op jit(solution)/shard_map/mix/seq3/ppermute | solution.py:75
  78.4 2.3 out_project.1
  84.3 12.0 %collective-permute-done.17.f2 = bf16[256,1024]{1,0:T(8,128)(2,1)S(1)} collective-permute-done((bf16[256,1024]{1,0:T(8,128)(2,1)S(1)}, bf16[256,1024]{1,0:T(8,128)(2,1)S(1)}, u32[]{:S(2)}, u32[]{:S(2)}) %collective-permute-start.17) | collective-permute-done | bytes 524320 | tf_op jit(solution)/shard_map/first/seq2/ppermute | solution.py:75
  98.4 1.9 all-gather.3.cloned.1.call-done
  101.3 9.6 %ffn.1 = (bf16[256,1024]{1,0:T(8,128)(2,1)S(1)}, bf16[256,1024]{1,0:T(8,128)(2,1)S(1)}, bf16[256,1024]{1,0:T(8,128)(2,1)S(1)}, bf16[256,1024]{1,0:T(8,128)(2,1)S...) custom-call(s32[2]{0:T(128)S(1)} %copy-done.19, bf16[256,1024]{1,0:T(8,128)(2,1)S(1)} %copy-done.6, ...), custom_call_target="tpu_custom_call" | custom-call | flops 4294967296 | bytes 12648456 | tf_op jit(solution)/shard_map/ffn/pallas_call | solution.py:56
  111.0 1.8 collective-permute-start.19
  112.8 1.5 collective-permute-done.19
  116.5 11.8 %collective-permute-done.21.p2 = bf16[256,1024]{1,0:T(8,128)(2,1)S(1)} collective-permute-done((bf16[256,1024]{1,0:T(8,128)(2,1)S(1)}, bf16[256,1024]{1,0:T(8,128)(2,1)S(1)}, u32[]{:S(2)}, u32[]{:S(2)}) %collective-permute-start.21) | collective-permute-done | bytes 524320 | tf_op jit(solution)/shard_map/ffn/seq2/ppermute | solution.py:75
  128.3 1.7 second_norm.1
  133.4 10.1 %collective-permute-done.23.d2 = bf16[256,1024]{1,0:T(8,128)(2,1)S(1)} collective-permute-done((bf16[256,1024]{1,0:T(8,128)(2,1)S(1)}, bf16[256,1024]{1,0:T(8,128)(2,1)S(1)}, u32[]{:S(2)}, u32[]{:S(2)}) %collective-permute-start.23) | collective-permute-done | bytes 524320 | tf_op jit(solution)/shard_map/low/seq2/ppermute | solution.py:75
  143.4 1.9 collective-permute-start.24
  146.8 3.4 %down_grads.1 = bf16[1024,1024]{1,0:T(8,128)(2,1)} custom-call(bf16[1024,1024]{1,0:T(8,128)(2,1)S(1)} %get-tuple-element.122.gelu, bf16[256,1024]{1,0:T(8,128)(2,1)S(1)} %get-tuple-element.120.d0, bf16[256,1024]{1,0:T(8,128)(2,1)S(1)} %collective-permute-done.22.d1, bf16[256,1024]{1,0:T(8,128)(2,1)S(1)} %collective-permute-done.23.d2, ...), custom_call_target="tpu_custom_call" | custom-call | flops 67108864 | bytes 196608 | tf_op jit(solution)/shard_map/down_grads/pallas_call | solution.py:56
  155.0 2.2 copy-done.20
  157.2 1.6 copy-done.33
  158.8 6.3 %ffn_back.1 = (bf16[256,1024]{1,0:T(8,128)(2,1)S(1)}, bf16[256,1024]{1,0:T(8,128)(2,1)S(1)}, bf16[256,1024]{1,0:T(8,128)(2,1)S(1)}, bf16[256,1024]{1,0:T(8,128)(...) custom-call(s32[2]{0:T(128)S(1)} %copy-done.19, bf16[256,1024]{1,0:T(8,128)(2,1)S(1)} %copy-done.8, ...), custom_call_target="tpu_custom_call" | custom-call | flops 4294967296 | bytes 12615688 | tf_op jit(solution)/shard_map/ffn_back/pallas_call | solution.py:56
  169.3 4.9 %up_grads.1 = (bf16[4,128,1024]{2,1,0:T(8,128)(2,1)S(1)}, bf16[4,128,1024]{2,1,0:T(8,128)(2,1)S(1)}) custom-call(s32[2]{0:T(128)S(1)} %copy-done.19, bf16[256,1024]{1,0:T(8,128)(2,1)} %copy-done.5, bf16[256,1024]{1,0:T(8,128)(2,1)} %copy-done.37, bf16[256,1024]{1,0:T(8,128)(2,1)} %copy-done.36, bf16[256,1024]{1,0:T(8,128)(2,1)} %collective-permute-done.18.f3, ...), custom_call_target="tpu_custom_call" | custom-call | flops 67108864 | bytes 196608 | tf_op jit(solution)/shard_map/up_grads/pallas_call | solution.py:56
  175.6 5.7 %collective-permute-done.27.p2 = bf16[256,1024]{1,0:T(8,128)(2,1)S(1)} collective-permute-done((bf16[256,1024]{1,0:T(8,128)(2,1)S(1)}, bf16[256,1024]{1,0:T(8,128)(2,1)S(1)}, u32[]{:S(2)}, u32[]{:S(2)}) %collective-permute-start.27) | collective-permute-done | bytes 524320 | tf_op jit(solution)/shard_map/ffnback/seq2/ppermute | solution.py:75
  181.3 2.2 first_norm.1
  188.8 1.6 collective-permute-done.30
  190.4 3.7 %collective-permute-done.31 = bf16[256,256]{1,0:T(8,128)(2,1)S(1)} collective-permute-done((bf16[256,256]{1,0:T(8,128)(2,1)S(1)}, bf16[256,256]{1,0:T(8,128)(2,1)S(1)}, u32[]{:S(2)}, u32[]{:S(2)}) %collective-permute-start.31) | collective-permute-done | bytes 131104 | tf_op jit(solution)/shard_map/mixback/seq3/ppermute | solution.py:75
  195.4 13.3 %attend_back.1 = (bf16[2,512,768]{2,1,0:T(8,128)(2,1)S(1)}, f32[8,768]{1,0:T(8,128)S(1)}, bf16[2,128,1024]{2,1,0:T(8,128)(2,1)S(1)}, bf16[2,128,1024]{2,1,0:T(8,...) custom-call(bf16[2,512,768]{2,1,0:T(8,128)(2,1)S(1)} %copy-done.31, ...), custom_call_target="tpu_custom_call" | custom-call | flops 92274688 | bytes 230656 | tf_op jit(solution)/shard_map/attend_back/pallas_call | solution.py:56
  212.0 5.0 %all-to-all-start = ((bf16[4,128,1024]{2,1,0:T(8,128)(2,1)}), bf16[4,128,1024]{2,1,0:T(8,128)(2,1)}, u32[]{:S(2)}, u32[]{:S(2)}) async-start(bf16[4,128,1024]{2,1,0:T(8,128)(2,1)} %add_convert_fusion), calls=%async_computation.1 | async-start | bytes 2097152 | tf_op jit(solution)/shard_map/gup/z/all_to_all | solution.py:107
  217.0 5.6 %reduce-scatter.2.cloned.1.call-done.refs_4_ = bf16[128,1024]{1,0:T(8,128)(2,1)} async-done(((bf16[1024,1024]{1,0:T(8,128)(2,1)}), bf16[128,1024]{1,0:T(8,128)(2,1)}) %reduce-scatter.2.cloned.1.call-update) | async-done | bytes 262160 | tf_op jit(solution)/shard_map/gdown/reduce_scatter | solution.py:973
  225.1 5.9 %qkvo_grads.1 = (bf16[144,1024]{1,0:T(8,128)(2,1)S(1)}, bf16[144,1024]{1,0:T(8,128)(2,1)S(1)}, bf16[144,1024]{1,0:T(8,128)(2,1)S(1)}, bf16[144,1024]{1,0:T(8,128...) custom-call(s32[2]{0:T(128)S(1)} %copy-done.19, ...), custom_call_target="tpu_custom_call" | custom-call | flops 1610612736 | bytes 7725064 | tf_op jit(solution)/shard_map/qkvo_grads/pallas_call | solution.py:56
  239.3 3.7 %collective-permute-done.40 = bf16[144,1024]{1,0:T(8,128)(2,1)S(1)} collective-permute-done((bf16[144,1024]{1,0:T(8,128)(2,1)S(1)}, bf16[144,1024]{1,0:T(8,128)(2,1)S(1)}, u32[]{:S(2)}, u32[]{:S(2)}) %collective-permute-start.40) | collective-permute-done | bytes 294944 | tf_op jit(solution)/shard_map/gqkvo/y/ppermute | solution.py:97
  243.8 1.6 collective-permute-start.41
  245.4 3.9 %collective-permute-done.42 = bf16[144,1024]{1,0:T(8,128)(2,1)S(1)} collective-permute-done((bf16[144,1024]{1,0:T(8,128)(2,1)S(1)}, bf16[144,1024]{1,0:T(8,128)(2,1)S(1)}, u32[]{:S(2)}, u32[]{:S(2)}) %collective-permute-start.42) | collective-permute-done | bytes 294944 | tf_op jit(solution)/shard_map/gqkvo/y/ppermute | solution.py:97
  252.5 3.6 %collective-permute-done.47.refs_6_ = bf16[128,1024]{1,0:T(8,128)(2,1)S(1)} collective-permute-done((bf16[128,1024]{1,0:T(8,128)(2,1)S(1)}, bf16[128,1024]{1,0:T(8,128)(2,1)S(1)}, u32[]{:S(2)}, u32[]{:S(2)}) %collective-permute-start.47) | collective-permute-done | bytes 262176 | tf_op jit(solution)/shard_map/fdown/seq2/ppermute | solution.py:75
  256.2 8.1 %collective-permute-start.33 = (bf16[256,1024]{1,0:T(8,128)(2,1)}, bf16[256,1024]{1,0:T(8,128)(2,1)S(1)}, u32[]{:S(2)}, u32[]{:S(2)}) collective-permute-start(bf16[256,1024]{1,0:T(8,128)(2,1)} %bitcast.24), channel_id=1, source_target_pairs={{0,8},{8,0},{16,24},{24,16},{1,9},{9,1},{17,25},{25,17},{2,10},{10... | collective-permute-start | bytes 1572872 | tf_op jit(solution)/shard_map/input/seq1/ppermute | solution.py:75
  264.3 1.8 collective-permute-start.49
  266.1 1.8 collective-permute-done.43
  269.8 5.3 %collective-permute-start.48 = (bf16[128,1024]{1,0:T(8,128)(2,1)S(1)}, bf16[128,1024]{1,0:T(8,128)(2,1)S(1)}, u32[]{:S(2)}, u32[]{:S(2)}) collective-permute-start(bf16[128,1024]{1,0:T(8,128)(2,1)S(1)} %reduce_sum.12.refs_0_), channel_id=1, source_target_pairs={{0,8},{8,0},{16,24},{24,16},{1,9},{9,1},{17,25},{25,17},{2,10},{10... | collective-permute-start | bytes 786440 | tf_op jit(solution)/shard_map/fup/seq1/ppermute | solution.py:75
  277.1 3.0 %finish_ffn.1 = (f32[128,4096]{1,0:T(8,128)}, f32[512,1024]{1,0:T(8,128)}) custom-call(s32[2]{0:T(128)S(1)} %copy-done.19, bf16[128,1024]{1,0:T(8,128)(2,1)S(1)} %reduce_sum.12.refs_0_, bf16[128,1024]{1,0:T(8,128)(2,1)S(1)} %collective-permute-done.48.refs_1_, bf16[128,1024]{1,0:T(8,128)(2,1)S(1)} %collective-permute-done.49.refs_2_, ...), custom_call_target="tpu_custom_call" | custom-call | bytes 6291464 | tf_op jit(solution)/shard_map/finish_ffn/pallas_call | solution.py:56
  282.1 2.0 finish_qkvo.1
  (179 shorter events, 64.9 us)
Async XLA Ops:
  7.2 93.1 %all-gather.3.cloned.1.call-start = ((), (), s32[]{:S(2)}) async-start(), calls=%async_computation.3 | async-start | bytes 4718592 | tf_op jit(solution)/shard_map/ffnw/all_gather | solution.py:952
  10.4 8.2 %collective-permute-start.6 = (bf16[144,1024]{1,0:T(8,128)(2,1)}, bf16[144,1024]{1,0:T(8,128)(2,1)S(1)}, u32[]{:S(2)}, u32[]{:S(2)}) collective-permute-start(bf16[144,1024]{1,0:T(8,128)(2,1)} %early_pack.1.refs_0_), channel_id=1, source_target_pairs={{0,1},{1,0},{2,3},{3,2},{4,5},{5,4},{6,7},{7,6},{8,9},{9,8},{10,11... | collective-permute-start | bytes 884744 | tf_op jit(solution)/shard_map/wqkv/y/ppermute | solution.py:97
  10.7 14.5 %collective-permute-start.5 = (bf16[144,1024]{1,0:T(8,128)(2,1)}, bf16[144,1024]{1,0:T(8,128)(2,1)S(1)}, u32[]{:S(2)}, u32[]{:S(2)}) collective-permute-start(bf16[144,1024]{1,0:T(8,128)(2,1)} %early_pack.1.refs_0_), channel_id=1, source_target_pairs={{0,6},{2,4},{4,2},{6,0},{1,7},{3,5},{5,3},{7,1},{8,14},{10,12},{12... | collective-permute-start | bytes 884744 | tf_op jit(solution)/shard_map/wqkv/z3/ppermute | solution.py:102
  25.3 197.4 %reduce-scatter.2.cloned.1.call-start = ((), (), s32[]{:S(2)}) async-start(), calls=%async_computation.2 | async-start | bytes 2359296 | tf_op jit(solution)/shard_map/gdown/reduce_scatter | solution.py:973
  25.3 12.4 %collective-permute-start.4 = (bf16[144,1024]{1,0:T(8,128)(2,1)S(1)}, bf16[144,1024]{1,0:T(8,128)(2,1)S(1)}, u32[]{:S(2)}, u32[]{:S(2)}) collective-permute-start(bf16[144,1024]{1,0:T(8,128)(2,1)S(1)} %copy-done.17), channel_id=1, source_target_pairs={{0,4},{2,6},{4,0},{6,2},{1,5},{3,7},{5,1},{7,3},{8,12},{10,14},{12... | collective-permute-start | bytes 884744 | tf_op jit(solution)/shard_map/wqkv/z2/ppermute | solution.py:102
  25.4 15.9 %collective-permute-start.3 = (bf16[144,1024]{1,0:T(8,128)(2,1)S(1)}, bf16[144,1024]{1,0:T(8,128)(2,1)S(1)}, u32[]{:S(2)}, u32[]{:S(2)}) collective-permute-start(bf16[144,1024]{1,0:T(8,128)(2,1)S(1)} %copy-done.17), channel_id=1, source_target_pairs={{0,2},{2,0},{4,6},{6,4},{1,3},{3,1},{5,7},{7,5},{8,10},{10,8},{12,... | collective-permute-start | bytes 884744 | tf_op jit(solution)/shard_map/wqkv/z1/ppermute | solution.py:102
  27.4 16.3 %collective-permute-start.1 = (bf16[2,128,1024]{2,1,0:T(8,128)(2,1)S(1)}, bf16[2,128,1024]{2,1,0:T(8,128)(2,1)S(1)}, u32[]{:S(2)}, u32[]{:S(2)}) collective-permute-start(bf16[2,128,1024]{2,1,0:T(8,128)(2,1)S(1)} %copy-done.15), channel_id=1, source_target_pairs={{0,16},{8,24},{16,0},{24,8},{1,17},{9,25},{17,1},{25,9},{2,18},{10... | collective-permute-start | bytes 1572872 | tf_op jit(solution)/shard_map/tok/seq2/ppermute | solution.py:75
  28.6 31.2 %collective-permute-start = (bf16[2,128,1024]{2,1,0:T(8,128)(2,1)S(1)}, bf16[2,128,1024]{2,1,0:T(8,128)(2,1)S(1)}, u32[]{:S(2)}, u32[]{:S(2)}) collective-permute-start(bf16[2,128,1024]{2,1,0:T(8,128)(2,1)S(1)} %copy-done.15), channel_id=1, source_target_pairs={{0,8},{8,0},{16,24},{24,16},{1,9},{9,1},{17,25},{25,17},{2,10},{10... | collective-permute-start | bytes 1572872 | tf_op jit(solution)/shard_map/tok/seq1/ppermute | solution.py:75
  31.4 24.2 %collective-permute-start.9 = (bf16[144,1024]{1,0:T(8,128)(2,1)S(1)}, bf16[144,1024]{1,0:T(8,128)(2,1)S(1)}, u32[]{:S(2)}, u32[]{:S(2)}) collective-permute-start(bf16[144,1024]{1,0:T(8,128)(2,1)S(1)} %collective-permute-done.5.refs_3_), channel_id=1, source_target_pairs={{0,1},{1,0},{2,3},{3,2},{4,5},{5,4},{6,7},{7,6},{8,9},{9,8},{10,11... | collective-permute-start | bytes 884744 | tf_op jit(solution)/shard_map/wqkv/y/ppermute | solution.py:97
  37.7 17.9 %collective-permute-start.8 = (bf16[144,1024]{1,0:T(8,128)(2,1)S(1)}, bf16[144,1024]{1,0:T(8,128)(2,1)S(1)}, u32[]{:S(2)}, u32[]{:S(2)}) collective-permute-start(bf16[144,1024]{1,0:T(8,128)(2,1)S(1)} %collective-permute-done.4.refs_2_), channel_id=1, source_target_pairs={{0,1},{1,0},{2,3},{3,2},{4,5},{5,4},{6,7},{7,6},{8,9},{9,8},{10,11... | collective-permute-start | bytes 884744 | tf_op jit(solution)/shard_map/wqkv/y/ppermute | solution.py:97
  41.3 14.3 %collective-permute-start.7 = (bf16[144,1024]{1,0:T(8,128)(2,1)S(1)}, bf16[144,1024]{1,0:T(8,128)(2,1)S(1)}, u32[]{:S(2)}, u32[]{:S(2)}) collective-permute-start(bf16[144,1024]{1,0:T(8,128)(2,1)S(1)} %collective-permute-done.3.refs_1_), channel_id=1, source_target_pairs={{0,1},{1,0},{2,3},{3,2},{4,5},{5,4},{6,7},{7,6},{8,9},{9,8},{10,11... | collective-permute-start | bytes 884744 | tf_op jit(solution)/shard_map/wqkv/y/ppermute | solution.py:97
  43.8 16.0 %collective-permute-start.2 = (bf16[2,128,1024]{2,1,0:T(8,128)(2,1)S(1)}, bf16[2,128,1024]{2,1,0:T(8,128)(2,1)S(1)}, u32[]{:S(2)}, u32[]{:S(2)}) collective-permute-start(bf16[2,128,1024]{2,1,0:T(8,128)(2,1)S(1)} %collective-permute-done.1.x2), channel_id=1, source_target_pairs={{0,8},{8,0},{16,24},{24,16},{1,9},{9,1},{17,25},{25,17},{2,10},{10... | collective-permute-start | bytes 1572872 | tf_op jit(solution)/shard_map/tok/seq1/ppermute | solution.py:75
  55.6 13.6 %collective-permute-start.14 = (bf16[8,128,256]{2,1,0:T(8,128)(2,1)S(1)}, bf16[8,128,256]{2,1,0:T(8,128)(2,1)S(1)}, u32[]{:S(2)}, u32[]{:S(2)}) collective-permute-start(bf16[8,128,256]{2,1,0:T(8,128)(2,1)S(1)} %fusion.3.w0), channel_id=1, source_target_pairs={{0,16},{8,24},{16,0},{24,8},{1,17},{9,25},{17,1},{25,9},{2,18},{10... | collective-permute-start | bytes 1572872 | tf_op jit(solution)/shard_map/wo/seq2/ppermute | solution.py:75
  55.7 16.5 %collective-permute-start.13 = (bf16[8,128,256]{2,1,0:T(8,128)(2,1)S(1)}, bf16[8,128,256]{2,1,0:T(8,128)(2,1)S(1)}, u32[]{:S(2)}, u32[]{:S(2)}) collective-permute-start(bf16[8,128,256]{2,1,0:T(8,128)(2,1)S(1)} %fusion.3.w0), channel_id=1, source_target_pairs={{0,8},{8,0},{16,24},{24,16},{1,9},{9,1},{17,25},{25,17},{2,10},{10... | collective-permute-start | bytes 1572872 | tf_op jit(solution)/shard_map/wo/seq1/ppermute | solution.py:75
  69.2 9.2 %collective-permute-start.15 = (bf16[8,128,256]{2,1,0:T(8,128)(2,1)S(1)}, bf16[8,128,256]{2,1,0:T(8,128)(2,1)S(1)}, u32[]{:S(2)}, u32[]{:S(2)}) collective-permute-start(bf16[8,128,256]{2,1,0:T(8,128)(2,1)S(1)} %collective-permute-done.14.w2), channel_id=1, source_target_pairs={{0,8},{8,0},{16,24},{24,16},{1,9},{9,1},{17,25},{25,17},{2,10},{10... | collective-permute-start | bytes 1572872 | tf_op jit(solution)/shard_map/wo/seq1/ppermute | solution.py:75
  70.0 4.7 %collective-permute-start.11 = (bf16[256,256]{1,0:T(8,128)(2,1)S(1)}, bf16[256,256]{1,0:T(8,128)(2,1)S(1)}, u32[]{:S(2)}, u32[]{:S(2)}) collective-permute-start(bf16[256,256]{1,0:T(8,128)(2,1)S(1)} %bitcast.66), channel_id=1, source_target_pairs={{0,16},{8,24},{16,0},{24,8},{1,17},{9,25},{17,1},{25,9},{2,18},{10... | collective-permute-start | bytes 393224 | tf_op jit(solution)/shard_map/mix/seq2/ppermute | solution.py:75
  70.9 7.5 %collective-permute-start.12 = (bf16[256,256]{1,0:T(8,128)(2,1)S(1)}, bf16[256,256]{1,0:T(8,128)(2,1)S(1)}, u32[]{:S(2)}, u32[]{:S(2)}) collective-permute-start(bf16[256,256]{1,0:T(8,128)(2,1)S(1)} %bitcast.64), channel_id=1, source_target_pairs={{0,24},{8,16},{16,8},{24,0},{1,25},{9,17},{17,9},{25,1},{2,26},{10... | collective-permute-start | bytes 393224 | tf_op jit(solution)/shard_map/mix/seq3/ppermute | solution.py:75
  82.5 13.8 %collective-permute-start.17 = (bf16[256,1024]{1,0:T(8,128)(2,1)S(1)}, bf16[256,1024]{1,0:T(8,128)(2,1)S(1)}, u32[]{:S(2)}, u32[]{:S(2)}) collective-permute-start(bf16[256,1024]{1,0:T(8,128)(2,1)S(1)} %get-tuple-element.111.f0), channel_id=1, source_target_pairs={{0,16},{8,24},{16,0},{24,8},{1,17},{9,25},{17,1},{25,9},{2,18},{10... | collective-permute-start | bytes 1572872 | tf_op jit(solution)/shard_map/first/seq2/ppermute | solution.py:75
  83.4 13.0 %collective-permute-start.16 = (bf16[256,1024]{1,0:T(8,128)(2,1)S(1)}, bf16[256,1024]{1,0:T(8,128)(2,1)S(1)}, u32[]{:S(2)}, u32[]{:S(2)}) collective-permute-start(bf16[256,1024]{1,0:T(8,128)(2,1)S(1)} %get-tuple-element.111.f0), channel_id=1, source_target_pairs={{0,8},{8,0},{16,24},{24,16},{1,9},{9,1},{17,25},{25,17},{2,10},{10... | collective-permute-start | bytes 1572872 | tf_op jit(solution)/shard_map/first/seq1/ppermute | solution.py:75
  111.0 3.3 %collective-permute-start.19 = (bf16[256,1024]{1,0:T(8,128)(2,1)S(1)}, bf16[256,1024]{1,0:T(8,128)(2,1)S(1)}, u32[]{:S(2)}, u32[]{:S(2)}) collective-permute-start(bf16[256,1024]{1,0:T(8,128)(2,1)S(1)} %get-tuple-element.116), channel_id=1, source_target_pairs={{0,8},{8,0},{16,24},{24,16},{1,9},{9,1},{17,25},{25,17},{2,10},{10... | collective-permute-start | bytes 1572872 | tf_op jit(solution)/shard_map/ffn/seq1/ppermute | solution.py:75
  114.9 13.4 %collective-permute-start.21 = (bf16[256,1024]{1,0:T(8,128)(2,1)S(1)}, bf16[256,1024]{1,0:T(8,128)(2,1)S(1)}, u32[]{:S(2)}, u32[]{:S(2)}) collective-permute-start(bf16[256,1024]{1,0:T(8,128)(2,1)S(1)} %add_convert_fusion.3), channel_id=1, source_target_pairs={{0,16},{8,24},{16,0},{24,8},{1,17},{9,25},{17,1},{25,9},{2,18},{10... | collective-permute-start | bytes 1572872 | tf_op jit(solution)/shard_map/ffn/seq2/ppermute | solution.py:75
  131.0 12.5 %collective-permute-start.23 = (bf16[256,1024]{1,0:T(8,128)(2,1)S(1)}, bf16[256,1024]{1,0:T(8,128)(2,1)S(1)}, u32[]{:S(2)}, u32[]{:S(2)}) collective-permute-start(bf16[256,1024]{1,0:T(8,128)(2,1)S(1)} %get-tuple-element.120.d0), channel_id=1, source_target_pairs={{0,16},{8,24},{16,0},{24,8},{1,17},{9,25},{17,1},{25,9},{2,18},{10... | collective-permute-start | bytes 1572872 | tf_op jit(solution)/shard_map/low/seq2/ppermute | solution.py:75
  132.1 13.2 %collective-permute-start.22 = (bf16[256,1024]{1,0:T(8,128)(2,1)S(1)}, bf16[256,1024]{1,0:T(8,128)(2,1)S(1)}, u32[]{:S(2)}, u32[]{:S(2)}) collective-permute-start(bf16[256,1024]{1,0:T(8,128)(2,1)S(1)} %get-tuple-element.120.d0), channel_id=1, source_target_pairs={{0,8},{8,0},{16,24},{24,16},{1,9},{9,1},{17,25},{25,17},{2,10},{10... | collective-permute-start | bytes 1572872 | tf_op jit(solution)/shard_map/low/seq1/ppermute | solution.py:75
  143.4 3.4 %collective-permute-start.24 = (bf16[256,1024]{1,0:T(8,128)(2,1)S(1)}, bf16[256,1024]{1,0:T(8,128)(2,1)S(1)}, u32[]{:S(2)}, u32[]{:S(2)}) collective-permute-start(bf16[256,1024]{1,0:T(8,128)(2,1)S(1)} %collective-permute-done.23.d2), channel_id=1, source_target_pairs={{0,8},{8,0},{16,24},{24,16},{1,9},{9,1},{17,25},{25,17},{2,10},{10... | collective-permute-start | bytes 1572872 | tf_op jit(solution)/shard_map/low/seq1/ppermute | solution.py:75
  167.8 13.5 %collective-permute-start.27 = (bf16[256,1024]{1,0:T(8,128)(2,1)S(1)}, bf16[256,1024]{1,0:T(8,128)(2,1)S(1)}, u32[]{:S(2)}, u32[]{:S(2)}) collective-permute-start(bf16[256,1024]{1,0:T(8,128)(2,1)S(1)} %add_convert_fusion.2), channel_id=1, source_target_pairs={{0,16},{8,24},{16,0},{24,8},{1,17},{9,25},{17,1},{25,9},{2,18},{10... | collective-permute-start | bytes 1572872 | tf_op jit(solution)/shard_map/ffnback/seq2/ppermute | solution.py:75
  174.2 36.4 %collective-permute-start.35 = (bf16[4,128,1024]{2,1,0:T(8,128)(2,1)S(1)}, bf16[4,128,1024]{2,1,0:T(8,128)(2,1)S(1)}, u32[]{:S(2)}, u32[]{:S(2)}) collective-permute-start(bf16[4,128,1024]{2,1,0:T(8,128)(2,1)S(1)} %get-tuple-element.154), channel_id=1, source_target_pairs={{0,1},{1,0},{2,3},{3,2},{4,5},{5,4},{6,7},{7,6},{8,9},{9,8},{10,11... | collective-permute-start | bytes 3145736 | tf_op jit(solution)/shard_map/gup/y/ppermute | solution.py:97
  185.7 9.7 %collective-permute-start.29 = (bf16[256,256]{1,0:T(8,128)(2,1)S(1)}, bf16[256,256]{1,0:T(8,128)(2,1)S(1)}, u32[]{:S(2)}, u32[]{:S(2)}) collective-permute-start(bf16[256,256]{1,0:T(8,128)(2,1)S(1)} %get-tuple-element.144), channel_id=1, source_target_pairs={{0,8},{8,0},{16,24},{24,16},{1,9},{9,1},{17,25},{25,17},{2,10},{10... | collective-permute-start | bytes 393224 | tf_op jit(solution)/shard_map/mixback/seq1/ppermute | solution.py:75
  185.8 4.6 %collective-permute-start.30 = (bf16[256,256]{1,0:T(8,128)(2,1)S(1)}, bf16[256,256]{1,0:T(8,128)(2,1)S(1)}, u32[]{:S(2)}, u32[]{:S(2)}) collective-permute-start(bf16[256,256]{1,0:T(8,128)(2,1)S(1)} %get-tuple-element.145), channel_id=1, source_target_pairs={{0,16},{8,24},{16,0},{24,8},{1,17},{9,25},{17,1},{25,9},{2,18},{10... | collective-permute-start | bytes 393224 | tf_op jit(solution)/shard_map/mixback/seq2/ppermute | solution.py:75
  187.0 7.2 %collective-permute-start.31 = (bf16[256,256]{1,0:T(8,128)(2,1)S(1)}, bf16[256,256]{1,0:T(8,128)(2,1)S(1)}, u32[]{:S(2)}, u32[]{:S(2)}) collective-permute-start(bf16[256,256]{1,0:T(8,128)(2,1)S(1)} %get-tuple-element.146), channel_id=1, source_target_pairs={{0,24},{8,16},{16,8},{24,0},{1,25},{9,17},{17,9},{25,1},{2,26},{10... | collective-permute-start | bytes 393224 | tf_op jit(solution)/shard_map/mixback/seq3/ppermute | solution.py:75
  194.1 28.6 %collective-permute-start.36 = (bf16[1024,256]{1,0:T(8,128)(2,1)S(1)}, bf16[1024,256]{1,0:T(8,128)(2,1)}, u32[]{:S(2)}, u32[]{:S(2)}) collective-permute-start(bf16[1024,256]{1,0:T(8,128)(2,1)S(1)} %get-tuple-element.159), channel_id=1, source_target_pairs={{0,8},{8,0},{16,24},{24,16},{1,9},{9,1},{17,25},{25,17},{2,10},{10... | collective-permute-start | bytes 1572872 | tf_op jit(solution)/shard_map/outs/seq1/ppermute | solution.py:75
  194.1 28.6 %collective-permute-start.37 = (bf16[1024,256]{1,0:T(8,128)(2,1)}, bf16[1024,256]{1,0:T(8,128)(2,1)}, u32[]{:S(2)}, u32[]{:S(2)}) collective-permute-start(bf16[1024,256]{1,0:T(8,128)(2,1)} %add_convert_fusion.1), channel_id=1, source_target_pairs={{0,16},{8,24},{16,0},{24,8},{1,17},{9,25},{17,1},{25,9},{2,18},{10... | collective-permute-start | bytes 1572872 | tf_op jit(solution)/shard_map/outs/seq2/ppermute | solution.py:75
  209.9 22.7 %collective-permute-start.32 = (bf16[256,1024]{1,0:T(8,128)(2,1)}, bf16[256,1024]{1,0:T(8,128)(2,1)}, u32[]{:S(2)}, u32[]{:S(2)}) collective-permute-start(bf16[256,1024]{1,0:T(8,128)(2,1)} %bitcast.26), channel_id=1, source_target_pairs={{0,8},{8,0},{16,24},{24,16},{1,9},{9,1},{17,25},{25,17},{2,10},{10... | collective-permute-start | bytes 1572872 | tf_op jit(solution)/shard_map/input/seq1/ppermute | solution.py:75
  212.0 39.1 %all-to-all-start = ((bf16[4,128,1024]{2,1,0:T(8,128)(2,1)}), bf16[4,128,1024]{2,1,0:T(8,128)(2,1)}, u32[]{:S(2)}, u32[]{:S(2)}) async-start(bf16[4,128,1024]{2,1,0:T(8,128)(2,1)} %add_convert_fusion), calls=%async_computation.1 | async-start | bytes 2097152 | tf_op jit(solution)/shard_map/gup/z/all_to_all | solution.py:107
  231.0 6.0 %collective-permute-start.38 = (bf16[144,1024]{1,0:T(8,128)(2,1)S(1)}, bf16[144,1024]{1,0:T(8,128)(2,1)S(1)}, u32[]{:S(2)}, u32[]{:S(2)}) collective-permute-start(bf16[144,1024]{1,0:T(8,128)(2,1)S(1)} %get-tuple-element.166), channel_id=1, source_target_pairs={{0,1},{1,0},{2,3},{3,2},{4,5},{5,4},{6,7},{7,6},{8,9},{9,8},{10,11... | collective-permute-start | bytes 884744 | tf_op jit(solution)/shard_map/gqkvo/y/ppermute | solution.py:97
  231.1 11.9 %collective-permute-start.40 = (bf16[144,1024]{1,0:T(8,128)(2,1)S(1)}, bf16[144,1024]{1,0:T(8,128)(2,1)S(1)}, u32[]{:S(2)}, u32[]{:S(2)}) collective-permute-start(bf16[144,1024]{1,0:T(8,128)(2,1)S(1)} %get-tuple-element.168), channel_id=1, source_target_pairs={{0,1},{1,0},{2,3},{3,2},{4,5},{5,4},{6,7},{7,6},{8,9},{9,8},{10,11... | collective-permute-start | bytes 884744 | tf_op jit(solution)/shard_map/gqkvo/y/ppermute | solution.py:97
  233.8 16.6 %collective-permute-start.34 = (bf16[256,1024]{1,0:T(8,128)(2,1)S(1)}, bf16[256,1024]{1,0:T(8,128)(2,1)S(1)}, u32[]{:S(2)}, u32[]{:S(2)}) collective-permute-start(bf16[256,1024]{1,0:T(8,128)(2,1)S(1)} %fusion), channel_id=1, source_target_pairs={{0,16},{8,24},{16,0},{24,8},{1,17},{9,25},{17,1},{25,9},{2,18},{10... | collective-permute-start | bytes 1572872 | tf_op jit(solution)/shard_map/input/seq2/ppermute | solution.py:75
  235.1 14.2 %collective-permute-start.42 = (bf16[144,1024]{1,0:T(8,128)(2,1)S(1)}, bf16[144,1024]{1,0:T(8,128)(2,1)S(1)}, u32[]{:S(2)}, u32[]{:S(2)}) collective-permute-start(bf16[144,1024]{1,0:T(8,128)(2,1)S(1)} %get-tuple-element.170), channel_id=1, source_target_pairs={{0,1},{1,0},{2,3},{3,2},{4,5},{5,4},{6,7},{7,6},{8,9},{9,8},{10,11... | collective-permute-start | bytes 884744 | tf_op jit(solution)/shard_map/gqkvo/y/ppermute | solution.py:97
  235.2 29.1 %collective-permute-start.44 = (bf16[144,1024]{1,0:T(8,128)(2,1)}, bf16[144,1024]{1,0:T(8,128)(2,1)}, u32[]{:S(2)}, u32[]{:S(2)}) collective-permute-start(bf16[144,1024]{1,0:T(8,128)(2,1)} %get-tuple-element.172), channel_id=1, source_target_pairs={{0,1},{1,0},{2,3},{3,2},{4,5},{5,4},{6,7},{7,6},{8,9},{9,8},{10,11... | collective-permute-start | bytes 884744 | tf_op jit(solution)/shard_map/gqkvo/y/ppermute | solution.py:97
  237.8 26.4 %collective-permute-start.39 = (bf16[144,1024]{1,0:T(8,128)(2,1)}, bf16[144,1024]{1,0:T(8,128)(2,1)}, u32[]{:S(2)}, u32[]{:S(2)}) collective-permute-start(bf16[144,1024]{1,0:T(8,128)(2,1)} %add_convert_fusion.7), channel_id=1, source_target_pairs={{0,2},{2,0},{4,6},{6,4},{1,3},{3,1},{5,7},{7,5},{8,10},{10,8},{12,... | collective-permute-start | bytes 884744 | tf_op jit(solution)/shard_map/gqkvo/z1/ppermute | solution.py:102
  243.8 22.3 %collective-permute-start.41 = (bf16[144,1024]{1,0:T(8,128)(2,1)}, bf16[144,1024]{1,0:T(8,128)(2,1)}, u32[]{:S(2)}, u32[]{:S(2)}) collective-permute-start(bf16[144,1024]{1,0:T(8,128)(2,1)} %add_convert_fusion.6), channel_id=1, source_target_pairs={{0,4},{2,6},{4,0},{6,2},{1,5},{3,7},{5,1},{7,3},{8,12},{10,14},{12... | collective-permute-start | bytes 884744 | tf_op jit(solution)/shard_map/gqkvo/z2/ppermute | solution.py:102
  250.1 17.8 %collective-permute-start.43 = (bf16[144,1024]{1,0:T(8,128)(2,1)}, bf16[144,1024]{1,0:T(8,128)(2,1)}, u32[]{:S(2)}, u32[]{:S(2)}) collective-permute-start(bf16[144,1024]{1,0:T(8,128)(2,1)} %add_convert_fusion.5), channel_id=1, source_target_pairs={{0,6},{2,4},{4,2},{6,0},{1,7},{3,5},{5,3},{7,1},{8,14},{10,12},{12... | collective-permute-start | bytes 884744 | tf_op jit(solution)/shard_map/gqkvo/z3/ppermute | solution.py:102
  250.5 5.7 %collective-permute-start.47 = (bf16[128,1024]{1,0:T(8,128)(2,1)S(1)}, bf16[128,1024]{1,0:T(8,128)(2,1)S(1)}, u32[]{:S(2)}, u32[]{:S(2)}) collective-permute-start(bf16[128,1024]{1,0:T(8,128)(2,1)S(1)} %copy-done.18), channel_id=1, source_target_pairs={{0,16},{8,24},{16,0},{24,8},{1,17},{9,25},{17,1},{25,9},{2,18},{10... | collective-permute-start | bytes 786440 | tf_op jit(solution)/shard_map/fdown/seq2/ppermute | solution.py:75
  256.2 24.6 %collective-permute-start.33 = (bf16[256,1024]{1,0:T(8,128)(2,1)}, bf16[256,1024]{1,0:T(8,128)(2,1)S(1)}, u32[]{:S(2)}, u32[]{:S(2)}) collective-permute-start(bf16[256,1024]{1,0:T(8,128)(2,1)} %bitcast.24), channel_id=1, source_target_pairs={{0,8},{8,0},{16,24},{24,16},{1,9},{9,1},{17,25},{25,17},{2,10},{10... | collective-permute-start | bytes 1572872 | tf_op jit(solution)/shard_map/input/seq1/ppermute | solution.py:75
  264.3 10.9 %collective-permute-start.51 = (bf16[128,1024]{1,0:T(8,128)(2,1)S(1)}, bf16[128,1024]{1,0:T(8,128)(2,1)S(1)}, u32[]{:S(2)}, u32[]{:S(2)}) collective-permute-start(bf16[128,1024]{1,0:T(8,128)(2,1)S(1)} %copy-done.18), channel_id=1, source_target_pairs={{0,8},{8,0},{16,24},{24,16},{1,9},{9,1},{17,25},{25,17},{2,10},{10... | collective-permute-start | bytes 786440 | tf_op jit(solution)/shard_map/fdown/seq1/ppermute | solution.py:75
  264.3 10.9 %collective-permute-start.49 = (bf16[128,1024]{1,0:T(8,128)(2,1)S(1)}, bf16[128,1024]{1,0:T(8,128)(2,1)S(1)}, u32[]{:S(2)}, u32[]{:S(2)}) collective-permute-start(bf16[128,1024]{1,0:T(8,128)(2,1)S(1)} %reduce_sum.12.refs_0_), channel_id=1, source_target_pairs={{0,16},{8,24},{16,0},{24,8},{1,17},{9,25},{17,1},{25,9},{2,18},{10... | collective-permute-start | bytes 786440 | tf_op jit(solution)/shard_map/fup/seq2/ppermute | solution.py:75
  269.3 10.7 %collective-permute-start.46 = (bf16[144,1024]{1,0:T(8,128)(2,1)S(1)}, bf16[144,1024]{1,0:T(8,128)(2,1)S(1)}, u32[]{:S(2)}, u32[]{:S(2)}) collective-permute-start(bf16[144,1024]{1,0:T(8,128)(2,1)S(1)} %add_convert_fusion.4.c0), channel_id=1, source_target_pairs={{0,16},{8,24},{16,0},{24,8},{1,17},{9,25},{17,1},{25,9},{2,18},{10... | collective-permute-start | bytes 884744 | tf_op jit(solution)/shard_map/small/seq2/ppermute | solution.py:75
  269.8 6.5 %collective-permute-start.48 = (bf16[128,1024]{1,0:T(8,128)(2,1)S(1)}, bf16[128,1024]{1,0:T(8,128)(2,1)S(1)}, u32[]{:S(2)}, u32[]{:S(2)}) collective-permute-start(bf16[128,1024]{1,0:T(8,128)(2,1)S(1)} %reduce_sum.12.refs_0_), channel_id=1, source_target_pairs={{0,8},{8,0},{16,24},{24,16},{1,9},{9,1},{17,25},{25,17},{2,10},{10... | collective-permute-start | bytes 786440 | tf_op jit(solution)/shard_map/fup/seq1/ppermute | solution.py:75
  276.3 5.8 %collective-permute-start.45 = (bf16[144,1024]{1,0:T(8,128)(2,1)S(1)}, bf16[144,1024]{1,0:T(8,128)(2,1)S(1)}, u32[]{:S(2)}, u32[]{:S(2)}) collective-permute-start(bf16[144,1024]{1,0:T(8,128)(2,1)S(1)} %add_convert_fusion.4.c0), channel_id=1, source_target_pairs={{0,8},{8,0},{16,24},{24,16},{1,9},{9,1},{17,25},{25,17},{2,10},{10... | collective-permute-start | bytes 884744 | tf_op jit(solution)/shard_map/small/seq1/ppermute | solution.py:75
  (47 other events, 371.8 us)
Sparse Core Ops, SparseCore 0:
  25.4 74.8 all-gather.2
  152.0 70.5 reduce-scatter.1
